TPU v7x, 32 devices: a whole 2x2x4 slice. The times are simulated.
32 devices in a mesh: pipe: 8 (over y, x, core), tensor: 4 (over z).
Axes of the slice: x: 2, y: 2, z: 4, core: 2. Of those that a mesh axis runs over, the one named last changes fastest.
Arguments:
- down_state: bfloat16 [8, 128, 4096], P('pipe', None, 'tensor'), may hold values from -64 to 64
- up_state: bfloat16 [8, 128, 4096], P('pipe', None, 'tensor'), may hold values from -64 to 64
- layer_proj: bfloat16 [8, 4096, 4096], P('pipe', 'tensor'), may hold values from -0.125 to 0.125
- conv_filters: float32 [8, 256, 128], P('pipe', 'tensor'), may hold values from -1.5 to 1.5
- norm_gains: float32 [8, 4096], P('pipe', 'tensor'), may hold values from 0.5 to 1.5
- embedding: bfloat16 [512, 4096], P(None, 'tensor'), may hold values from -6 to 6
- dna_tokens: int32 [2, 8, 128], replicated, may hold values from 0 to 511
- entry_order: int32 [2, 8], replicated, may hold values from 0 to 7, each once within a row
Outputs:
- section_outputs: bfloat16 [3, 2, 8, 128, 4096], P(None, None, 'pipe', None, 'tensor')
All inputs are finite; a program needn't handle non-finite values.
Results may differ from a plain program's by a relative error of at most 0.0065.
Values may be sent and summed in bfloat16 or wider, within the bound.
No kernel may reach another device: no remote copies, remote signals or barrier semaphores. Data moves between devices by JAX's collectives and lax.ppermute only.
A program may use at most 64 MiB of HBM per device.

v0:
```python
import jax
import jax.numpy as jnp
from jax import lax
from jax.sharding import PartitionSpec as P

WIDTH = 4096
SHORT_TAPS = 7
LONG_TAPS = 128
TICK_COUNT = 3


EPSILON = 1e-06


def partner(value, axis, bit):
    mask = 2**bit
    pairs = [(source, source ^ mask) for source in range(lax.axis_size(axis))]
    return lax.ppermute(value, axis, pairs)


def shifted(value, axis, steps):
    count = lax.axis_size(axis)
    leading, last = (max(0, -steps), min(count, count - steps))
    return lax.ppermute(value, axis, [(source, source + steps) for source in range(leading, last)])


def causal_mixing(normed, filters, taps):
    seq = normed.shape[0]
    groups = filters.shape[0]
    longest = filters.shape[1]
    later = lax.broadcasted_iota(jnp.int32, (seq, seq), 0)
    earlier = lax.broadcasted_iota(jnp.int32, (seq, seq), 1)
    offsets = later - earlier
    picked = filters[:, jnp.clip(offsets, 0, longest - 1)]
    toeplitz = jnp.where((offsets >= 0) & (offsets < taps), picked, jnp.zeros_like(picked))
    grouped = normed.reshape(seq, groups, -1)
    mixed = jnp.einsum("gts,sgc->tgc", toeplitz, grouped, precision=lax.Precision.HIGHEST)
    return mixed.reshape(seq, -1)


def embed_tokens(token_ids, table):
    onehot = (
        token_ids[:, None]
        == lax.broadcasted_iota(jnp.int32, (token_ids.shape[0], table.shape[0]), 1)
    ).astype(jnp.bfloat16)
    return jnp.dot(onehot, table, preferred_element_type=jnp.float32).astype(jnp.bfloat16)


def mirror_entering(values):
    for bit in range(lax.axis_size("pipe").bit_length() - 1):
        values = partner(values, "pipe", bit)
    return values


def mirror_step(values):
    for bit in range(lax.axis_size("pipe").bit_length() - 1):
        values = partner(values, "pipe", bit)
    return values


def apply_layer(layer_input, weight, filters, gains, taps):
    channels = layer_input.shape[-1]
    values = layer_input.astype(jnp.float32)
    squares = lax.psum(jnp.sum(values * values, axis=-1), "tensor")
    normed = values * lax.rsqrt(squares / WIDTH + EPSILON)[..., None] * gains

    def mix_one(piece):
        return causal_mixing(piece, filters, taps)

    mixed = jax.vmap(mix_one)(normed)
    gated = (normed * mixed).astype(jnp.bfloat16).reshape(-1, channels)
    partial_value = jnp.dot(gated, weight, preferred_element_type=jnp.float32)
    summed = lax.psum_scatter(
        partial_value.astype(jnp.bfloat16), "tensor", scatter_dimension=1, tiled=True
    ).astype(jnp.float32)
    result = (values.reshape(-1, channels) + summed).astype(jnp.bfloat16)
    return result.reshape(layer_input.shape)


def local(
    down_state, up_state, layer_proj, conv_filters, norm_gains, embedding, dna_tokens, entry_order
):
    section = lax.axis_index("pipe")
    weight = layer_proj[0]
    filters = conv_filters[0]
    gains = norm_gains[0]
    taps = jnp.where(section % 2 == 0, SHORT_TAPS, LONG_TAPS)
    downward = down_state[0]
    upward = mirror_entering(up_state[0])
    down_records = []
    up_records = []
    for tick in range(TICK_COUNT):
        if tick > 0:
            downward, upward = shifted((downward, upward), "pipe", 1)
            fresh_down = embed_tokens(dna_tokens[0, entry_order[0, tick - 1]], embedding)
            fresh_up = embed_tokens(dna_tokens[1, entry_order[1, tick - 1]], embedding)
            downward = jnp.where(section == 0, fresh_down, downward)
            upward = jnp.where(section == 0, fresh_up, upward)
        result = apply_layer(jnp.stack([downward, upward]), weight, filters, gains, taps)
        downward = result[0]
        upward = result[1]
        down_records.append(downward)
        up_records.append(mirror_step(upward))
    down_all = jnp.stack(down_records)
    up_all = jnp.stack(up_records)
    return jnp.stack([down_all, up_all], axis=1)[:, :, None]


def solution(mesh):
    placed = (
        P("pipe", None, "tensor"),
        P("pipe", None, "tensor"),
        P("pipe", "tensor", None),
        P("pipe", "tensor", None),
        P("pipe", "tensor"),
        P(None, "tensor"),
        P(),
        P(),
    )
    return jax.shard_map(
        local,
        mesh=mesh,
        in_specs=placed,
        out_specs=P(None, None, "pipe", None, "tensor"),
        check_vma=False,
    )
```

profile of v0, /device:TPU:0, one launch (start us, length us, event | category | flops | bytes accessed | tf_op | source)
XLA Modules:
  0.0 361.0 jit_solution(13246932724315263816)
XLA Ops:
  8.4 2.9 collective-permute-start.1
  12.1 5.8 %collective-permute-done.1 = bf16[128,1024]{1,0:T(8,128)(2,1)S(1)} collective-permute-done((bf16[128,1024]{1,0:T(8,128)(2,1)S(1)}, bf16[128,1024]{1,0:T(8,128)(2,1)S(1)}, u32[]{:S(2)}, u32[]{:S(2)}) %collective-permute-start.1) | collective-permute-done | bytes 262176 | tf_op jit(solution)/shard_map/ppermute | solution.py:18
  17.8 1.8 collective-permute-start.2
  19.6 54.8 %gather_fusion = f32[16384,64]{1,0:T(8,128)} fusion(f32[64,128]{0,1:T(8,128)S(1)} %bitcast.142, s32[16384]{0:T(1024)S(1)} %fusion.99), kind=kCustom, calls=%fused_computation | custom fusion | bytes 8454144 | tf_op jit(solution)/shard_map/vmap()/gather | solution.py:34
  74.4 7.4 %copy.21 = f32[128,128,64]{1,0,2:T(8,128)} copy(f32[128,128,64]{2,1,0:T(8,128)} %bitcast.143) | data formatting | bytes 8388608 | tf_op jit(solution)/shard_map/vmap()/gather | solution.py:34
  83.5 12.0 %psum.21 = f32[2,128]{1,0:T(2,128)S(1)} all-reduce(f32[2,128]{1,0:T(2,128)S(1)} %multiply_reduce_fusion.2), channel_id=1, replica_groups=mesh['pipe'=8,'tensor'=4] {'tensor'}, use_global_device_ids=true, to_apply=%region_1.2 | all-reduce | flops 256 | bytes 2048 | tf_op jit(solution)/shard_map/psum | solution.py:64
  95.6 8.4 %fusion.54 = bf16[2,128,64,16]{1,3,0,2:T(8,128)(2,1)S(1)} fusion(f32[128,128,64]{1,0,2:T(8,128)} %copy.21, pred[128,128]{1,0:T(8,128)(4,1)S(1)} %fusion.102, bf16[1,128,64,16]{1,3,0,2:T(8,128)(2,1)S(1)} %bitcast.160, bf16[1,128,64,16]{1,3,0,2:T(8,128)(2,1)S(1)} %bitcast.156, f32[64,16]{1,0:T(8,128)S(1)} %mul.91, f32[2,128]{1,0:T(2,128)S(1)} %add_rsqrt_fusion.2), kind=kOutput, calls=%fused_computation.34 | convolution fusion | flops 406323200 | bytes 5264384 | tf_op jit(solution)/shard_map/vmap(gts,sgc->tgc)/dot_general | solution.py:37
  104.5 7.1 %fusion.6 = bf16[256,4096]{1,0:T(8,128)(2,1)} fusion(bf16[1,1024,4096]{2,1,0:T(8,128)(2,1)} %param.10, bf16[128,8,2,128]{3,2,1,0:T(2,128)(2,1)S(1)} %bitcast.152), kind=kOutput, calls=%fused_computation.7 | convolution fusion | flops 2148532224 | bytes 11010048 | tf_op jit(solution)/shard_map/dot_general | solution.py:72
  111.7 41.1 %reduce-scatter.4.cloned.1.call-done = bf16[256,1024]{1,0:T(8,128)(2,1)} async-done(((bf16[256,4096]{1,0:T(8,128)(2,1)}), bf16[256,1024]{1,0:T(8,128)(2,1)}) %reduce-scatter.4.cloned.1.call-update) | async-done | bytes 524304 | tf_op jit(solution)/shard_map/reduce_scatter | solution.py:73
  154.2 1.6 collective-permute-start.3
  164.8 3.8 %collective-permute-start.4 = (bf16[128,1024]{1,0:T(8,128)(2,1)S(1)}, bf16[128,1024]{1,0:T(8,128)(2,1)S(1)}, u32[]{:S(2)}, u32[]{:S(2)}) collective-permute-start(bf16[128,1024]{1,0:T(8,128)(2,1)S(1)} %get-tuple-element.6), channel_id=1, source_target_pairs={{0,4},{4,8},{8,12},{12,16},{16,20},{20,24},{24,28},{1,5},{5,9},{9,... | collective-permute-start | bytes 786440 | tf_op jit(solution)/shard_map/ppermute | solution.py:24
  170.5 10.2 %psum.22 = f32[2,128]{1,0:T(2,128)S(1)} all-reduce(f32[2,128]{1,0:T(2,128)S(1)} %multiply_reduce_fusion.1), channel_id=1, replica_groups=mesh['pipe'=8,'tensor'=4] {'tensor'}, use_global_device_ids=true, to_apply=%region_4.5 | all-reduce | flops 256 | bytes 2048 | tf_op jit(solution)/shard_map/psum | solution.py:64
  180.7 8.4 %fusion.51 = bf16[2,128,64,16]{1,3,0,2:T(8,128)(2,1)S(1)} fusion(f32[128,128,64]{1,0,2:T(8,128)} %copy.21, pred[128,128]{1,0:T(8,128)(4,1)S(1)} %fusion.102, bf16[1,128,64,16]{1,3,0,2:T(8,128)(2,1)S(1)} %bitcast.159, bf16[1,128,64,16]{1,3,0,2:T(8,128)(2,1)S(1)} %bitcast.157, f32[2,128]{1,0:T(2,128)S(1)} %add_rsqrt_fusion.1, f32[64,16]{1,0:T(8,128)S(1)} %mul.91), kind=kOutput, calls=%fused_computation.33 | convolution fusion | flops 406323200 | bytes 5264384 | tf_op jit(solution)/shard_map/vmap(gts,sgc->tgc)/dot_general | solution.py:37
  189.5 7.1 %fusion.9 = bf16[256,4096]{1,0:T(8,128)(2,1)} fusion(bf16[1,1024,4096]{2,1,0:T(8,128)(2,1)} %param.10, bf16[128,8,2,128]{3,2,1,0:T(2,128)(2,1)S(1)} %bitcast.153), kind=kOutput, calls=%fused_computation.8 | convolution fusion | flops 2148532224 | bytes 11010048 | tf_op jit(solution)/shard_map/dot_general | solution.py:72
  196.8 45.1 %reduce-scatter.6.cloned.1.call-done = bf16[256,1024]{1,0:T(8,128)(2,1)} async-done(((bf16[256,4096]{1,0:T(8,128)(2,1)}), bf16[256,1024]{1,0:T(8,128)(2,1)}) %reduce-scatter.6.cloned.1.call-update) | async-done | bytes 524304 | tf_op jit(solution)/shard_map/reduce_scatter | solution.py:73
  245.5 3.8 %collective-permute-start.6 = (bf16[128,1024]{1,0:T(8,128)(2,1)}, bf16[128,1024]{1,0:T(8,128)(2,1)S(1)}, u32[]{:S(2)}, u32[]{:S(2)}) collective-permute-start(bf16[128,1024]{1,0:T(8,128)(2,1)} %get-tuple-element.9), channel_id=1, source_target_pairs={{0,4},{4,8},{8,12},{12,16},{16,20},{20,24},{24,28},{1,5},{5,9},{9,... | collective-permute-start | bytes 786440 | tf_op jit(solution)/shard_map/ppermute | solution.py:24
  251.4 10.2 %psum.23 = f32[2,128]{1,0:T(2,128)S(1)} all-reduce(f32[2,128]{1,0:T(2,128)S(1)} %multiply_reduce_fusion), channel_id=1, replica_groups=mesh['pipe'=8,'tensor'=4] {'tensor'}, use_global_device_ids=true, to_apply=%region_7.8 | all-reduce | flops 256 | bytes 2048 | tf_op jit(solution)/shard_map/psum | solution.py:64
  261.7 8.4 %fusion.48 = bf16[2,128,64,16]{1,3,0,2:T(8,128)(2,1)S(1)} fusion(f32[128,128,64]{1,0,2:T(8,128)} %copy.21, pred[128,128]{1,0:T(8,128)(4,1)S(1)} %fusion.102, bf16[1,128,64,16]{1,3,0,2:T(8,128)(2,1)S(1)} %bitcast.158, bf16[1,128,64,16]{1,3,0,2:T(8,128)(2,1)S(1)} %bitcast.155, f32[2,128]{1,0:T(2,128)S(1)} %add_rsqrt_fusion, f32[64,16]{1,0:T(8,128)S(1)} %mul.91), kind=kOutput, calls=%fused_computation.32 | convolution fusion | flops 406323200 | bytes 5264384 | tf_op jit(solution)/shard_map/vmap(gts,sgc->tgc)/dot_general | solution.py:37
  270.5 7.1 %fusion.12 = bf16[256,4096]{1,0:T(8,128)(2,1)} fusion(bf16[1,1024,4096]{2,1,0:T(8,128)(2,1)} %param.10, bf16[128,8,2,128]{3,2,1,0:T(2,128)(2,1)S(1)} %bitcast.154), kind=kOutput, calls=%fused_computation.9 | convolution fusion | flops 2148532224 | bytes 11010048 | tf_op jit(solution)/shard_map/dot_general | solution.py:72
  278.8 44.7 %reduce-scatter.8.cloned.1.call-done = bf16[256,1024]{1,0:T(8,128)(2,1)} async-done(((bf16[256,4096]{1,0:T(8,128)(2,1)}), bf16[256,1024]{1,0:T(8,128)(2,1)}) %reduce-scatter.8.cloned.1.call-update) | async-done | bytes 524304 | tf_op jit(solution)/shard_map/reduce_scatter | solution.py:73
  328.5 5.8 %collective-permute-done.8 = bf16[128,1024]{1,0:T(8,128)(2,1)S(1)} collective-permute-done((bf16[128,1024]{1,0:T(8,128)(2,1)}, bf16[128,1024]{1,0:T(8,128)(2,1)S(1)}, u32[]{:S(2)}, u32[]{:S(2)}) %collective-permute-start.8) | collective-permute-done | bytes 262176 | tf_op jit(solution)/shard_map/ppermute | solution.py:18
  335.8 4.1 %collective-permute-done.11 = bf16[128,1024]{1,0:T(8,128)(2,1)S(1)} collective-permute-done((bf16[128,1024]{1,0:T(8,128)(2,1)}, bf16[128,1024]{1,0:T(8,128)(2,1)S(1)}, u32[]{:S(2)}, u32[]{:S(2)}) %collective-permute-start.11) | collective-permute-done | bytes 262176 | tf_op jit(solution)/shard_map/ppermute | solution.py:18
  341.4 3.7 %collective-permute-done.14 = bf16[128,1024]{1,0:T(8,128)(2,1)S(1)} collective-permute-done((bf16[128,1024]{1,0:T(8,128)(2,1)S(1)}, bf16[128,1024]{1,0:T(8,128)(2,1)S(1)}, u32[]{:S(2)}, u32[]{:S(2)}) %collective-permute-start.14) | collective-permute-done | bytes 262176 | tf_op jit(solution)/shard_map/ppermute | solution.py:18
  347.3 5.6 %collective-permute-done.15 = bf16[128,1024]{1,0:T(8,128)(2,1)S(1)} collective-permute-done((bf16[128,1024]{1,0:T(8,128)(2,1)S(1)}, bf16[128,1024]{1,0:T(8,128)(2,1)S(1)}, u32[]{:S(2)}, u32[]{:S(2)}) %collective-permute-start.15) | collective-permute-done | bytes 262176 | tf_op jit(solution)/shard_map/ppermute | solution.py:18
  (76 shorter events, 29.1 us)
Async XLA Ops:
  6.5 162.1 %copy-start = (bf16[512,1024]{1,0:T(8,128)(2,1)S(1)}, bf16[512,1024]{1,0:T(8,128)(2,1)}, u32[]{:S(2)}) copy-start(bf16[512,1024]{1,0:T(8,128)(2,1)} %param.13) | copy-start | bytes 3145732
  6.5 146.3 %reduce-scatter.4.cloned.1.call-start = ((), (), s32[]{:S(2)}) async-start(), calls=%async_computation.3 | async-start | bytes 2621440 | tf_op jit(solution)/shard_map/reduce_scatter | solution.py:73
  6.5 1.8 collective-permute-start
  8.4 9.5 %collective-permute-start.1 = (bf16[128,1024]{1,0:T(8,128)(2,1)S(1)}, bf16[128,1024]{1,0:T(8,128)(2,1)S(1)}, u32[]{:S(2)}, u32[]{:S(2)}) collective-permute-start(bf16[128,1024]{1,0:T(8,128)(2,1)S(1)} %collective-permute-done), channel_id=1, source_target_pairs={{0,8},{4,12},{8,0},{12,4},{16,24},{20,28},{24,16},{28,20},{1,9},{5... | collective-permute-start | bytes 786440 | tf_op jit(solution)/shard_map/ppermute | solution.py:18
  17.8 65.5 %collective-permute-start.2 = (bf16[128,1024]{1,0:T(8,128)(2,1)S(1)}, bf16[128,1024]{1,0:T(8,128)(2,1)S(1)}, u32[]{:S(2)}, u32[]{:S(2)}) collective-permute-start(bf16[128,1024]{1,0:T(8,128)(2,1)S(1)} %collective-permute-done.1), channel_id=1, source_target_pairs={{0,16},{4,20},{8,24},{12,28},{16,0},{20,4},{24,8},{28,12},{1,17},{... | collective-permute-start | bytes 786440 | tf_op jit(solution)/shard_map/ppermute | solution.py:18
  74.4 7.9 %copy-start.2 = (f32[1,1024]{1,0:T(1,128)S(1)}, f32[1,1024]{1,0:T(1,128)}, u32[]{:S(2)}) copy-start(f32[1,1024]{1,0:T(1,128)} %param.12) | copy-start | bytes 12292
  74.4 8.7 %copy-start.1 = (bf16[1,128,1024]{2,1,0:T(8,128)(2,1)S(1)}, bf16[1,128,1024]{2,1,0:T(8,128)(2,1)}, u32[]{:S(2)}) copy-start(bf16[1,128,1024]{2,1,0:T(8,128)(2,1)} %param.8) | copy-start | bytes 786436
  111.6 44.2 %copy-start.3 = (s32[2,8]{1,0:T(2,128)S(1)}, s32[2,8]{1,0:T(2,128)}, u32[]{:S(2)}) copy-start(s32[2,8]{1,0:T(2,128)} %param.15) | copy-start | bytes 196
  111.6 130.3 %reduce-scatter.6.cloned.1.call-start = ((), (), s32[]{:S(2)}) async-start(), calls=%async_computation.4 | async-start | bytes 2621440 | tf_op jit(solution)/shard_map/reduce_scatter | solution.py:73
  154.2 14.5 %collective-permute-start.3 = (bf16[128,1024]{1,0:T(8,128)(2,1)S(1)}, bf16[128,1024]{1,0:T(8,128)(2,1)S(1)}, u32[]{:S(2)}, u32[]{:S(2)}) collective-permute-start(bf16[128,1024]{1,0:T(8,128)(2,1)S(1)} %get-tuple-element.7), channel_id=1, source_target_pairs={{0,4},{4,8},{8,12},{12,16},{16,20},{20,24},{24,28},{1,5},{5,9},{9,... | collective-permute-start | bytes 786440 | tf_op jit(solution)/shard_map/ppermute | solution.py:24
  164.8 5.0 %collective-permute-start.4 = (bf16[128,1024]{1,0:T(8,128)(2,1)S(1)}, bf16[128,1024]{1,0:T(8,128)(2,1)S(1)}, u32[]{:S(2)}, u32[]{:S(2)}) collective-permute-start(bf16[128,1024]{1,0:T(8,128)(2,1)S(1)} %get-tuple-element.6), channel_id=1, source_target_pairs={{0,4},{4,8},{8,12},{12,16},{16,20},{20,24},{24,28},{1,5},{5,9},{9,... | collective-permute-start | bytes 786440 | tf_op jit(solution)/shard_map/ppermute | solution.py:24
  196.7 126.9 %reduce-scatter.8.cloned.1.call-start = ((), (), s32[]{:S(2)}) async-start(), calls=%async_computation.5 | async-start | bytes 2621440 | tf_op jit(solution)/shard_map/reduce_scatter | solution.py:73
  244.0 5.4 %collective-permute-start.5 = (bf16[128,1024]{1,0:T(8,128)(2,1)S(1)}, bf16[128,1024]{1,0:T(8,128)(2,1)S(1)}, u32[]{:S(2)}, u32[]{:S(2)}) collective-permute-start(bf16[128,1024]{1,0:T(8,128)(2,1)S(1)} %get-tuple-element.10), channel_id=1, source_target_pairs={{0,4},{4,8},{8,12},{12,16},{16,20},{20,24},{24,28},{1,5},{5,9},{9,... | collective-permute-start | bytes 786440 | tf_op jit(solution)/shard_map/ppermute | solution.py:24
  245.5 5.2 %collective-permute-start.6 = (bf16[128,1024]{1,0:T(8,128)(2,1)}, bf16[128,1024]{1,0:T(8,128)(2,1)S(1)}, u32[]{:S(2)}, u32[]{:S(2)}) collective-permute-start(bf16[128,1024]{1,0:T(8,128)(2,1)} %get-tuple-element.9), channel_id=1, source_target_pairs={{0,4},{4,8},{8,12},{12,16},{16,20},{20,24},{24,28},{1,5},{5,9},{9,... | collective-permute-start | bytes 786440 | tf_op jit(solution)/shard_map/ppermute | solution.py:24
  277.6 47.3 %collective-permute-start.7 = (bf16[128,1024]{1,0:T(8,128)(2,1)S(1)}, bf16[128,1024]{1,0:T(8,128)(2,1)}, u32[]{:S(2)}, u32[]{:S(2)}) collective-permute-start(bf16[128,1024]{1,0:T(8,128)(2,1)S(1)} %get-tuple-element.6), channel_id=1, source_target_pairs={{0,4},{4,0},{8,12},{12,8},{16,20},{20,16},{24,28},{28,24},{1,5},{5... | collective-permute-start | bytes 786440 | tf_op jit(solution)/shard_map/ppermute | solution.py:18
  278.7 47.8 %collective-permute-start.10 = (bf16[128,1024]{1,0:T(8,128)(2,1)}, bf16[128,1024]{1,0:T(8,128)(2,1)}, u32[]{:S(2)}, u32[]{:S(2)}) collective-permute-start(bf16[128,1024]{1,0:T(8,128)(2,1)} %get-tuple-element.9), channel_id=1, source_target_pairs={{0,4},{4,0},{8,12},{12,8},{16,20},{20,16},{24,28},{28,24},{1,5},{5... | collective-permute-start | bytes 786440 | tf_op jit(solution)/shard_map/ppermute | solution.py:18
  324.8 2.2 collective-permute-start.13
  324.9 9.4 %collective-permute-start.8 = (bf16[128,1024]{1,0:T(8,128)(2,1)}, bf16[128,1024]{1,0:T(8,128)(2,1)S(1)}, u32[]{:S(2)}, u32[]{:S(2)}) collective-permute-start(bf16[128,1024]{1,0:T(8,128)(2,1)} %collective-permute-done.7), channel_id=1, source_target_pairs={{0,8},{4,12},{8,0},{12,4},{16,24},{20,28},{24,16},{28,20},{1,9},{5... | collective-permute-start | bytes 786440 | tf_op jit(solution)/shard_map/ppermute | solution.py:18
  326.5 13.5 %collective-permute-start.11 = (bf16[128,1024]{1,0:T(8,128)(2,1)}, bf16[128,1024]{1,0:T(8,128)(2,1)S(1)}, u32[]{:S(2)}, u32[]{:S(2)}) collective-permute-start(bf16[128,1024]{1,0:T(8,128)(2,1)} %collective-permute-done.10), channel_id=1, source_target_pairs={{0,8},{4,12},{8,0},{12,4},{16,24},{20,28},{24,16},{28,20},{1,9},{5... | collective-permute-start | bytes 786440 | tf_op jit(solution)/shard_map/ppermute | solution.py:18
  327.0 18.1 %collective-permute-start.14 = (bf16[128,1024]{1,0:T(8,128)(2,1)S(1)}, bf16[128,1024]{1,0:T(8,128)(2,1)S(1)}, u32[]{:S(2)}, u32[]{:S(2)}) collective-permute-start(bf16[128,1024]{1,0:T(8,128)(2,1)S(1)} %collective-permute-done.13), channel_id=1, source_target_pairs={{0,8},{4,12},{8,0},{12,4},{16,24},{20,28},{24,16},{28,20},{1,9},{5... | collective-permute-start | bytes 786440 | tf_op jit(solution)/shard_map/ppermute | solution.py:18
  334.3 12.3 %collective-permute-start.9 = (bf16[128,1024]{1,0:T(8,128)(2,1)S(1)}, bf16[128,1024]{1,0:T(8,128)(2,1)S(1)}, u32[]{:S(2)}, u32[]{:S(2)}) collective-permute-start(bf16[128,1024]{1,0:T(8,128)(2,1)S(1)} %collective-permute-done.8), channel_id=1, source_target_pairs={{0,16},{4,20},{8,24},{12,28},{16,0},{20,4},{24,8},{28,12},{1,17},{... | collective-permute-start | bytes 786440 | tf_op jit(solution)/shard_map/ppermute | solution.py:18
  339.9 7.4 %collective-permute-start.12 = (bf16[128,1024]{1,0:T(8,128)(2,1)S(1)}, bf16[128,1024]{1,0:T(8,128)(2,1)S(1)}, u32[]{:S(2)}, u32[]{:S(2)}) collective-permute-start(bf16[128,1024]{1,0:T(8,128)(2,1)S(1)} %collective-permute-done.11), channel_id=1, source_target_pairs={{0,16},{4,20},{8,24},{12,28},{16,0},{20,4},{24,8},{28,12},{1,17},{... | collective-permute-start | bytes 786440 | tf_op jit(solution)/shard_map/ppermute | solution.py:18
  345.1 7.9 %collective-permute-start.15 = (bf16[128,1024]{1,0:T(8,128)(2,1)S(1)}, bf16[128,1024]{1,0:T(8,128)(2,1)S(1)}, u32[]{:S(2)}, u32[]{:S(2)}) collective-permute-start(bf16[128,1024]{1,0:T(8,128)(2,1)S(1)} %collective-permute-done.14), channel_id=1, source_target_pairs={{0,16},{4,20},{8,24},{12,28},{16,0},{20,4},{24,8},{28,12},{1,17},{... | collective-permute-start | bytes 786440 | tf_op jit(solution)/shard_map/ppermute | solution.py:18
Sparse Core Ops, SparseCore 0:
  111.7 41.0 reduce-scatter.3
  196.8 45.0 reduce-scatter.5
  277.8 45.7 reduce-scatter.7
where the time goes:
time: 362 us; the launch traced here: 361 us
  waiting for transfers between devices  159 us (44%)
  local copies, waits for them, and re-layouts  69.5 us (19%)
  matrix products  47.9 us (13%)
  blocking collectives  32.4 us (9%)
  starting transfers between devices  25.2 us (7%)
  between operations  21 us (6%)
  other arithmetic  5.57 us (2%)
    reduce_scatter x3, waiting for transfers between devices, apply_layer(): lax.psum_scatter(partial_value.astype(jnp.bfloat16), 'tensor', scatter_di...  131 us
    gather x2, local copies, waits for them, and re-layouts, causal_mixing(): picked = filters[:, jnp.clip(offsets, 0, longest - 1)]  62.2 us
    psum x3, blocking collectives, apply_layer(): squares = lax.psum(jnp.sum(values * values, axis=-1), 'tensor')  32.4 us
    ppermute x12, waiting for transfers between devices, partner(): return lax.ppermute(value, axis, pairs)  27 us
    dot_general x3, matrix products, causal_mixing(): jnp.einsum('gts,sgc->tgc', toeplitz, grouped, precision=lax.Precision.HIG...  25.2 us
    dot_general x3, matrix products, apply_layer(): partial_value = jnp.dot(gated, weight, preferred_element_type=jnp.float32)  21.3 us
    ppermute x12, starting transfers between devices, partner(): return lax.ppermute(value, axis, pairs)  14.3 us
    ppermute x4, starting transfers between devices, shifted(): lax.ppermute(value, axis, [(source, source + steps) for source in range(l...  10.8 us
  transfers between devices with their start and end apart: 19, of which 12 were waited for; matrix products, arithmetic and copies ran while one was open for 19% of the time, Pallas kernels for 0%

commit v1 on v0

v1 whole, which is shorter than its diff:
```python
import functools

import jax
import jax.numpy as jnp
from jax import lax
from jax.experimental import pallas as pl
from jax.experimental.pallas import tpu as pltpu
from jax.sharding import PartitionSpec as P

WIDTH = 4096
SHORT_TAPS = 7
LONG_TAPS = 128
GROUP_SIZE = 16
TICK_COUNT = 3
EPSILON = 1e-06

LANES = 128
PER_BLOCK = LANES // GROUP_SIZE
IN_VMEM = pl.BlockSpec(memory_space=pltpu.VMEM)
IN_SMEM = pl.BlockSpec(memory_space=pltpu.SMEM)
IN_PLACE = pl.BlockSpec(memory_space=pl.ANY)


def toeplitz_kernel(taps_ref, filters_ref, blocks_ref):
    groups, seq = filters_ref.shape
    lane = lax.broadcasted_iota(jnp.int32, (groups, seq), 1)
    kept = jnp.where(lane < taps_ref[0], filters_ref[...], 0.0).astype(jnp.bfloat16)
    row = lax.broadcasted_iota(jnp.int32, (seq, seq), 0)
    col = lax.broadcasted_iota(jnp.int32, (seq, seq), 1)
    flip = ((row + col) % seq == 0).astype(jnp.bfloat16)
    backward = jnp.dot(kept, flip, preferred_element_type=jnp.float32)
    for group in range(groups):
        wide = jnp.broadcast_to(backward[group : group + 1, :], (seq, seq))
        turned = pltpu.roll(wide, 0, 1, stride=1, stride_axis=0)
        start = group % PER_BLOCK * seq
        blocks_ref[group // PER_BLOCK, :, start : start + seq] = jnp.where(
            row >= col, turned, 0.0
        ).astype(jnp.bfloat16)


def toeplitz_blocks(filters, taps):
    groups, seq = filters.shape
    return pl.pallas_call(
        toeplitz_kernel,
        out_shape=jax.ShapeDtypeStruct((groups // PER_BLOCK, seq, PER_BLOCK * seq), jnp.bfloat16),
        in_specs=[IN_SMEM, IN_VMEM],
        out_specs=IN_VMEM,
        name="toeplitz",
    )(taps, filters)


def row_squares(values):
    seq, channels = values.shape
    squares = values * values
    total = squares[:, :LANES]
    for start in range(LANES, channels, LANES):
        total = total + squares[:, start : start + LANES]
    return jnp.sum(total.T, axis=0, keepdims=True)


def squares_kernel(values_ref, squares_ref):
    squares_ref[...] = row_squares(values_ref[...].astype(jnp.float32))


def squares_of(values):
    return pl.pallas_call(
        squares_kernel,
        out_shape=jax.ShapeDtypeStruct((1, values.shape[0]), jnp.float32),
        in_specs=[IN_VMEM],
        out_specs=IN_VMEM,
        name="squares",
    )(values)


def layer_kernel(count, place_ref, x_ref, gains_ref, blocks_ref, weight_ref, *refs):
    squares_refs, refs = refs[: count - 1], refs[count - 1 :]
    out_refs, (weight_buf, gated_buf, sems) = refs[:count], refs[count:]
    place = place_ref[0]
    seq, channels = x_ref.shape
    order = [apart for apart in reversed(range(count))]
    copies = {}
    for apart in order:
        start = pl.multiple_of((place ^ apart) * channels, channels)
        copies[apart] = pltpu.make_async_copy(
            weight_ref.at[:, pl.ds(start, channels)], weight_buf.at[apart], sems.at[apart]
        )
        copies[apart].start()
    values = x_ref[...].astype(jnp.float32)
    others = squares_refs[0][...]
    for ref in squares_refs[1:]:
        others = others + ref[...]
    squares = jnp.broadcast_to(others, (seq, seq)).T + jnp.sum(
        values * values, axis=-1, keepdims=True
    )
    scale = lax.rsqrt(squares / WIDTH + EPSILON)
    lane_group = lax.broadcasted_iota(jnp.int32, (seq, LANES), 1) // GROUP_SIZE
    for block in range(channels // LANES):
        lanes = slice(block * LANES, (block + 1) * LANES)
        normed = values[:, lanes] * scale * gains_ref[:, lanes]
        narrow = normed.astype(jnp.bfloat16)
        spread = jnp.concatenate(
            [
                jnp.where(lane_group == part, narrow, jnp.zeros_like(narrow))
                for part in range(PER_BLOCK)
            ],
            axis=0,
        )
        mixed = jnp.dot(blocks_ref[block], spread, preferred_element_type=jnp.float32)
        gated_buf[:, lanes] = (normed * mixed).astype(jnp.bfloat16)
    for apart in order:
        copies[apart].wait()
        out_refs[apart][...] = jnp.dot(
            gated_buf[...], weight_buf[apart], preferred_element_type=jnp.float32
        ).astype(out_refs[apart].dtype)


def layer_partials(x, squares, place, gains, blocks, weight, count):
    seq, channels = x.shape
    kinds = [jnp.bfloat16 if apart % 2 else jnp.float32 for apart in range(count)]
    return pl.pallas_call(
        functools.partial(layer_kernel, count),
        out_shape=[jax.ShapeDtypeStruct((seq, channels), kind) for kind in kinds],
        in_specs=[IN_SMEM, IN_VMEM, IN_VMEM, IN_VMEM, IN_PLACE] + [IN_VMEM] * (count - 1),
        out_specs=[IN_VMEM] * count,
        scratch_shapes=[
            pltpu.VMEM((count, channels, channels), jnp.bfloat16),
            pltpu.VMEM((seq, channels), jnp.bfloat16),
            pltpu.SemaphoreType.DMA((count,)),
        ],
        compiler_params=pltpu.CompilerParams(vmem_limit_bytes=40 * 2**20),
        name="layer",
    )(place, x, gains, blocks, weight, *squares)


def merge_kernel(count, last_ref, x_ref, fresh_ref, own_ref, *refs):
    arrived, (y_ref, sent_ref, squares_ref) = refs[:count], refs[count:]
    total = own_ref[...]
    for ref in arrived:
        total = total + ref[...].astype(jnp.float32)
    y = (x_ref[...].astype(jnp.float32) + total).astype(jnp.bfloat16)
    y_ref[...] = y
    sent = jnp.where(last_ref[0] == 1, fresh_ref[...].astype(jnp.float32), y.astype(jnp.float32))
    sent_ref[...] = sent.astype(jnp.bfloat16)
    squares_ref[...] = row_squares(sent)


def merge(x, fresh, own, arrived, last):
    seq, channels = x.shape
    return pl.pallas_call(
        functools.partial(merge_kernel, len(arrived)),
        out_shape=[
            jax.ShapeDtypeStruct((seq, channels), jnp.bfloat16),
            jax.ShapeDtypeStruct((seq, channels), jnp.bfloat16),
            jax.ShapeDtypeStruct((1, seq), jnp.float32),
        ],
        in_specs=[IN_SMEM] + [IN_VMEM] * (3 + len(arrived)),
        out_specs=[IN_VMEM] * 3,
        name="merge",
    )(last, x, fresh, own, *arrived)


def embed_tokens(token_ids, table):
    onehot = (
        token_ids[:, None]
        == lax.broadcasted_iota(jnp.int32, (token_ids.shape[0], table.shape[0]), 1)
    ).astype(jnp.bfloat16)
    return jnp.dot(onehot, table, preferred_element_type=jnp.float32).astype(jnp.bfloat16)


def send(values, target):
    pipe, tensor = lax.axis_size("pipe"), lax.axis_size("tensor")
    pairs = []
    for k in range(pipe):
        for z in range(tensor):
            to_k, to_z = target(k, z)
            pairs.append((k * tensor + z, to_k * tensor + to_z))
    return lax.ppermute(values, ("pipe", "tensor"), pairs)


def add_up(partials):
    count = len(partials)
    partials = list(partials)
    arrived = []
    bit = 1
    while bit < count:
        for apart in reversed(range(bit, count, 2 * bit)):
            outgoing = partials[apart].astype(jnp.bfloat16)
            incoming = send(outgoing, lambda k, z: (k, z ^ bit))
            if apart == bit:
                arrived.append(incoming)
            else:
                partials[apart ^ bit] = partials[apart ^ bit] + incoming.astype(jnp.float32)
        bit *= 2
    return arrived


def local(
    down_state, up_state, layer_proj, conv_filters, norm_gains, embedding, dna_tokens, entry_order
):
    pipe, tensor = lax.axis_size("pipe"), lax.axis_size("tensor")
    section = lax.axis_index("pipe")
    place = lax.axis_index("tensor").astype(jnp.int32).reshape(1)
    last = (section == pipe - 1).astype(jnp.int32).reshape(1)
    taps = jnp.where(section % 2 == 0, SHORT_TAPS, LONG_TAPS).astype(jnp.int32).reshape(1)
    weight, gains = layer_proj[0], norm_gains

    def mirrored(k):
        return pipe - 1 - k

    def following(k):
        return (k + 1) % pipe

    def spread_squares(squares, target):
        return [
            send(squares, lambda k, z, apart=apart: (target(k), z ^ apart))
            for apart in range(1, tensor)
        ]

    entering = [down_state[0], up_state[0]]
    squares = [squares_of(values) for values in entering]
    squares = [spread_squares(squares[0], lambda k: k), spread_squares(squares[1], mirrored)]
    entering[1] = send(entering[1], lambda k, z: (mirrored(k), z))
    blocks = toeplitz_blocks(conv_filters[0], taps)
    fresh = [
        [
            embed_tokens(dna_tokens[way, entry_order[way, tick]], embedding)
            for tick in range(TICK_COUNT - 1)
        ]
        for way in range(2)
    ]
    records = []
    for tick in range(TICK_COUNT):
        leaving = []
        for way in range(2):
            x = entering[way]
            partials = layer_partials(x, squares[way], place, gains, blocks, weight, tensor)
            arrived = add_up(partials)
            newcomer = fresh[way][min(tick, TICK_COUNT - 2)]
            y, sent, own = merge(x, newcomer, partials[0], arrived, last)
            if tick < TICK_COUNT - 1:
                squares[way] = spread_squares(own, following)
                entering[way] = send(sent, lambda k, z: (following(k), z))
            leaving.append(y if way == 0 else send(y, lambda k, z: (mirrored(k), z)))
        records.append(jnp.stack(leaving))
    return jnp.stack(records)[:, :, None]


def solution(mesh):
    placed = (
        P("pipe", None, "tensor"),
        P("pipe", None, "tensor"),
        P("pipe", "tensor", None),
        P("pipe", "tensor", None),
        P("pipe", "tensor"),
        P(None, "tensor"),
        P(),
        P(),
    )
    return jax.shard_map(
        local,
        mesh=mesh,
        in_specs=placed,
        out_specs=P(None, None, "pipe", None, "tensor"),
        check_vma=False,
    )
```

time: 362 us -> 224 us (0.62)
  waiting for transfers between devices: 159 us -> 81.2 us
  Pallas kernels: 0 us -> 48.5 us
  local copies, waits for them, and re-layouts: 69.5 us -> 25.1 us
  matrix products: 47.9 us -> 4.25 us
  blocking collectives: 32.4 us -> 0 us
  starting transfers between devices: 25.2 us -> 50.1 us
  between operations: 21 us -> 7.95 us
    reduce_scatter x3 -> x0, waiting for transfers between devices: 131 us -> none  [apply_layer(): lax.psum_scatter(partial_value.astype(jnp.bfloat16), 'tensor', scatter_di...]
    gather x2 -> x0, local copies, waits for them, and re-layouts: 62.2 us -> none  [causal_mixing(): picked = filters[:, jnp.clip(offsets, 0, longest - 1)]]
    ppermute x16 -> x44, waiting for transfers between devices: 28.4 us -> 81.2 us  [send(): return lax.ppermute(values, ('pipe', 'tensor'), pairs)]
    pallas_call x0 -> x15, Pallas kernels: none -> 48.5 us  [the longest x6 28.3 us: layer_partials(): pl.pallas_call(functools.partial(layer_kernel, count), out_shape=[jax.Sha...]
    dot_general x6 -> x0, matrix products: 46.5 us -> none  [the longest x3 25.2 us: causal_mixing(): jnp.einsum('gts,sgc->tgc', toeplitz, grouped, precision=lax.Precision.HIG...]
    psum x3 -> x0, blocking collectives: 32.4 us -> none  [apply_layer(): squares = lax.psum(jnp.sum(values * values, axis=-1), 'tensor')]
    ppermute x16 -> x44, starting transfers between devices: 25.1 us -> 50.1 us  [send(): return lax.ppermute(values, ('pipe', 'tensor'), pairs)]
    unnamed x11 -> x72, local copies, waits for them, and re-layouts: 1.54 us -> 23.7 us
  transfers between devices with their start and end apart: 19 -> 44, of which waited for: 12 -> 15; matrix products, arithmetic and copies ran while one was open for 19% -> 4% of each run, Pallas kernels for 0% -> 20%
where the time goes in v1:
time: 224 us
  waiting for transfers between devices  81.2 us (36%)
  starting transfers between devices  50.1 us (22%)
  Pallas kernels  48.5 us (22%)
  local copies, waits for them, and re-layouts  25.1 us (11%)
  between operations  7.95 us (4%)
  other arithmetic  6.6 us (3%)
  matrix products  4.25 us (2%)
    ppermute x44, waiting for transfers between devices, send(): return lax.ppermute(values, ('pipe', 'tensor'), pairs)  81.2 us
    ppermute x44, starting transfers between devices, send(): return lax.ppermute(values, ('pipe', 'tensor'), pairs)  50.1 us
    pallas_call x6, Pallas kernels, layer_partials(): pl.pallas_call(functools.partial(layer_kernel, count), out_shape=[jax.Sha...  28.3 us
    unnamed x72, local copies, waits for them, and re-layouts  23.7 us
    pallas_call x6, Pallas kernels, merge(): pl.pallas_call(functools.partial(merge_kernel, len(arrived)), out_shape=[...  14.2 us
  transfers between devices with their start and end apart: 44, of which 15 were waited for; matrix products, arithmetic and copies ran while one was open for 4% of the time, Pallas kernels for 20%

profile of v1, /device:TPU:0, one launch (start us, length us, event | category | flops | bytes accessed | tf_op | source)
XLA Modules:
  0.0 223.6 jit_solution(10709358933051781474)
XLA Ops:
  0.0 3.3 %collective-permute-start.6 = (bf16[128,1024]{1,0:T(8,128)(2,1)}, bf16[128,1024]{1,0:T(8,128)(2,1)S(1)}, u32[]{:S(2)}, u32[]{:S(2)}) collective-permute-start(bf16[128,1024]{1,0:T(8,128)(2,1)} %bitcast.48), channel_id=1, source_target_pairs={{0,28},{1,29},{2,30},{3,31},{4,24},{5,25},{6,26},{7,27},{8,20},{9,... | collective-permute-start | bytes 786440 | tf_op jit(solution)/shard_map/ppermute | solution.py:177
  6.7 3.9 %collective-permute-start.8 = (f32[1,128]{1,0:T(1,128)}, f32[1,128]{1,0:T(1,128)S(1)}, u32[]{:S(2)}, u32[]{:S(2)}) collective-permute-start(f32[1,128]{1,0:T(1,128)} %squares.3), channel_id=1, source_target_pairs={{0,30},{1,31},{2,28},{3,29},{4,26},{5,27},{6,24},{7,25},{8,22},{9,... | collective-permute-start | bytes 1544 | tf_op jit(solution)/shard_map/ppermute | solution.py:177
  13.5 3.8 %collective-permute-done.9.refs_2_ = f32[1,128]{1,0:T(1,128)S(1)} collective-permute-done((f32[1,128]{1,0:T(1,128)}, f32[1,128]{1,0:T(1,128)S(1)}, u32[]{:S(2)}, u32[]{:S(2)}) %collective-permute-start.9) | collective-permute-done | bytes 544 | tf_op jit(solution)/shard_map/ppermute | solution.py:177
  18.0 3.4 %copy-done.1 = bf16[1,1024,4096]{2,1,0:T(8,128)(2,1)S(1)} copy-done((bf16[1,1024,4096]{2,1,0:T(8,128)(2,1)S(1)}, bf16[1,1024,4096]{2,1,0:T(8,128)(2,1)}, u32[]{:S(2)}) %copy-start.1) | copy-done | bytes 8388632
  23.9 4.6 %layer.7 = (f32[128,1024]{1,0:T(8,128)S(1)}, bf16[128,1024]{1,0:T(8,128)(2,1)}, f32[128,1024]{1,0:T(8,128)S(1)}, bf16[128,1024]{1,0:T(8,128)(2,1)}) custom-call(s32[1]{0:T(128)} %bitcast.4.place_ref, bf16[128,1024]{1,0:T(8,128)(2,1)S(1)} %copy-done.9, f32[1,1024]{1,0:T(1,128)S(1)} %copy-done.20, bf16[8,128,1024]{2,1,0:T(8,128)(2,1)S(1)} %copy-done.5, ...), custom_call_target="tpu_custom_call" | custom-call | tf_op jit(solution)/shard_map/layer/pallas_call | solution.py:120
  44.4 3.4 %copy-done.2 = bf16[1,1024,4096]{2,1,0:T(8,128)(2,1)S(1)} copy-done((bf16[1,1024,4096]{2,1,0:T(8,128)(2,1)S(1)}, bf16[1,1024,4096]{2,1,0:T(8,128)(2,1)}, u32[]{:S(2)}) %copy-start.2) | copy-done | bytes 8388632
  47.8 4.1 %layer.6 = (f32[128,1024]{1,0:T(8,128)S(1)}, bf16[128,1024]{1,0:T(8,128)(2,1)}, f32[128,1024]{1,0:T(8,128)S(1)}, bf16[128,1024]{1,0:T(8,128)(2,1)S(1)}) custom-call(s32[1]{0:T(128)} %bitcast.4.place_ref, bf16[128,1024]{1,0:T(8,128)(2,1)S(1)} %bitcast.47, f32[1,1024]{1,0:T(1,128)S(1)} %copy-done.20, bf16[8,128,1024]{2,1,0:T(8,128)(2,1)S(1)} %copy-done.6, ...), custom_call_target="tpu_custom_call" | custom-call | tf_op jit(solution)/shard_map/layer/pallas_call | solution.py:120
  58.5 11.0 %collective-permute-done.4 = bf16[128,1024]{1,0:T(8,128)(2,1)S(1)} collective-permute-done((bf16[128,1024]{1,0:T(8,128)(2,1)S(1)}, bf16[128,1024]{1,0:T(8,128)(2,1)S(1)}, u32[]{:S(2)}, u32[]{:S(2)}) %collective-permute-start.4) | collective-permute-done | bytes 262176 | tf_op jit(solution)/shard_map/ppermute | solution.py:177
  71.4 8.6 %collective-permute-done.10.refs_0_ = bf16[128,1024]{1,0:T(8,128)(2,1)} collective-permute-done((bf16[128,1024]{1,0:T(8,128)(2,1)}, bf16[128,1024]{1,0:T(8,128)(2,1)}, u32[]{:S(2)}, u32[]{:S(2)}) %collective-permute-start.10) | collective-permute-done | bytes 262176 | tf_op jit(solution)/shard_map/ppermute | solution.py:177
  93.9 3.5 %collective-permute-done.24.refs_2_ = f32[1,128]{1,0:T(1,128)S(1)} collective-permute-done((f32[1,128]{1,0:T(1,128)S(1)}, f32[1,128]{1,0:T(1,128)S(1)}, u32[]{:S(2)}, u32[]{:S(2)}) %collective-permute-start.24) | collective-permute-done | bytes 544 | tf_op jit(solution)/shard_map/ppermute | solution.py:177
  97.5 3.4 %copy-done.3 = bf16[1,1024,4096]{2,1,0:T(8,128)(2,1)S(1)} copy-done((bf16[1,1024,4096]{2,1,0:T(8,128)(2,1)S(1)}, bf16[1,1024,4096]{2,1,0:T(8,128)(2,1)}, u32[]{:S(2)}) %copy-start.3) | copy-done | bytes 8388632
  100.8 5.3 %layer.9 = (f32[128,1024]{1,0:T(8,128)S(1)}, bf16[128,1024]{1,0:T(8,128)(2,1)S(1)}, f32[128,1024]{1,0:T(8,128)S(1)}, bf16[128,1024]{1,0:T(8,128)(2,1)S(1)}) custom-call(s32[1]{0:T(128)} %bitcast.4.place_ref, bf16[128,1024]{1,0:T(8,128)(2,1)} %collective-permute-done.21.x_ref, f32[1,1024]{1,0:T(1,128)S(1)} %copy-done.20, bf16[8,128,1024]{2,1,0:T(8,128)(2,1)S(1)} %copy-done.6, ...), custom_call_target="tpu_custom_call" | custom-call | tf_op jit(solution)/shard_map/layer/pallas_call | solution.py:120
  110.9 3.5 %collective-permute-done.15.refs_0_ = f32[1,128]{1,0:T(1,128)S(1)} collective-permute-done((f32[1,128]{1,0:T(1,128)S(1)}, f32[1,128]{1,0:T(1,128)S(1)}, u32[]{:S(2)}, u32[]{:S(2)}) %collective-permute-start.15) | collective-permute-done | bytes 544 | tf_op jit(solution)/shard_map/ppermute | solution.py:177
  115.0 4.6 %layer.8 = (f32[128,1024]{1,0:T(8,128)S(1)}, bf16[128,1024]{1,0:T(8,128)(2,1)}, f32[128,1024]{1,0:T(8,128)S(1)}, bf16[128,1024]{1,0:T(8,128)(2,1)S(1)}) custom-call(s32[1]{0:T(128)} %bitcast.4.place_ref, bf16[128,1024]{1,0:T(8,128)(2,1)S(1)} %collective-permute-done.14.x_ref, f32[1,1024]{1,0:T(1,128)S(1)} %copy-done.20, bf16[8,128,1024]{2,1,0:T(8,128)(2,1)S(1)} %copy-done.6, ...), custom_call_target="tpu_custom_call" | custom-call | tf_op jit(solution)/shard_map/layer/pallas_call | solution.py:120
  125.0 9.4 %collective-permute-done.19 = bf16[128,1024]{1,0:T(8,128)(2,1)S(1)} collective-permute-done((bf16[128,1024]{1,0:T(8,128)(2,1)S(1)}, bf16[128,1024]{1,0:T(8,128)(2,1)S(1)}, u32[]{:S(2)}, u32[]{:S(2)}) %collective-permute-start.19) | collective-permute-done | bytes 262176 | tf_op jit(solution)/shard_map/ppermute | solution.py:177
  137.0 10.1 %collective-permute-done.25.refs_0_ = bf16[128,1024]{1,0:T(8,128)(2,1)S(1)} collective-permute-done((bf16[128,1024]{1,0:T(8,128)(2,1)S(1)}, bf16[128,1024]{1,0:T(8,128)(2,1)S(1)}, u32[]{:S(2)}, u32[]{:S(2)}) %collective-permute-start.25) | collective-permute-done | bytes 262176 | tf_op jit(solution)/shard_map/ppermute | solution.py:177
  153.7 3.3 %collective-permute-start.39 = (f32[1,128]{1,0:T(1,128)}, f32[1,128]{1,0:T(1,128)S(1)}, u32[]{:S(2)}, u32[]{:S(2)}) collective-permute-start(f32[1,128]{1,0:T(1,128)} %get-tuple-element.75), channel_id=1, source_target_pairs={{0,7},{1,6},{2,5},{3,4},{4,11},{5,10},{6,9},{7,8},{8,15},{9,14},{1... | collective-permute-start | bytes 1544 | tf_op jit(solution)/shard_map/ppermute | solution.py:177
  160.4 3.4 %copy-done.4 = bf16[1,1024,4096]{2,1,0:T(8,128)(2,1)S(1)} copy-done((bf16[1,1024,4096]{2,1,0:T(8,128)(2,1)S(1)}, bf16[1,1024,4096]{2,1,0:T(8,128)(2,1)}, u32[]{:S(2)}) %copy-start.4) | copy-done | bytes 8388632
  163.8 5.3 %layer.11 = (f32[128,1024]{1,0:T(8,128)S(1)}, bf16[128,1024]{1,0:T(8,128)(2,1)S(1)}, f32[128,1024]{1,0:T(8,128)S(1)}, bf16[128,1024]{1,0:T(8,128)(2,1)S(1)}) custom-call(s32[1]{0:T(128)} %bitcast.4.place_ref, bf16[128,1024]{1,0:T(8,128)(2,1)} %collective-permute-done.36.x_ref, f32[1,1024]{1,0:T(1,128)S(1)} %copy-done.20, ...), custom_call_target="tpu_custom_call" | custom-call | tf_op jit(solution)/shard_map/layer/pallas_call | solution.py:120
  175.3 4.7 %collective-permute-done.30.refs_0_ = f32[1,128]{1,0:T(1,128)S(1)} collective-permute-done((f32[1,128]{1,0:T(1,128)S(1)}, f32[1,128]{1,0:T(1,128)S(1)}, u32[]{:S(2)}, u32[]{:S(2)}) %collective-permute-start.30) | collective-permute-done | bytes 544 | tf_op jit(solution)/shard_map/ppermute | solution.py:177
  180.1 4.5 %layer.10 = (f32[128,1024]{1,0:T(8,128)S(1)}, bf16[128,1024]{1,0:T(8,128)(2,1)}, f32[128,1024]{1,0:T(8,128)S(1)}, bf16[128,1024]{1,0:T(8,128)(2,1)S(1)}) custom-call(s32[1]{0:T(128)} %bitcast.4.place_ref, bf16[128,1024]{1,0:T(8,128)(2,1)S(1)} %collective-permute-done.29.x_ref, f32[1,1024]{1,0:T(1,128)S(1)} %copy-done.20, ...), custom_call_target="tpu_custom_call" | custom-call | tf_op jit(solution)/shard_map/layer/pallas_call | solution.py:120
  191.1 9.1 %collective-permute-done.34 = bf16[128,1024]{1,0:T(8,128)(2,1)S(1)} collective-permute-done((bf16[128,1024]{1,0:T(8,128)(2,1)S(1)}, bf16[128,1024]{1,0:T(8,128)(2,1)S(1)}, u32[]{:S(2)}, u32[]{:S(2)}) %collective-permute-start.34) | collective-permute-done | bytes 262176 | tf_op jit(solution)/shard_map/ppermute | solution.py:177
  201.0 5.3 %collective-permute-done.40.refs_0_ = bf16[128,1024]{1,0:T(8,128)(2,1)S(1)} collective-permute-done((bf16[128,1024]{1,0:T(8,128)(2,1)S(1)}, bf16[128,1024]{1,0:T(8,128)(2,1)S(1)}, u32[]{:S(2)}, u32[]{:S(2)}) %collective-permute-start.40) | collective-permute-done | bytes 262176 | tf_op jit(solution)/shard_map/ppermute | solution.py:177
  212.7 5.5 %collective-permute-done.35.refs_1_ = bf16[128,1024]{1,0:T(8,128)(2,1)S(1)} collective-permute-done((bf16[128,1024]{1,0:T(8,128)(2,1)}, bf16[128,1024]{1,0:T(8,128)(2,1)S(1)}, u32[]{:S(2)}, u32[]{:S(2)}) %collective-permute-start.35) | collective-permute-done | bytes 262176 | tf_op jit(solution)/shard_map/ppermute | solution.py:177
  (167 shorter events, 88.6 us)
Async XLA Ops:
  0.0 17.3 %collective-permute-start.6 = (bf16[128,1024]{1,0:T(8,128)(2,1)}, bf16[128,1024]{1,0:T(8,128)(2,1)S(1)}, u32[]{:S(2)}, u32[]{:S(2)}) collective-permute-start(bf16[128,1024]{1,0:T(8,128)(2,1)} %bitcast.48), channel_id=1, source_target_pairs={{0,28},{1,29},{2,30},{3,31},{4,24},{5,25},{6,26},{7,27},{8,20},{9,... | collective-permute-start | bytes 786440 | tf_op jit(solution)/shard_map/ppermute | solution.py:177
  30.1 25.7 %collective-permute-start.11 = (bf16[128,1024]{1,0:T(8,128)(2,1)}, bf16[128,1024]{1,0:T(8,128)(2,1)}, u32[]{:S(2)}, u32[]{:S(2)}) collective-permute-start(bf16[128,1024]{1,0:T(8,128)(2,1)} %get-tuple-element.51), channel_id=1, source_target_pairs={{0,1},{1,0},{2,3},{3,2},{4,5},{5,4},{6,7},{7,6},{8,9},{9,8},{10,11... | collective-permute-start | bytes 786440 | tf_op jit(solution)/shard_map/ppermute | solution.py:177
  31.8 12.6 %collective-permute-start = (f32[1,128]{1,0:T(1,128)}, f32[1,128]{1,0:T(1,128)S(1)}, u32[]{:S(2)}, u32[]{:S(2)}) collective-permute-start(f32[1,128]{1,0:T(1,128)} %squares.2), channel_id=1, source_target_pairs={{0,1},{1,0},{2,3},{3,2},{4,5},{5,4},{6,7},{7,6},{8,9},{9,8},{10,11... | collective-permute-start | bytes 1544 | tf_op jit(solution)/shard_map/ppermute | solution.py:177
  51.9 17.7 %collective-permute-start.4 = (bf16[128,1024]{1,0:T(8,128)(2,1)S(1)}, bf16[128,1024]{1,0:T(8,128)(2,1)S(1)}, u32[]{:S(2)}, u32[]{:S(2)}) collective-permute-start(bf16[128,1024]{1,0:T(8,128)(2,1)S(1)} %get-tuple-element.46), channel_id=1, source_target_pairs={{0,1},{1,0},{2,3},{3,2},{4,5},{5,4},{6,7},{7,6},{8,9},{9,8},{10,11... | collective-permute-start | bytes 786440 | tf_op jit(solution)/shard_map/ppermute | solution.py:177
  53.8 29.7 %collective-permute-start.3 = (bf16[128,1024]{1,0:T(8,128)(2,1)}, bf16[128,1024]{1,0:T(8,128)(2,1)S(1)}, u32[]{:S(2)}, u32[]{:S(2)}) collective-permute-start(bf16[128,1024]{1,0:T(8,128)(2,1)} %get-tuple-element.44), channel_id=1, source_target_pairs={{0,1},{1,0},{2,3},{3,2},{4,5},{5,4},{6,7},{7,6},{8,9},{9,8},{10,11... | collective-permute-start | bytes 786440 | tf_op jit(solution)/shard_map/ppermute | solution.py:177
  54.7 25.3 %collective-permute-start.10 = (bf16[128,1024]{1,0:T(8,128)(2,1)}, bf16[128,1024]{1,0:T(8,128)(2,1)}, u32[]{:S(2)}, u32[]{:S(2)}) collective-permute-start(bf16[128,1024]{1,0:T(8,128)(2,1)} %get-tuple-element.49), channel_id=1, source_target_pairs={{0,1},{1,0},{2,3},{3,2},{4,5},{5,4},{6,7},{7,6},{8,9},{9,8},{10,11... | collective-permute-start | bytes 786440 | tf_op jit(solution)/shard_map/ppermute | solution.py:177
  57.6 22.4 %collective-permute-start.12 = (bf16[128,1024]{1,0:T(8,128)(2,1)}, bf16[128,1024]{1,0:T(8,128)(2,1)}, u32[]{:S(2)}, u32[]{:S(2)}) collective-permute-start(bf16[128,1024]{1,0:T(8,128)(2,1)} %add_convert_fusion.4), channel_id=1, source_target_pairs={{0,2},{1,3},{2,0},{3,1},{4,6},{5,7},{6,4},{7,5},{8,10},{9,11},{10,... | collective-permute-start | bytes 786440 | tf_op jit(solution)/shard_map/ppermute | solution.py:177
  70.3 15.2 %collective-permute-start.5 = (bf16[128,1024]{1,0:T(8,128)(2,1)}, bf16[128,1024]{1,0:T(8,128)(2,1)}, u32[]{:S(2)}, u32[]{:S(2)}) collective-permute-start(bf16[128,1024]{1,0:T(8,128)(2,1)} %add_convert_fusion.5), channel_id=1, source_target_pairs={{0,2},{1,3},{2,0},{3,1},{4,6},{5,7},{6,4},{7,5},{8,10},{9,11},{10,... | collective-permute-start | bytes 786440 | tf_op jit(solution)/shard_map/ppermute | solution.py:177
  82.4 15.0 %collective-permute-start.21 = (bf16[128,1024]{1,0:T(8,128)(2,1)}, bf16[128,1024]{1,0:T(8,128)(2,1)}, u32[]{:S(2)}, u32[]{:S(2)}) collective-permute-start(bf16[128,1024]{1,0:T(8,128)(2,1)} %get-tuple-element.60), channel_id=1, source_target_pairs={{0,4},{1,5},{2,6},{3,7},{4,8},{5,9},{6,10},{7,11},{8,12},{9,13},{1... | collective-permute-start | bytes 786440 | tf_op jit(solution)/shard_map/ppermute | solution.py:177
  87.9 27.0 %collective-permute-start.14 = (bf16[128,1024]{1,0:T(8,128)(2,1)}, bf16[128,1024]{1,0:T(8,128)(2,1)S(1)}, u32[]{:S(2)}, u32[]{:S(2)}) collective-permute-start(bf16[128,1024]{1,0:T(8,128)(2,1)} %get-tuple-element.53), channel_id=1, source_target_pairs={{0,4},{1,5},{2,6},{3,7},{4,8},{5,9},{6,10},{7,11},{8,12},{9,13},{1... | collective-permute-start | bytes 786440 | tf_op jit(solution)/shard_map/ppermute | solution.py:177
  106.9 14.9 %collective-permute-start.26 = (bf16[128,1024]{1,0:T(8,128)(2,1)S(1)}, bf16[128,1024]{1,0:T(8,128)(2,1)S(1)}, u32[]{:S(2)}, u32[]{:S(2)}) collective-permute-start(bf16[128,1024]{1,0:T(8,128)(2,1)S(1)} %get-tuple-element.65), channel_id=1, source_target_pairs={{0,1},{1,0},{2,3},{3,2},{4,5},{5,4},{6,7},{7,6},{8,9},{9,8},{10,11... | collective-permute-start | bytes 786440 | tf_op jit(solution)/shard_map/ppermute | solution.py:177
  119.5 14.9 %collective-permute-start.19 = (bf16[128,1024]{1,0:T(8,128)(2,1)S(1)}, bf16[128,1024]{1,0:T(8,128)(2,1)S(1)}, u32[]{:S(2)}, u32[]{:S(2)}) collective-permute-start(bf16[128,1024]{1,0:T(8,128)(2,1)S(1)} %get-tuple-element.58), channel_id=1, source_target_pairs={{0,1},{1,0},{2,3},{3,2},{4,5},{5,4},{6,7},{7,6},{8,9},{9,8},{10,11... | collective-permute-start | bytes 786440 | tf_op jit(solution)/shard_map/ppermute | solution.py:177
  119.8 33.9 %collective-permute-start.18 = (bf16[128,1024]{1,0:T(8,128)(2,1)}, bf16[128,1024]{1,0:T(8,128)(2,1)S(1)}, u32[]{:S(2)}, u32[]{:S(2)}) collective-permute-start(bf16[128,1024]{1,0:T(8,128)(2,1)} %get-tuple-element.56), channel_id=1, source_target_pairs={{0,1},{1,0},{2,3},{3,2},{4,5},{5,4},{6,7},{7,6},{8,9},{9,8},{10,11... | collective-permute-start | bytes 786440 | tf_op jit(solution)/shard_map/ppermute | solution.py:177
  121.6 25.5 %collective-permute-start.25 = (bf16[128,1024]{1,0:T(8,128)(2,1)S(1)}, bf16[128,1024]{1,0:T(8,128)(2,1)S(1)}, u32[]{:S(2)}, u32[]{:S(2)}) collective-permute-start(bf16[128,1024]{1,0:T(8,128)(2,1)S(1)} %get-tuple-element.63), channel_id=1, source_target_pairs={{0,1},{1,0},{2,3},{3,2},{4,5},{5,4},{6,7},{7,6},{8,9},{9,8},{10,11... | collective-permute-start | bytes 786440 | tf_op jit(solution)/shard_map/ppermute | solution.py:177
  121.9 26.0 %collective-permute-start.27 = (bf16[128,1024]{1,0:T(8,128)(2,1)S(1)}, bf16[128,1024]{1,0:T(8,128)(2,1)S(1)}, u32[]{:S(2)}, u32[]{:S(2)}) collective-permute-start(bf16[128,1024]{1,0:T(8,128)(2,1)S(1)} %add_convert_fusion.2), channel_id=1, source_target_pairs={{0,2},{1,3},{2,0},{3,1},{4,6},{5,7},{6,4},{7,5},{8,10},{9,11},{10,... | collective-permute-start | bytes 786440 | tf_op jit(solution)/shard_map/ppermute | solution.py:177
  135.2 22.9 %collective-permute-start.20 = (bf16[128,1024]{1,0:T(8,128)(2,1)}, bf16[128,1024]{1,0:T(8,128)(2,1)}, u32[]{:S(2)}, u32[]{:S(2)}) collective-permute-start(bf16[128,1024]{1,0:T(8,128)(2,1)} %add_convert_fusion.3), channel_id=1, source_target_pairs={{0,2},{1,3},{2,0},{3,1},{4,6},{5,7},{6,4},{7,5},{8,10},{9,11},{10,... | collective-permute-start | bytes 786440 | tf_op jit(solution)/shard_map/ppermute | solution.py:177
  160.4 19.7 %collective-permute-start.29 = (bf16[128,1024]{1,0:T(8,128)(2,1)}, bf16[128,1024]{1,0:T(8,128)(2,1)S(1)}, u32[]{:S(2)}, u32[]{:S(2)}) collective-permute-start(bf16[128,1024]{1,0:T(8,128)(2,1)} %get-tuple-element.67), channel_id=1, source_target_pairs={{0,4},{1,5},{2,6},{3,7},{4,8},{5,9},{6,10},{7,11},{8,12},{9,13},{1... | collective-permute-start | bytes 786440 | tf_op jit(solution)/shard_map/ppermute | solution.py:177
  169.9 17.6 %collective-permute-start.41 = (bf16[128,1024]{1,0:T(8,128)(2,1)S(1)}, bf16[128,1024]{1,0:T(8,128)(2,1)S(1)}, u32[]{:S(2)}, u32[]{:S(2)}) collective-permute-start(bf16[128,1024]{1,0:T(8,128)(2,1)S(1)} %get-tuple-element.79), channel_id=1, source_target_pairs={{0,1},{1,0},{2,3},{3,2},{4,5},{5,4},{6,7},{7,6},{8,9},{9,8},{10,11... | collective-permute-start | bytes 786440 | tf_op jit(solution)/shard_map/ppermute | solution.py:177
  185.4 14.9 %collective-permute-start.34 = (bf16[128,1024]{1,0:T(8,128)(2,1)S(1)}, bf16[128,1024]{1,0:T(8,128)(2,1)S(1)}, u32[]{:S(2)}, u32[]{:S(2)}) collective-permute-start(bf16[128,1024]{1,0:T(8,128)(2,1)S(1)} %get-tuple-element.72), channel_id=1, source_target_pairs={{0,1},{1,0},{2,3},{3,2},{4,5},{5,4},{6,7},{7,6},{8,9},{9,8},{10,11... | collective-permute-start | bytes 786440 | tf_op jit(solution)/shard_map/ppermute | solution.py:177
  185.6 20.8 %collective-permute-start.40 = (bf16[128,1024]{1,0:T(8,128)(2,1)S(1)}, bf16[128,1024]{1,0:T(8,128)(2,1)S(1)}, u32[]{:S(2)}, u32[]{:S(2)}) collective-permute-start(bf16[128,1024]{1,0:T(8,128)(2,1)S(1)} %get-tuple-element.77), channel_id=1, source_target_pairs={{0,1},{1,0},{2,3},{3,2},{4,5},{5,4},{6,7},{7,6},{8,9},{9,8},{10,11... | collective-permute-start | bytes 786440 | tf_op jit(solution)/shard_map/ppermute | solution.py:177
  187.5 18.8 %collective-permute-start.42 = (bf16[128,1024]{1,0:T(8,128)(2,1)S(1)}, bf16[128,1024]{1,0:T(8,128)(2,1)S(1)}, u32[]{:S(2)}, u32[]{:S(2)}) collective-permute-start(bf16[128,1024]{1,0:T(8,128)(2,1)S(1)} %add_convert_fusion), channel_id=1, source_target_pairs={{0,2},{1,3},{2,0},{3,1},{4,6},{5,7},{6,4},{7,5},{8,10},{9,11},{10,... | collective-permute-start | bytes 786440 | tf_op jit(solution)/shard_map/ppermute | solution.py:177
  188.5 21.0 %collective-permute-start.13 = (bf16[128,1024]{1,0:T(8,128)(2,1)S(1)}, bf16[128,1024]{1,0:T(8,128)(2,1)S(1)}, u32[]{:S(2)}, u32[]{:S(2)}) collective-permute-start(bf16[128,1024]{1,0:T(8,128)(2,1)S(1)} %copy-done.32), channel_id=1, source_target_pairs={{0,28},{1,29},{2,30},{3,31},{4,24},{5,25},{6,26},{7,27},{8,20},{9,... | collective-permute-start | bytes 786440 | tf_op jit(solution)/shard_map/ppermute | solution.py:177
  188.5 21.1 %collective-permute-start.28 = (bf16[128,1024]{1,0:T(8,128)(2,1)}, bf16[128,1024]{1,0:T(8,128)(2,1)S(1)}, u32[]{:S(2)}, u32[]{:S(2)}) collective-permute-start(bf16[128,1024]{1,0:T(8,128)(2,1)} %get-tuple-element.66), channel_id=1, source_target_pairs={{0,28},{1,29},{2,30},{3,31},{4,24},{5,25},{6,26},{7,27},{8,20},{9,... | collective-permute-start | bytes 786440 | tf_op jit(solution)/shard_map/ppermute | solution.py:177
  200.3 12.4 %collective-permute-start.33 = (bf16[128,1024]{1,0:T(8,128)(2,1)}, bf16[128,1024]{1,0:T(8,128)(2,1)S(1)}, u32[]{:S(2)}, u32[]{:S(2)}) collective-permute-start(bf16[128,1024]{1,0:T(8,128)(2,1)} %get-tuple-element.70), channel_id=1, source_target_pairs={{0,1},{1,0},{2,3},{3,2},{4,5},{5,4},{6,7},{7,6},{8,9},{9,8},{10,11... | collective-permute-start | bytes 786440 | tf_op jit(solution)/shard_map/ppermute | solution.py:177
  (56 other events, 465.2 us)

commit v2 on v1

--- a/solution.py
+++ b/solution.py
@@ -19,6 +19,7 @@
 IN_VMEM = pl.BlockSpec(memory_space=pltpu.VMEM)
 IN_SMEM = pl.BlockSpec(memory_space=pltpu.SMEM)
 IN_PLACE = pl.BlockSpec(memory_space=pl.ANY)
+IN_HBM = pl.BlockSpec(memory_space=pltpu.HBM)
 
 
 def toeplitz_kernel(taps_ref, filters_ref, blocks_ref):
@@ -45,6 +46,7 @@
         out_shape=jax.ShapeDtypeStruct((groups // PER_BLOCK, seq, PER_BLOCK * seq), jnp.bfloat16),
         in_specs=[IN_SMEM, IN_VMEM],
         out_specs=IN_VMEM,
+        compiler_params=pltpu.CompilerParams(vmem_limit_bytes=6 * 2**20),
         name="toeplitz",
     )(taps, filters)
 
@@ -58,22 +60,25 @@
     return jnp.sum(total.T, axis=0, keepdims=True)
 
 
-def squares_kernel(values_ref, squares_ref):
-    squares_ref[...] = row_squares(values_ref[...].astype(jnp.float32))
-
-
-def squares_of(values):
-    return pl.pallas_call(
-        squares_kernel,
-        out_shape=jax.ShapeDtypeStruct((1, values.shape[0]), jnp.float32),
-        in_specs=[IN_VMEM],
-        out_specs=IN_VMEM,
+def squares_kernel(count, *refs):
+    for values_ref, squares_ref in zip(refs[:count], refs[count:]):
+        squares_ref[...] = row_squares(values_ref[...].astype(jnp.float32))
+
+
+def squares_of(*arrays):
+    return pl.pallas_call(
+        functools.partial(squares_kernel, len(arrays)),
+        out_shape=[jax.ShapeDtypeStruct((1, array.shape[0]), jnp.float32) for array in arrays],
+        in_specs=[IN_VMEM] * len(arrays),
+        out_specs=[IN_VMEM] * len(arrays),
+        compiler_params=pltpu.CompilerParams(vmem_limit_bytes=6 * 2**20),
         name="squares",
-    )(values)
+    )(*arrays)
 
 
 def layer_kernel(count, place_ref, x_ref, gains_ref, blocks_ref, weight_ref, *refs):
     squares_refs, refs = refs[: count - 1], refs[count - 1 :]
+    refs = refs[-count - 3 :]
     out_refs, (weight_buf, gated_buf, sems) = refs[:count], refs[count:]
     place = place_ref[0]
     seq, channels = x_ref.shape
@@ -114,22 +119,29 @@
         ).astype(out_refs[apart].dtype)
 
 
-def layer_partials(x, squares, place, gains, blocks, weight, count):
+def layer_partials(x, squares, place, gains, blocks, weight, count, after):
     seq, channels = x.shape
     kinds = [jnp.bfloat16 if apart % 2 else jnp.float32 for apart in range(count)]
     return pl.pallas_call(
         functools.partial(layer_kernel, count),
         out_shape=[jax.ShapeDtypeStruct((seq, channels), kind) for kind in kinds],
-        in_specs=[IN_SMEM, IN_VMEM, IN_VMEM, IN_VMEM, IN_PLACE] + [IN_VMEM] * (count - 1),
+        in_specs=[IN_SMEM, IN_VMEM, IN_VMEM, IN_VMEM, IN_HBM]
+        + [IN_VMEM] * (count - 1)
+        + [IN_PLACE] * len(after),
         out_specs=[IN_VMEM] * count,
         scratch_shapes=[
             pltpu.VMEM((count, channels, channels), jnp.bfloat16),
             pltpu.VMEM((seq, channels), jnp.bfloat16),
             pltpu.SemaphoreType.DMA((count,)),
         ],
-        compiler_params=pltpu.CompilerParams(vmem_limit_bytes=40 * 2**20),
+        compiler_params=pltpu.CompilerParams(vmem_limit_bytes=20 * 2**20),
+        cost_estimate=pl.CostEstimate(
+            flops=2 * seq * channels * (channels * count + PER_BLOCK * seq),
+            transcendentals=0,
+            bytes_accessed=2 * channels * channels * count,
+        ),
         name="layer",
-    )(place, x, gains, blocks, weight, *squares)
+    )(place, x, gains, blocks, weight, *squares, *after)
 
 
 def merge_kernel(count, last_ref, x_ref, fresh_ref, own_ref, *refs):
@@ -155,6 +167,7 @@
         ],
         in_specs=[IN_SMEM] + [IN_VMEM] * (3 + len(arrived)),
         out_specs=[IN_VMEM] * 3,
+        compiler_params=pltpu.CompilerParams(vmem_limit_bytes=6 * 2**20),
         name="merge",
     )(last, x, fresh, own, *arrived)
 
@@ -180,18 +193,24 @@
 def add_up(partials):
     count = len(partials)
     partials = list(partials)
-    arrived = []
+    arrived, early = [], None
     bit = 1
     while bit < count:
         for apart in reversed(range(bit, count, 2 * bit)):
             outgoing = partials[apart].astype(jnp.bfloat16)
+            if apart == bit and bit < count // 2:
+                ahead = partials[2 * bit].astype(jnp.bfloat16)
+                early = ahead if early is None else early
+                outgoing, partials[2 * bit] = lax.optimization_barrier((outgoing, ahead))
             incoming = send(outgoing, lambda k, z: (k, z ^ bit))
             if apart == bit:
                 arrived.append(incoming)
             else:
-                partials[apart ^ bit] = partials[apart ^ bit] + incoming.astype(jnp.float32)
+                partials[apart ^ bit] = partials[apart ^ bit].astype(
+                    jnp.float32
+                ) + incoming.astype(jnp.float32)
         bit *= 2
-    return arrived
+    return arrived, early
 
 
 def local(
@@ -217,9 +236,9 @@
         ]
 
     entering = [down_state[0], up_state[0]]
-    squares = [squares_of(values) for values in entering]
+    squares = squares_of(*entering)
+    entering[1] = send(entering[1], lambda k, z: (mirrored(k), z))
     squares = [spread_squares(squares[0], lambda k: k), spread_squares(squares[1], mirrored)]
-    entering[1] = send(entering[1], lambda k, z: (mirrored(k), z))
     blocks = toeplitz_blocks(conv_filters[0], taps)
     fresh = [
         [
@@ -228,21 +247,23 @@
         ]
         for way in range(2)
     ]
-    records = []
+    leaving = [[], []]
+    after = []
     for tick in range(TICK_COUNT):
-        leaving = []
-        for way in range(2):
+        for way in (1, 0):
             x = entering[way]
-            partials = layer_partials(x, squares[way], place, gains, blocks, weight, tensor)
-            arrived = add_up(partials)
+            partials = layer_partials(
+                x, squares[way], place, gains, blocks, weight, tensor, after
+            )
+            arrived, early = add_up(partials)
+            after = [] if early is None else [early]
             newcomer = fresh[way][min(tick, TICK_COUNT - 2)]
             y, sent, own = merge(x, newcomer, partials[0], arrived, last)
             if tick < TICK_COUNT - 1:
                 squares[way] = spread_squares(own, following)
                 entering[way] = send(sent, lambda k, z: (following(k), z))
-            leaving.append(y if way == 0 else send(y, lambda k, z: (mirrored(k), z)))
-        records.append(jnp.stack(leaving))
-    return jnp.stack(records)[:, :, None]
+            leaving[way].append(send(y, lambda k, z: (mirrored(k), z)) if way else y)
+    return jnp.stack([jnp.stack(way) for way in leaving], axis=1)[:, :, None]
 
 
 def solution(mesh):

time: 224 us -> 166 us (0.74)
  waiting for transfers between devices: 81.2 us -> 52.4 us
  Pallas kernels: 48.5 us -> 30.6 us
  local copies, waits for them, and re-layouts: 25.1 us -> 16.2 us
  starting transfers between devices: 50.1 us -> 55.4 us
  other arithmetic: 6.6 us -> 1.84 us
  matrix products: 4.25 us -> 1.39 us
    ppermute x44, waiting for transfers between devices: 81.2 us -> 52.4 us  [send(): return lax.ppermute(values, ('pipe', 'tensor'), pairs)]
    pallas_call x6, Pallas kernels: 14.2 us -> 3.6 us  [merge(): pl.pallas_call(functools.partial(merge_kernel, len(arrived)), out_shape=[...]
    unnamed x72 -> x34, local copies, waits for them, and re-layouts: 23.7 us -> 13.4 us
    ppermute x44, starting transfers between devices: 50.1 us -> 55.4 us  [send(): return lax.ppermute(values, ('pipe', 'tensor'), pairs)]
    pallas_call x2 -> x1, Pallas kernels: 3.24 us -> 0.18 us  [squares_of(): pl.pallas_call(functools.partial(squares_kernel, len(arrays)), out_shape=...]
    dot_general x4, matrix products: 4.25 us -> 1.39 us  [embed_tokens(): jnp.dot(onehot, table, preferred_element_type=jnp.float32)]
    convert_element_type x6, other arithmetic: 4.1 us -> 1.52 us  [add_up(): ahead = partials[2 * bit].astype(jnp.bfloat16)]
  transfers between devices with their start and end apart: 44 -> 44, of which waited for: 15 -> 16; matrix products, arithmetic and copies ran while one was open for 4% -> 3% of each run, Pallas kernels for 20% -> 15%
where the time goes in v2:
time: 166 us; the launch traced here: 165 us
  starting transfers between devices  55.4 us (33%)
  waiting for transfers between devices  52.4 us (32%)
  Pallas kernels  30.6 us (18%)
  local copies, waits for them, and re-layouts  16.2 us (10%)
  between operations  7.56 us (5%)
  other arithmetic  1.84 us (1%)
    ppermute x44, starting transfers between devices, send(): return lax.ppermute(values, ('pipe', 'tensor'), pairs)  55.4 us
    ppermute x44, waiting for transfers between devices, send(): return lax.ppermute(values, ('pipe', 'tensor'), pairs)  52.4 us
    pallas_call x6, Pallas kernels, layer_partials(): pl.pallas_call(functools.partial(layer_kernel, count), out_shape=[jax.Sha...  26.1 us
    unnamed x34, local copies, waits for them, and re-layouts  13.4 us
    pallas_call x6, Pallas kernels, merge(): pl.pallas_call(functools.partial(merge_kernel, len(arrived)), out_shape=[...  3.6 us
  transfers between devices with their start and end apart: 44, of which 16 were waited for; matrix products, arithmetic and copies ran while one was open for 3% of the time, Pallas kernels for 15%

profile of v2, /device:TPU:0, one launch (start us, length us, event | category | flops | bytes accessed | tf_op | source)
XLA Modules:
  0.0 165.3 jit_solution(11104298034031727725)
XLA Ops:
  0.0 3.3 %collective-permute-start.3 = (bf16[128,1024]{1,0:T(8,128)(2,1)}, bf16[128,1024]{1,0:T(8,128)(2,1)S(1)}, u32[]{:S(2)}, u32[]{:S(2)}) collective-permute-start(bf16[128,1024]{1,0:T(8,128)(2,1)} %bitcast.44), channel_id=1, source_target_pairs={{0,28},{1,29},{2,30},{3,31},{4,24},{5,25},{6,26},{7,27},{8,20},{9,... | collective-permute-start | bytes 786440 | tf_op jit(solution)/shard_map/ppermute | solution.py:190
  7.3 3.9 %collective-permute-start.5 = (f32[1,128]{1,0:T(1,128)S(1)}, f32[1,128]{1,0:T(1,128)S(1)}, u32[]{:S(2)}, u32[]{:S(2)}) collective-permute-start(f32[1,128]{1,0:T(1,128)S(1)} %get-tuple-element.58), channel_id=1, source_target_pairs={{0,30},{1,31},{2,28},{3,29},{4,26},{5,27},{6,24},{7,25},{8,22},{9,... | collective-permute-start | bytes 1544 | tf_op jit(solution)/shard_map/ppermute | solution.py:190
  12.9 4.8 %collective-permute-done.6.refs_2_ = f32[1,128]{1,0:T(1,128)S(1)} collective-permute-done((f32[1,128]{1,0:T(1,128)S(1)}, f32[1,128]{1,0:T(1,128)S(1)}, u32[]{:S(2)}, u32[]{:S(2)}) %collective-permute-start.6) | collective-permute-done | bytes 544 | tf_op jit(solution)/shard_map/ppermute | solution.py:190
  18.4 3.4 %copy-done.1 = bf16[1,1024,4096]{2,1,0:T(8,128)(2,1)S(1)} copy-done((bf16[1,1024,4096]{2,1,0:T(8,128)(2,1)S(1)}, bf16[1,1024,4096]{2,1,0:T(8,128)(2,1)}, u32[]{:S(2)}) %copy-start.1) | copy-done | bytes 8388632
  22.8 4.6 %layer.6 = (f32[128,1024]{1,0:T(8,128)S(1)}, bf16[128,1024]{1,0:T(8,128)(2,1)S(1)}, f32[128,1024]{1,0:T(8,128)S(1)}, bf16[128,1024]{1,0:T(8,128)(2,1)}) custom-call(s32[1]{0:T(128)} %bitcast.4.place_ref, bf16[128,1024]{1,0:T(8,128)(2,1)S(1)} %copy-done.7, f32[1,1024]{1,0:T(1,128)S(1)} %copy-done.13, bf16[8,128,1024]{2,1,0:T(8,128)(2,1)S(1)} %toeplitz.1.blocks_ref, ...), custom_call_target="tpu_custom_call" | custom-call | flops 1342177280 | bytes 8388608 | tf_op jit(solution)/shard_map/layer/pallas_call | solution.py:125
  46.1 3.4 %copy-done.2 = bf16[1,1024,4096]{2,1,0:T(8,128)(2,1)S(1)} copy-done((bf16[1,1024,4096]{2,1,0:T(8,128)(2,1)S(1)}, bf16[1,1024,4096]{2,1,0:T(8,128)(2,1)}, u32[]{:S(2)}) %copy-start.2) | copy-done | bytes 8388632
  49.4 4.3 %layer.7 = (f32[128,1024]{1,0:T(8,128)S(1)}, bf16[128,1024]{1,0:T(8,128)(2,1)S(1)}, f32[128,1024]{1,0:T(8,128)S(1)}, bf16[128,1024]{1,0:T(8,128)(2,1)S(1)}) custom-call(s32[1]{0:T(128)} %bitcast.4.place_ref, bf16[128,1024]{1,0:T(8,128)(2,1)S(1)} %bitcast.42, f32[1,1024]{1,0:T(1,128)S(1)} %copy-done.13, bf16[8,128,1024]{2,1,0:T(8,128)(2,1)S(1)} %toeplitz.1.blocks_ref, ...), custom_call_target="tpu_custom_call" | custom-call | flops 1342177280 | bytes 8388608 | tf_op jit(solution)/shard_map/layer/pallas_call | solution.py:125
  54.7 3.4 %collective-permute-done.15.refs_0_ = bf16[128,1024]{1,0:T(8,128)(2,1)S(1)} collective-permute-done((bf16[128,1024]{1,0:T(8,128)(2,1)}, bf16[128,1024]{1,0:T(8,128)(2,1)S(1)}, u32[]{:S(2)}, u32[]{:S(2)}) %collective-permute-start.15) | collective-permute-done | bytes 262176 | tf_op jit(solution)/shard_map/ppermute | solution.py:190
  61.8 3.2 %collective-permute-start.20 = (f32[1,128]{1,0:T(1,128)S(1)}, f32[1,128]{1,0:T(1,128)S(1)}, u32[]{:S(2)}, u32[]{:S(2)}) collective-permute-start(f32[1,128]{1,0:T(1,128)S(1)} %get-tuple-element.75), channel_id=1, source_target_pairs={{0,7},{1,6},{2,5},{3,4},{4,11},{5,10},{6,9},{7,8},{8,15},{9,14},{1... | collective-permute-start | bytes 1544 | tf_op jit(solution)/shard_map/ppermute | solution.py:190
  68.4 4.3 %layer.8 = (f32[128,1024]{1,0:T(8,128)S(1)}, bf16[128,1024]{1,0:T(8,128)(2,1)S(1)}, f32[128,1024]{1,0:T(8,128)S(1)}, bf16[128,1024]{1,0:T(8,128)(2,1)S(1)}) custom-call(s32[1]{0:T(128)} %bitcast.4.place_ref, bf16[128,1024]{1,0:T(8,128)(2,1)S(1)} %collective-permute-done.17.x_ref, f32[1,1024]{1,0:T(1,128)S(1)} %copy-done.13, ...), custom_call_target="tpu_custom_call" | custom-call | flops 1342177280 | bytes 8388608 | tf_op jit(solution)/shard_map/layer/pallas_call | solution.py:125
  73.1 6.8 %collective-permute-done.9.refs_0_ = bf16[128,1024]{1,0:T(8,128)(2,1)S(1)} collective-permute-done((bf16[128,1024]{1,0:T(8,128)(2,1)S(1)}, bf16[128,1024]{1,0:T(8,128)(2,1)S(1)}, u32[]{:S(2)}, u32[]{:S(2)}) %collective-permute-start.9) | collective-permute-done | bytes 262176 | tf_op jit(solution)/shard_map/ppermute | solution.py:190
  83.0 3.7 %collective-permute-start.14 = (f32[1,128]{1,0:T(1,128)S(1)}, f32[1,128]{1,0:T(1,128)S(1)}, u32[]{:S(2)}, u32[]{:S(2)}) collective-permute-start(f32[1,128]{1,0:T(1,128)S(1)} %get-tuple-element.69), channel_id=1, source_target_pairs={{0,7},{1,6},{2,5},{3,4},{4,11},{5,10},{6,9},{7,8},{8,15},{9,14},{1... | collective-permute-start | bytes 1544 | tf_op jit(solution)/shard_map/ppermute | solution.py:190
  89.6 4.3 %layer.9 = (f32[128,1024]{1,0:T(8,128)S(1)}, bf16[128,1024]{1,0:T(8,128)(2,1)S(1)}, f32[128,1024]{1,0:T(8,128)S(1)}, bf16[128,1024]{1,0:T(8,128)(2,1)S(1)}) custom-call(s32[1]{0:T(128)} %bitcast.4.place_ref, bf16[128,1024]{1,0:T(8,128)(2,1)S(1)} %collective-permute-done.11.x_ref, f32[1,1024]{1,0:T(1,128)S(1)} %copy-done.13, ...), custom_call_target="tpu_custom_call" | custom-call | flops 1342177280 | bytes 8388608 | tf_op jit(solution)/shard_map/layer/pallas_call | solution.py:125
  94.3 7.2 %collective-permute-done.29.refs_0_ = bf16[128,1024]{1,0:T(8,128)(2,1)S(1)} collective-permute-done((bf16[128,1024]{1,0:T(8,128)(2,1)S(1)}, bf16[128,1024]{1,0:T(8,128)(2,1)S(1)}, u32[]{:S(2)}, u32[]{:S(2)}) %collective-permute-start.29) | collective-permute-done | bytes 262176 | tf_op jit(solution)/shard_map/ppermute | solution.py:190
  104.6 2.8 %collective-permute-start.34 = (f32[1,128]{1,0:T(1,128)S(1)}, f32[1,128]{1,0:T(1,128)S(1)}, u32[]{:S(2)}, u32[]{:S(2)}) collective-permute-start(f32[1,128]{1,0:T(1,128)S(1)} %get-tuple-element.92), channel_id=1, source_target_pairs={{0,7},{1,6},{2,5},{3,4},{4,11},{5,10},{6,9},{7,8},{8,15},{9,14},{1... | collective-permute-start | bytes 1544 | tf_op jit(solution)/shard_map/ppermute | solution.py:190
  111.1 4.3 %layer.10 = (f32[128,1024]{1,0:T(8,128)S(1)}, bf16[128,1024]{1,0:T(8,128)(2,1)S(1)}, f32[128,1024]{1,0:T(8,128)S(1)}, bf16[128,1024]{1,0:T(8,128)(2,1)S(1)}) custom-call(s32[1]{0:T(128)} %bitcast.4.place_ref, bf16[128,1024]{1,0:T(8,128)(2,1)S(1)} %collective-permute-done.31.x_ref, f32[1,1024]{1,0:T(1,128)S(1)} %copy-done.13, ...), custom_call_target="tpu_custom_call" | custom-call | flops 1342177280 | bytes 8388608 | tf_op jit(solution)/shard_map/layer/pallas_call | solution.py:125
  115.9 6.4 %collective-permute-done.23.refs_0_ = bf16[128,1024]{1,0:T(8,128)(2,1)S(1)} collective-permute-done((bf16[128,1024]{1,0:T(8,128)(2,1)S(1)}, bf16[128,1024]{1,0:T(8,128)(2,1)S(1)}, u32[]{:S(2)}, u32[]{:S(2)}) %collective-permute-start.23) | collective-permute-done | bytes 262176 | tf_op jit(solution)/shard_map/ppermute | solution.py:190
  125.5 3.5 %collective-permute-start.28 = (f32[1,128]{1,0:T(1,128)S(1)}, f32[1,128]{1,0:T(1,128)S(1)}, u32[]{:S(2)}, u32[]{:S(2)}) collective-permute-start(f32[1,128]{1,0:T(1,128)S(1)} %get-tuple-element.86), channel_id=1, source_target_pairs={{0,7},{1,6},{2,5},{3,4},{4,11},{5,10},{6,9},{7,8},{8,15},{9,14},{1... | collective-permute-start | bytes 1544 | tf_op jit(solution)/shard_map/ppermute | solution.py:190
  129.2 2.8 %collective-permute-start.42 = (bf16[128,1024]{1,0:T(8,128)(2,1)S(1)}, bf16[128,1024]{1,0:T(8,128)(2,1)S(1)}, u32[]{:S(2)}, u32[]{:S(2)}) collective-permute-start(bf16[128,1024]{1,0:T(8,128)(2,1)S(1)} %add_convert_fusion.1.refs_3_), channel_id=1, source_target_pairs={{0,2},{1,3},{2,0},{3,1},{4,6},{5,7},{6,4},{7,5},{8,10},{9,11},{10,... | collective-permute-start | bytes 786440 | tf_op jit(solution)/shard_map/ppermute | solution.py:190
  132.1 4.3 %layer.11 = (f32[128,1024]{1,0:T(8,128)S(1)}, bf16[128,1024]{1,0:T(8,128)(2,1)S(1)}, f32[128,1024]{1,0:T(8,128)S(1)}, bf16[128,1024]{1,0:T(8,128)(2,1)S(1)}) custom-call(s32[1]{0:T(128)} %bitcast.4.place_ref, bf16[128,1024]{1,0:T(8,128)(2,1)S(1)} %collective-permute-done.25.x_ref, f32[1,1024]{1,0:T(1,128)S(1)} %copy-done.13, ...), custom_call_target="tpu_custom_call" | custom-call | flops 1342177280 | bytes 8388608 | tf_op jit(solution)/shard_map/layer/pallas_call | solution.py:125
  139.2 4.8 %collective-permute-done.41.refs_0_ = bf16[128,1024]{1,0:T(8,128)(2,1)S(1)} collective-permute-done((bf16[128,1024]{1,0:T(8,128)(2,1)S(1)}, bf16[128,1024]{1,0:T(8,128)(2,1)S(1)}, u32[]{:S(2)}, u32[]{:S(2)}) %collective-permute-start.41) | collective-permute-done | bytes 262176 | tf_op jit(solution)/shard_map/ppermute | solution.py:190
  144.9 3.6 %collective-permute-done.36 = bf16[128,1024]{1,0:T(8,128)(2,1)S(1)} collective-permute-done((bf16[128,1024]{1,0:T(8,128)(2,1)S(1)}, bf16[128,1024]{1,0:T(8,128)(2,1)S(1)}, u32[]{:S(2)}, u32[]{:S(2)}) %collective-permute-start.36) | collective-permute-done | bytes 262176 | tf_op jit(solution)/shard_map/ppermute | solution.py:190
  151.5 5.0 %collective-permute-done.43 = bf16[128,1024]{1,0:T(8,128)(2,1)S(1)} collective-permute-done((bf16[128,1024]{1,0:T(8,128)(2,1)S(1)}, bf16[128,1024]{1,0:T(8,128)(2,1)S(1)}, u32[]{:S(2)}, u32[]{:S(2)}) %collective-permute-start.43) | collective-permute-done | bytes 262176 | tf_op jit(solution)/shard_map/ppermute | solution.py:190
  156.6 4.6 %collective-permute-done.37.refs_0_ = bf16[128,1024]{1,0:T(8,128)(2,1)S(1)} collective-permute-done((bf16[128,1024]{1,0:T(8,128)(2,1)S(1)}, bf16[128,1024]{1,0:T(8,128)(2,1)S(1)}, u32[]{:S(2)}, u32[]{:S(2)}) %collective-permute-start.37) | collective-permute-done | bytes 262176 | tf_op jit(solution)/shard_map/ppermute | solution.py:190
  (128 shorter events, 54.9 us)
Async XLA Ops:
  0.0 17.7 %collective-permute-start.3 = (bf16[128,1024]{1,0:T(8,128)(2,1)}, bf16[128,1024]{1,0:T(8,128)(2,1)S(1)}, u32[]{:S(2)}, u32[]{:S(2)}) collective-permute-start(bf16[128,1024]{1,0:T(8,128)(2,1)} %bitcast.44), channel_id=1, source_target_pairs={{0,28},{1,29},{2,30},{3,31},{4,24},{5,25},{6,26},{7,27},{8,20},{9,... | collective-permute-start | bytes 786440 | tf_op jit(solution)/shard_map/ppermute | solution.py:190
  29.7 13.1 %collective-permute-start.7 = (bf16[128,1024]{1,0:T(8,128)(2,1)}, bf16[128,1024]{1,0:T(8,128)(2,1)}, u32[]{:S(2)}, u32[]{:S(2)}) collective-permute-start(bf16[128,1024]{1,0:T(8,128)(2,1)} %get-tuple-element.60), channel_id=1, source_target_pairs={{0,1},{1,0},{2,3},{3,2},{4,5},{5,4},{6,7},{7,6},{8,9},{9,8},{10,11... | collective-permute-start | bytes 786440 | tf_op jit(solution)/shard_map/ppermute | solution.py:190
  29.7 16.4 %collective-permute-start = (f32[1,128]{1,0:T(1,128)S(1)}, f32[1,128]{1,0:T(1,128)S(1)}, u32[]{:S(2)}, u32[]{:S(2)}) collective-permute-start(f32[1,128]{1,0:T(1,128)S(1)} %get-tuple-element.57), channel_id=1, source_target_pairs={{0,1},{1,0},{2,3},{3,2},{4,5},{5,4},{6,7},{7,6},{8,9},{9,8},{10,11... | collective-permute-start | bytes 1544 | tf_op jit(solution)/shard_map/ppermute | solution.py:190
  31.7 14.3 %collective-permute-start.1 = (f32[1,128]{1,0:T(1,128)S(1)}, f32[1,128]{1,0:T(1,128)S(1)}, u32[]{:S(2)}, u32[]{:S(2)}) collective-permute-start(f32[1,128]{1,0:T(1,128)S(1)} %get-tuple-element.57), channel_id=1, source_target_pairs={{0,2},{1,3},{2,0},{3,1},{4,6},{5,7},{6,4},{7,5},{8,10},{9,11},{10,... | collective-permute-start | bytes 1544 | tf_op jit(solution)/shard_map/ppermute | solution.py:190
  31.7 14.3 %collective-permute-start.2 = (f32[1,128]{1,0:T(1,128)S(1)}, f32[1,128]{1,0:T(1,128)S(1)}, u32[]{:S(2)}, u32[]{:S(2)}) collective-permute-start(f32[1,128]{1,0:T(1,128)S(1)} %get-tuple-element.57), channel_id=1, source_target_pairs={{0,3},{1,2},{2,1},{3,0},{4,7},{5,6},{6,5},{7,4},{8,11},{9,10},{10,... | collective-permute-start | bytes 1544 | tf_op jit(solution)/shard_map/ppermute | solution.py:190
  44.0 14.2 %collective-permute-start.15 = (bf16[128,1024]{1,0:T(8,128)(2,1)}, bf16[128,1024]{1,0:T(8,128)(2,1)S(1)}, u32[]{:S(2)}, u32[]{:S(2)}) collective-permute-start(bf16[128,1024]{1,0:T(8,128)(2,1)} %copy-done.15), channel_id=1, source_target_pairs={{0,1},{1,0},{2,3},{3,2},{4,5},{5,4},{6,7},{7,6},{8,9},{9,8},{10,11... | collective-permute-start | bytes 786440 | tf_op jit(solution)/shard_map/ppermute | solution.py:190
  45.1 14.1 %collective-permute-start.16 = (bf16[128,1024]{1,0:T(8,128)(2,1)S(1)}, bf16[128,1024]{1,0:T(8,128)(2,1)S(1)}, u32[]{:S(2)}, u32[]{:S(2)}) collective-permute-start(bf16[128,1024]{1,0:T(8,128)(2,1)S(1)} %add_convert_fusion.5.refs_3_), channel_id=1, source_target_pairs={{0,2},{1,3},{2,0},{3,1},{4,6},{5,7},{6,4},{7,5},{8,10},{9,11},{10,... | collective-permute-start | bytes 786440 | tf_op jit(solution)/shard_map/ppermute | solution.py:190
  65.1 14.9 %collective-permute-start.9 = (bf16[128,1024]{1,0:T(8,128)(2,1)S(1)}, bf16[128,1024]{1,0:T(8,128)(2,1)S(1)}, u32[]{:S(2)}, u32[]{:S(2)}) collective-permute-start(bf16[128,1024]{1,0:T(8,128)(2,1)S(1)} %get-tuple-element.65), channel_id=1, source_target_pairs={{0,1},{1,0},{2,3},{3,2},{4,5},{5,4},{6,7},{7,6},{8,9},{9,8},{10,11... | collective-permute-start | bytes 786440 | tf_op jit(solution)/shard_map/ppermute | solution.py:190
  65.2 14.8 %collective-permute-start.10 = (bf16[128,1024]{1,0:T(8,128)(2,1)S(1)}, bf16[128,1024]{1,0:T(8,128)(2,1)S(1)}, u32[]{:S(2)}, u32[]{:S(2)}) collective-permute-start(bf16[128,1024]{1,0:T(8,128)(2,1)S(1)} %add_convert_fusion.4.refs_3_), channel_id=1, source_target_pairs={{0,2},{1,3},{2,0},{3,1},{4,6},{5,7},{6,4},{7,5},{8,10},{9,11},{10,... | collective-permute-start | bytes 786440 | tf_op jit(solution)/shard_map/ppermute | solution.py:190
  72.7 14.0 %collective-permute-start.21 = (bf16[128,1024]{1,0:T(8,128)(2,1)S(1)}, bf16[128,1024]{1,0:T(8,128)(2,1)S(1)}, u32[]{:S(2)}, u32[]{:S(2)}) collective-permute-start(bf16[128,1024]{1,0:T(8,128)(2,1)S(1)} %get-tuple-element.77), channel_id=1, source_target_pairs={{0,1},{1,0},{2,3},{3,2},{4,5},{5,4},{6,7},{7,6},{8,9},{9,8},{10,11... | collective-permute-start | bytes 786440 | tf_op jit(solution)/shard_map/ppermute | solution.py:190
  86.7 14.9 %collective-permute-start.29 = (bf16[128,1024]{1,0:T(8,128)(2,1)S(1)}, bf16[128,1024]{1,0:T(8,128)(2,1)S(1)}, u32[]{:S(2)}, u32[]{:S(2)}) collective-permute-start(bf16[128,1024]{1,0:T(8,128)(2,1)S(1)} %get-tuple-element.89), channel_id=1, source_target_pairs={{0,1},{1,0},{2,3},{3,2},{4,5},{5,4},{6,7},{7,6},{8,9},{9,8},{10,11... | collective-permute-start | bytes 786440 | tf_op jit(solution)/shard_map/ppermute | solution.py:190
  86.9 14.7 %collective-permute-start.30 = (bf16[128,1024]{1,0:T(8,128)(2,1)S(1)}, bf16[128,1024]{1,0:T(8,128)(2,1)S(1)}, u32[]{:S(2)}, u32[]{:S(2)}) collective-permute-start(bf16[128,1024]{1,0:T(8,128)(2,1)S(1)} %add_convert_fusion.3.refs_3_), channel_id=1, source_target_pairs={{0,2},{1,3},{2,0},{3,1},{4,6},{5,7},{6,4},{7,5},{8,10},{9,11},{10,... | collective-permute-start | bytes 786440 | tf_op jit(solution)/shard_map/ppermute | solution.py:190
  93.9 13.5 %collective-permute-start.22 = (bf16[128,1024]{1,0:T(8,128)(2,1)S(1)}, bf16[128,1024]{1,0:T(8,128)(2,1)S(1)}, u32[]{:S(2)}, u32[]{:S(2)}) collective-permute-start(bf16[128,1024]{1,0:T(8,128)(2,1)S(1)} %get-tuple-element.81), channel_id=1, source_target_pairs={{0,1},{1,0},{2,3},{3,2},{4,5},{5,4},{6,7},{7,6},{8,9},{9,8},{10,11... | collective-permute-start | bytes 786440 | tf_op jit(solution)/shard_map/ppermute | solution.py:190
  107.5 14.9 %collective-permute-start.23 = (bf16[128,1024]{1,0:T(8,128)(2,1)S(1)}, bf16[128,1024]{1,0:T(8,128)(2,1)S(1)}, u32[]{:S(2)}, u32[]{:S(2)}) collective-permute-start(bf16[128,1024]{1,0:T(8,128)(2,1)S(1)} %get-tuple-element.82), channel_id=1, source_target_pairs={{0,1},{1,0},{2,3},{3,2},{4,5},{5,4},{6,7},{7,6},{8,9},{9,8},{10,11... | collective-permute-start | bytes 786440 | tf_op jit(solution)/shard_map/ppermute | solution.py:190
  107.5 14.8 %collective-permute-start.24 = (bf16[128,1024]{1,0:T(8,128)(2,1)S(1)}, bf16[128,1024]{1,0:T(8,128)(2,1)S(1)}, u32[]{:S(2)}, u32[]{:S(2)}) collective-permute-start(bf16[128,1024]{1,0:T(8,128)(2,1)S(1)} %add_convert_fusion.2.refs_3_), channel_id=1, source_target_pairs={{0,2},{1,3},{2,0},{3,1},{4,6},{5,7},{6,4},{7,5},{8,10},{9,11},{10,... | collective-permute-start | bytes 786440 | tf_op jit(solution)/shard_map/ppermute | solution.py:190
  115.4 13.6 %collective-permute-start.35 = (bf16[128,1024]{1,0:T(8,128)(2,1)S(1)}, bf16[128,1024]{1,0:T(8,128)(2,1)S(1)}, u32[]{:S(2)}, u32[]{:S(2)}) collective-permute-start(bf16[128,1024]{1,0:T(8,128)(2,1)S(1)} %get-tuple-element.94), channel_id=1, source_target_pairs={{0,1},{1,0},{2,3},{3,2},{4,5},{5,4},{6,7},{7,6},{8,9},{9,8},{10,11... | collective-permute-start | bytes 786440 | tf_op jit(solution)/shard_map/ppermute | solution.py:190
  129.1 14.9 %collective-permute-start.41 = (bf16[128,1024]{1,0:T(8,128)(2,1)S(1)}, bf16[128,1024]{1,0:T(8,128)(2,1)S(1)}, u32[]{:S(2)}, u32[]{:S(2)}) collective-permute-start(bf16[128,1024]{1,0:T(8,128)(2,1)S(1)} %get-tuple-element.106), channel_id=1, source_target_pairs={{0,1},{1,0},{2,3},{3,2},{4,5},{5,4},{6,7},{7,6},{8,9},{9,8},{10,11... | collective-permute-start | bytes 786440 | tf_op jit(solution)/shard_map/ppermute | solution.py:190
  129.2 14.8 %collective-permute-start.42 = (bf16[128,1024]{1,0:T(8,128)(2,1)S(1)}, bf16[128,1024]{1,0:T(8,128)(2,1)S(1)}, u32[]{:S(2)}, u32[]{:S(2)}) collective-permute-start(bf16[128,1024]{1,0:T(8,128)(2,1)S(1)} %add_convert_fusion.1.refs_3_), channel_id=1, source_target_pairs={{0,2},{1,3},{2,0},{3,1},{4,6},{5,7},{6,4},{7,5},{8,10},{9,11},{10,... | collective-permute-start | bytes 786440 | tf_op jit(solution)/shard_map/ppermute | solution.py:190
  136.4 12.1 %collective-permute-start.36 = (bf16[128,1024]{1,0:T(8,128)(2,1)S(1)}, bf16[128,1024]{1,0:T(8,128)(2,1)S(1)}, u32[]{:S(2)}, u32[]{:S(2)}) collective-permute-start(bf16[128,1024]{1,0:T(8,128)(2,1)S(1)} %get-tuple-element.98), channel_id=1, source_target_pairs={{0,1},{1,0},{2,3},{3,2},{4,5},{5,4},{6,7},{7,6},{8,9},{9,8},{10,11... | collective-permute-start | bytes 786440 | tf_op jit(solution)/shard_map/ppermute | solution.py:190
  136.5 15.0 %collective-permute-start.39 = (bf16[128,1024]{1,0:T(8,128)(2,1)S(1)}, bf16[128,1024]{1,0:T(8,128)(2,1)S(1)}, u32[]{:S(2)}, u32[]{:S(2)}) collective-permute-start(bf16[128,1024]{1,0:T(8,128)(2,1)S(1)} %get-tuple-element.102), channel_id=1, source_target_pairs={{0,28},{1,29},{2,30},{3,31},{4,24},{5,25},{6,26},{7,27},{8,20},{9,... | collective-permute-start | bytes 786440 | tf_op jit(solution)/shard_map/ppermute | solution.py:190
  137.4 14.0 %collective-permute-start.40 = (bf16[128,1024]{1,0:T(8,128)(2,1)S(1)}, bf16[128,1024]{1,0:T(8,128)(2,1)S(1)}, u32[]{:S(2)}, u32[]{:S(2)}) collective-permute-start(bf16[128,1024]{1,0:T(8,128)(2,1)S(1)} %get-tuple-element.103), channel_id=1, source_target_pairs={{0,28},{1,29},{2,30},{3,31},{4,24},{5,25},{6,26},{7,27},{8,20},{9,... | collective-permute-start | bytes 786440 | tf_op jit(solution)/shard_map/ppermute | solution.py:190
  144.9 11.6 %collective-permute-start.43 = (bf16[128,1024]{1,0:T(8,128)(2,1)S(1)}, bf16[128,1024]{1,0:T(8,128)(2,1)S(1)}, u32[]{:S(2)}, u32[]{:S(2)}) collective-permute-start(bf16[128,1024]{1,0:T(8,128)(2,1)S(1)} %get-tuple-element.108), channel_id=1, source_target_pairs={{0,28},{1,29},{2,30},{3,31},{4,24},{5,25},{6,26},{7,27},{8,20},{9,... | collective-permute-start | bytes 786440 | tf_op jit(solution)/shard_map/ppermute | solution.py:190
  148.6 12.6 %collective-permute-start.37 = (bf16[128,1024]{1,0:T(8,128)(2,1)S(1)}, bf16[128,1024]{1,0:T(8,128)(2,1)S(1)}, u32[]{:S(2)}, u32[]{:S(2)}) collective-permute-start(bf16[128,1024]{1,0:T(8,128)(2,1)S(1)} %get-tuple-element.99), channel_id=1, source_target_pairs={{0,1},{1,0},{2,3},{3,2},{4,5},{5,4},{6,7},{7,6},{8,9},{9,8},{10,11... | collective-permute-start | bytes 786440 | tf_op jit(solution)/shard_map/ppermute | solution.py:190
  149.0 13.9 %collective-permute-start.38 = (bf16[128,1024]{1,0:T(8,128)(2,1)S(1)}, bf16[128,1024]{1,0:T(8,128)(2,1)S(1)}, u32[]{:S(2)}, u32[]{:S(2)}) collective-permute-start(bf16[128,1024]{1,0:T(8,128)(2,1)S(1)} %add_convert_fusion), channel_id=1, source_target_pairs={{0,2},{1,3},{2,0},{3,1},{4,6},{5,7},{6,4},{7,5},{8,10},{9,11},{10,... | collective-permute-start | bytes 786440 | tf_op jit(solution)/shard_map/ppermute | solution.py:190
  (37 other events, 303.1 us)

commit v3 on v1

v3 whole, which is shorter than its diff:
```python
import functools

import jax
import jax.numpy as jnp
from jax import lax
from jax.experimental import pallas as pl
from jax.experimental.pallas import tpu as pltpu
from jax.sharding import PartitionSpec as P

WIDTH = 4096
SHORT_TAPS = 7
LONG_TAPS = 128
GROUP_SIZE = 16
TICK_COUNT = 3
EPSILON = 1e-06

LANES = 128
PER_BLOCK = LANES // GROUP_SIZE
IN_VMEM = pl.BlockSpec(memory_space=pltpu.VMEM)
IN_PLACE = pl.BlockSpec(memory_space=pl.ANY)


def prepare_kernel(
    ticks, order_hbm, filters_hbm, tokens_hbm, table_hbm, weight_hbm, *refs
):
    blocks_ref, weight_ref, refs = refs[0], refs[1], refs[2:]
    fresh_refs, refs = refs[: 2 * ticks], refs[2 * ticks :]
    order_ref, filters_ref, tokens_ref, table_ref, sems = refs
    copies = [
        pltpu.make_async_copy(source, target, sems.at[spot])
        for spot, (source, target) in enumerate(
            [
                (filters_hbm, filters_ref),
                (order_hbm, order_ref),
                (tokens_hbm, tokens_ref),
                (table_hbm, table_ref),
                (weight_hbm, weight_ref),
            ]
        )
    ]
    for copy in copies:
        copy.start()
    copies[0].wait()
    groups, seq = filters_ref.shape
    taps = jnp.where(lax.axis_index("pipe") % 2 == 0, SHORT_TAPS, LONG_TAPS)
    lane = lax.broadcasted_iota(jnp.int32, (groups, seq), 1)
    kept = jnp.where(lane < taps, filters_ref[...], 0.0).astype(jnp.bfloat16)
    row = lax.broadcasted_iota(jnp.int32, (seq, seq), 0)
    col = lax.broadcasted_iota(jnp.int32, (seq, seq), 1)
    flip = ((row + col) % seq == 0).astype(jnp.bfloat16)
    backward = jnp.dot(kept, flip, preferred_element_type=jnp.float32)
    for group in range(groups):
        wide = jnp.broadcast_to(backward[group : group + 1, :], (seq, seq))
        turned = pltpu.roll(wide, 0, 1, stride=1, stride_axis=0)
        start = group % PER_BLOCK * seq
        blocks_ref[group // PER_BLOCK, :, start : start + seq] = jnp.where(
            row >= col, turned, 0.0
        ).astype(jnp.bfloat16)
    for copy in copies[1:4]:
        copy.wait()
    word = lax.broadcasted_iota(jnp.int32, (table_ref.shape[0], seq), 0)
    for entry, fresh_ref in enumerate(fresh_refs):
        way, tick = entry // ticks, entry % ticks
        chosen = tokens_ref[way, pl.ds(order_ref[way, tick], 1), :]
        onehot = (word == chosen).astype(jnp.bfloat16)
        fresh_ref[...] = lax.dot_general(
            onehot, table_ref[...], (((0,), (0,)), ((), ())), preferred_element_type=jnp.float32
        ).astype(fresh_ref.dtype)
    copies[4].wait()


def in_hbm(array):
    return pltpu.with_memory_space_constraint(array, pltpu.HBM)


def prepare(filters, weight, tokens, order, table):
    groups, seq = filters.shape
    ticks = TICK_COUNT - 1
    blocks, held, *fresh = pl.pallas_call(
        functools.partial(prepare_kernel, ticks),
        out_shape=[
            jax.ShapeDtypeStruct((groups // PER_BLOCK, seq, PER_BLOCK * seq), jnp.bfloat16),
            jax.ShapeDtypeStruct(weight.shape, weight.dtype),
        ]
        + [jax.ShapeDtypeStruct((seq, table.shape[1]), table.dtype)] * (2 * ticks),
        in_specs=[IN_PLACE] * 5,
        out_specs=[IN_VMEM] * (2 + 2 * ticks),
        scratch_shapes=[
            pltpu.SMEM(order.shape, order.dtype),
            pltpu.VMEM(filters.shape, filters.dtype),
            pltpu.VMEM(tokens.shape, tokens.dtype),
            pltpu.VMEM(table.shape, table.dtype),
            pltpu.SemaphoreType.DMA((5,)),
        ],
        compiler_params=pltpu.CompilerParams(vmem_limit_bytes=16 * 2**20),
        name="prepare",
    )(in_hbm(order), in_hbm(filters), in_hbm(tokens), in_hbm(table), in_hbm(weight))
    return blocks, held, [fresh[:ticks], fresh[ticks:]]


def row_squares(values):
    seq, channels = values.shape
    squares = values * values
    total = squares[:, :LANES]
    for start in range(LANES, channels, LANES):
        total = total + squares[:, start : start + LANES]
    return jnp.sum(total.T, axis=0, keepdims=True)


def squares_kernel(count, *refs):
    sources, squares_ref, held_ref, sems = refs[:count], refs[-3], refs[-2], refs[-1]
    copies = [
        pltpu.make_async_copy(source, held_ref.at[spot], sems.at[spot])
        for spot, source in enumerate(sources)
    ]
    for copy in copies:
        copy.start()
    for spot, copy in enumerate(copies):
        copy.wait()
        squares_ref[spot : spot + 1, :] = row_squares(held_ref[spot].astype(jnp.float32))


def squares_of(*arrays):
    count = len(arrays)
    return pl.pallas_call(
        functools.partial(squares_kernel, count),
        out_shape=jax.ShapeDtypeStruct((count, arrays[0].shape[0]), jnp.float32),
        in_specs=[IN_PLACE] * count,
        out_specs=IN_VMEM,
        scratch_shapes=[
            pltpu.VMEM((count, *arrays[0].shape), arrays[0].dtype),
            pltpu.SemaphoreType.DMA((count,)),
        ],
        compiler_params=pltpu.CompilerParams(vmem_limit_bytes=6 * 2**20),
        name="squares",
    )(*[in_hbm(array) for array in arrays])


def layer_kernel(count, line, x_ref, gains_ref, blocks_ref, weight_ref, *refs):
    squares_refs, out_refs, gated_buf = refs[: count - 1], refs[-count - 1 : -1], refs[-1]
    place = lax.axis_index("tensor")
    seq, channels = x_ref.shape
    values = x_ref[...].astype(jnp.float32)
    others = squares_refs[0][line : line + 1, :]
    for ref in squares_refs[1:]:
        others = others + ref[line : line + 1, :]
    squares = jnp.broadcast_to(others, (seq, seq)).T + jnp.sum(
        values * values, axis=-1, keepdims=True
    )
    scale = lax.rsqrt(squares / WIDTH + EPSILON)
    lane_group = lax.broadcasted_iota(jnp.int32, (seq, LANES), 1) // GROUP_SIZE
    for block in range(channels // LANES):
        lanes = slice(block * LANES, (block + 1) * LANES)
        normed = values[:, lanes] * scale * gains_ref[:, lanes]
        narrow = normed.astype(jnp.bfloat16)
        spread = jnp.concatenate(
            [
                jnp.where(lane_group == part, narrow, jnp.zeros_like(narrow))
                for part in range(PER_BLOCK)
            ],
            axis=0,
        )
        mixed = jnp.dot(blocks_ref[block], spread, preferred_element_type=jnp.float32)
        gated_buf[:, lanes] = (normed * mixed).astype(jnp.bfloat16)
    for apart in reversed(range(count)):
        start = pl.multiple_of((place ^ apart) * channels, channels)
        out_refs[apart][...] = jnp.dot(
            gated_buf[...],
            weight_ref[:, pl.ds(start, channels)],
            preferred_element_type=jnp.float32,
        ).astype(out_refs[apart].dtype)


def layer_partials(x, squares, line, gains, blocks, weight, count, after):
    seq, channels = x.shape
    kinds = [jnp.bfloat16 if apart % 2 else jnp.float32 for apart in range(count)]
    return pl.pallas_call(
        functools.partial(layer_kernel, count, line),
        out_shape=[jax.ShapeDtypeStruct((seq, channels), kind) for kind in kinds],
        in_specs=[IN_VMEM] * (3 + count) + [IN_PLACE] * len(after),
        out_specs=[IN_VMEM] * count,
        scratch_shapes=[pltpu.VMEM((seq, channels), jnp.bfloat16)],
        compiler_params=pltpu.CompilerParams(vmem_limit_bytes=12 * 2**20),
        cost_estimate=pl.CostEstimate(
            flops=1 * 2 * seq * channels * channels * count,
            transcendentals=0,
            bytes_accessed=1 * 2 * channels * channels * count,
        ),
        name="layer",
    )(x, gains, blocks, weight, *squares, *after)


def merge_kernel(count, x_ref, fresh_ref, own_ref, *refs):
    arrived, (y_ref, sent_ref, squares_ref) = refs[:count], refs[-3:]
    total = own_ref[...]
    for ref in arrived:
        total = total + ref[...].astype(jnp.float32)
    y = (x_ref[...].astype(jnp.float32) + total).astype(jnp.bfloat16)
    y_ref[...] = y
    last = lax.axis_index("pipe") == lax.axis_size("pipe") - 1
    sent = jnp.where(last, fresh_ref[...].astype(jnp.float32), y.astype(jnp.float32))
    sent_ref[...] = sent.astype(jnp.bfloat16)
    squares_ref[...] = row_squares(sent)


def merge(x, fresh, own, arrived, after):
    seq, channels = x.shape
    return pl.pallas_call(
        functools.partial(merge_kernel, len(arrived)),
        out_shape=[
            jax.ShapeDtypeStruct((seq, channels), jnp.bfloat16),
            jax.ShapeDtypeStruct((seq, channels), jnp.bfloat16),
            jax.ShapeDtypeStruct((1, seq), jnp.float32),
        ],
        in_specs=[IN_VMEM] * (3 + len(arrived)) + [IN_PLACE] * len(after),
        out_specs=[IN_VMEM] * 3,
        compiler_params=pltpu.CompilerParams(vmem_limit_bytes=6 * 2**20),
        name="merge",
    )(x, fresh, own, *arrived, *after)


def send(values, target):
    pipe, tensor = lax.axis_size("pipe"), lax.axis_size("tensor")
    pairs = []
    for k in range(pipe):
        for z in range(tensor):
            to_k, to_z = target(k, z)
            pairs.append((k * tensor + z, to_k * tensor + to_z))
    return lax.ppermute(values, ("pipe", "tensor"), pairs)


def first_halving(partials, after):
    partials = list(partials)
    for apart in reversed(range(3, len(partials), 2)):
        incoming = send(partials[apart], lambda k, z: (k, z ^ 1))
        incoming, after = lax.optimization_barrier((incoming, after))
        partials[apart ^ 1] = partials[apart ^ 1] + incoming.astype(jnp.float32)
    kept = partials[:2] + [
        partial.astype(jnp.bfloat16) if apart == 2 else partial
        for apart, partial in enumerate(partials)
        if apart >= 2 and apart % 2 == 0
    ]
    return kept, after


def other_halvings(partials):
    pair, rest = partials[:2], partials[2:]
    arrived = [send(pair[1], lambda k, z: (k, z ^ 1))]
    left = {2 * (spot + 1): partial for spot, partial in enumerate(rest)}
    bit = 2
    while left:
        for apart in sorted(left, reverse=True):
            if apart & bit:
                incoming = send(
                    left.pop(apart).astype(jnp.bfloat16), lambda k, z: (k, z ^ bit)
                )
                if apart == bit:
                    arrived.append(incoming)
                else:
                    left[apart ^ bit] = left[apart ^ bit].astype(jnp.float32) + incoming.astype(
                        jnp.float32
                    )
        bit *= 2
    return arrived


def local(
    down_state, up_state, layer_proj, conv_filters, norm_gains, embedding, dna_tokens, entry_order
):
    pipe, tensor = lax.axis_size("pipe"), lax.axis_size("tensor")
    gains = norm_gains

    def mirrored(k):
        return pipe - 1 - k

    def following(k):
        return (k + 1) % pipe

    def spread(sums, target):
        return [
            send(sums, lambda k, z, apart=apart: (target(k), z ^ apart))
            for apart in range(1, tensor)
        ]

    down, up = 0, 1
    entering = [down_state[0], up_state[0]]
    sums = squares_of(*entering)
    squares = [spread(sums, lambda k: k), spread(sums, mirrored)]
    entering[up] = send(entering[up], lambda k, z: (mirrored(k), z))
    blocks, weight, fresh = prepare(
        conv_filters[0], layer_proj[0], dna_tokens, entry_order, embedding
    )

    def go_on(partials):
        own, *rest = partials
        rest = lax.optimization_barrier(rest)
        return own, other_halvings([own, *rest]), rest[1:2]

    def run_layer(way, tick, after, held):
        *partials, neighbour = layer_partials(
            entering[way],
            squares[way],
            way if tick == 0 else 0,
            gains,
            blocks,
            weight,
            tensor,
            after,
        )
        if way == up and tick > 0:
            neighbour, y = lax.optimization_barrier((neighbour, leaving[up].pop()))
            leaving[up].append(send(y, lambda k, z: (mirrored(k), z)))
        return first_halving([*partials, neighbour], held)

    def finish(way, tick, own, arrived):
        newcomer = fresh[way][min(tick, TICK_COUNT - 2)]
        y, sent, sums = merge(entering[way], newcomer, own, arrived, leaving[way][-1:])
        leaving[way].append(y)
        if tick < TICK_COUNT - 1:
            entering[way] = send(sent, lambda k, z: (following(k), z))
            squares[way] = spread(sums, following)

    leaving = [[], []]
    early = []
    for tick in range(TICK_COUNT):
        for way in (up, down):
            ending = tick == TICK_COUNT - 1 and way == down
            held = [leaving[up].pop()] if ending else []
            partials, held = run_layer(way, tick, early, held)
            leaving[up].extend(held)
            own, arrived, early = go_on(partials)
            finish(way, tick, own, arrived)
    leaving[up].append(send(leaving[up].pop(), lambda k, z: (mirrored(k), z)))
    return jnp.stack([jnp.stack(way) for way in leaving], axis=1)[:, :, None]


def solution(mesh):
    placed = (
        P("pipe", None, "tensor"),
        P("pipe", None, "tensor"),
        P("pipe", "tensor", None),
        P("pipe", "tensor", None),
        P("pipe", "tensor"),
        P(None, "tensor"),
        P(),
        P(),
    )
    return jax.shard_map(
        local,
        mesh=mesh,
        in_specs=placed,
        out_specs=P(None, None, "pipe", None, "tensor"),
        check_vma=False,
    )
```

time: 224 us -> 153 us (0.68)
  Pallas kernels: 48.5 us -> 20.5 us
  local copies, waits for them, and re-layouts: 25.1 us -> 1.28 us
  waiting for transfers between devices: 81.2 us -> 66.1 us
  starting transfers between devices: 50.1 us -> 64.3 us
  between operations: 7.95 us -> 0.32 us
  other arithmetic: 6.6 us -> 0.69 us
  matrix products: 4.25 us -> 0 us
    unnamed x72 -> x4, local copies, waits for them, and re-layouts: 23.7 us -> 0.01 us
    pallas_call x9 -> x8, Pallas kernels: 34.4 us -> 16.7 us  [the longest x6 11.7 us: layer_partials(): pl.pallas_call(functools.partial(layer_kernel, count, line), out_shape=[j...]
    ppermute x44, waiting for transfers between devices: 81.2 us -> 66.1 us  [send(): return lax.ppermute(values, ('pipe', 'tensor'), pairs)]
    ppermute x44, starting transfers between devices: 50.1 us -> 64.3 us  [send(): return lax.ppermute(values, ('pipe', 'tensor'), pairs)]
    pallas_call x6, Pallas kernels: 14.2 us -> 3.75 us  [merge(): pl.pallas_call(functools.partial(merge_kernel, len(arrived)), out_shape=[...]
    dot_general x4 -> x0, matrix products: 4.25 us -> none  [embed_tokens(): jnp.dot(onehot, table, preferred_element_type=jnp.float32)]
    convert_element_type x6, other arithmetic: 4.1 us -> 0.36 us  [first_halving(): partial.astype(jnp.bfloat16)]
  transfers between devices with their start and end apart: 44 -> 44, of which waited for: 15 -> 19; matrix products, arithmetic and copies ran while one was open for 4% -> 0% of each run, Pallas kernels for 20% -> 12%
where the time goes in v3:
time: 153 us
  waiting for transfers between devices  66.1 us (43%)
  starting transfers between devices  64.3 us (42%)
  Pallas kernels  20.5 us (13%)
    ppermute x44, waiting for transfers between devices, send(): return lax.ppermute(values, ('pipe', 'tensor'), pairs)  66.1 us
    ppermute x44, starting transfers between devices, send(): return lax.ppermute(values, ('pipe', 'tensor'), pairs)  64.3 us
    pallas_call x6, Pallas kernels, layer_partials(): pl.pallas_call(functools.partial(layer_kernel, count, line), out_shape=[j...  11.7 us
    pallas_call x1, Pallas kernels, prepare(): pl.pallas_call(functools.partial(prepare_kernel, ticks), out_shape=[jax.S...  3.8 us
    pallas_call x6, Pallas kernels, merge(): pl.pallas_call(functools.partial(merge_kernel, len(arrived)), out_shape=[...  3.75 us
  transfers between devices with their start and end apart: 44, of which 19 were waited for; matrix products, arithmetic and copies ran while one was open for 0% of the time, Pallas kernels for 12%

profile of v3, /device:TPU:0, one launch (start us, length us, event | category | flops | bytes accessed | tf_op | source)
XLA Modules:
  0.0 153.2 jit_solution(7416276246897202409)
XLA Ops:
  0.0 3.3 %collective-permute-start.3 = (bf16[128,1024]{1,0:T(8,128)(2,1)}, bf16[128,1024]{1,0:T(8,128)(2,1)S(1)}, u32[]{:S(2)}, u32[]{:S(2)}) collective-permute-start(bf16[128,1024]{1,0:T(8,128)(2,1)} %bitcast.25), channel_id=1, source_target_pairs={{0,28},{1,29},{2,30},{3,31},{4,24},{5,25},{6,26},{7,27},{8,20},{9,... | collective-permute-start | bytes 786440 | tf_op jit(solution)/shard_map/ppermute | solution.py:229
  4.6 3.9 %collective-permute-start.6 = (f32[2,128]{1,0:T(2,128)S(1)}, f32[2,128]{1,0:T(2,128)S(1)}, u32[]{:S(2)}, u32[]{:S(2)}) collective-permute-start(f32[2,128]{1,0:T(2,128)S(1)} %squares.1), channel_id=1, source_target_pairs={{0,31},{1,30},{2,29},{3,28},{4,27},{5,26},{6,25},{7,24},{8,23},{9,... | collective-permute-start | bytes 3080 | tf_op jit(solution)/shard_map/ppermute | solution.py:229
  10.4 3.8 %prepare.1 = (bf16[8,128,1024]{2,1,0:T(8,128)(2,1)S(1)}, bf16[1024,4096]{1,0:T(8,128)(2,1)S(1)}, bf16[128,1024]{1,0:T(8,128)(2,1)S(1)}, bf16[128,1024]{1,0:T(8,1...) custom-call(s32[2,8]{1,0:T(2,128)} %order_hbm.1, f32[64,128]{1,0:T(8,128)} %bitcast.28, ...), custom_call_target="tpu_custom_call" | custom-call | tf_op jit(solution)/shard_map/prepare/pallas_call | solution.py:79
  17.7 3.3 %collective-permute-start.2 = (f32[2,128]{1,0:T(2,128)S(1)}, f32[2,128]{1,0:T(2,128)S(1)}, u32[]{:S(2)}, u32[]{:S(2)}) collective-permute-start(f32[2,128]{1,0:T(2,128)S(1)} %squares.1), channel_id=1, source_target_pairs={{0,3},{1,2},{2,1},{3,0},{4,7},{5,6},{6,5},{7,4},{8,11},{9,10},{10,... | collective-permute-start | bytes 3080 | tf_op jit(solution)/shard_map/ppermute | solution.py:229
  22.1 3.1 %collective-permute-done.7 = bf16[128,1024]{1,0:T(8,128)(2,1)S(1)} collective-permute-done((bf16[128,1024]{1,0:T(8,128)(2,1)S(1)}, bf16[128,1024]{1,0:T(8,128)(2,1)S(1)}, u32[]{:S(2)}, u32[]{:S(2)}) %collective-permute-start.7) | collective-permute-done | bytes 262176 | tf_op jit(solution)/shard_map/ppermute | solution.py:229
  26.7 2.4 %collective-permute-start.16 = (bf16[128,1024]{1,0:T(8,128)(2,1)S(1)}, bf16[128,1024]{1,0:T(8,128)(2,1)S(1)}, u32[]{:S(2)}, u32[]{:S(2)}) collective-permute-start(bf16[128,1024]{1,0:T(8,128)(2,1)S(1)} %add_convert_fusion.5.refs_3_), channel_id=1, source_target_pairs={{0,2},{1,3},{2,0},{3,1},{4,6},{5,7},{6,4},{7,5},{8,10},{9,11},{10,... | collective-permute-start | bytes 786440 | tf_op jit(solution)/shard_map/ppermute | solution.py:229
  29.1 2.0 %layer.7 = (f32[128,1024]{1,0:T(8,128)S(1)}, bf16[128,1024]{1,0:T(8,128)(2,1)S(1)}, f32[128,1024]{1,0:T(8,128)S(1)}, bf16[128,1024]{1,0:T(8,128)(2,1)S(1)}) custom-call(bf16[128,1024]{1,0:T(8,128)(2,1)S(1)} %bitcast.17, f32[1,1024]{1,0:T(1,128)S(1)} %copy-done.1, bf16[8,128,1024]{2,1,0:T(8,128)(2,1)S(1)} %get-tuple-element.68.blocks_ref, ...), custom_call_target="tpu_custom_call" | custom-call | flops 1073741824 | bytes 8388608 | tf_op jit(solution)/shard_map/layer/pallas_call | solution.py:177
  32.6 7.5 %collective-permute-done.15.refs_0_ = bf16[128,1024]{1,0:T(8,128)(2,1)S(1)} collective-permute-done((bf16[128,1024]{1,0:T(8,128)(2,1)S(1)}, bf16[128,1024]{1,0:T(8,128)(2,1)S(1)}, u32[]{:S(2)}, u32[]{:S(2)}) %collective-permute-start.15) | collective-permute-done | bytes 262176 | tf_op jit(solution)/shard_map/ppermute | solution.py:229
  40.7 4.4 %collective-permute-start.20 = (f32[1,128]{1,0:T(1,128)S(1)}, f32[1,128]{1,0:T(1,128)S(1)}, u32[]{:S(2)}, u32[]{:S(2)}) collective-permute-start(f32[1,128]{1,0:T(1,128)S(1)} %get-tuple-element.88), channel_id=1, source_target_pairs={{0,7},{1,6},{2,5},{3,4},{4,11},{5,10},{6,9},{7,8},{8,15},{9,14},{1... | collective-permute-start | bytes 1544 | tf_op jit(solution)/shard_map/ppermute | solution.py:229
  48.4 2.3 %collective-permute-start.10 = (bf16[128,1024]{1,0:T(8,128)(2,1)S(1)}, bf16[128,1024]{1,0:T(8,128)(2,1)S(1)}, u32[]{:S(2)}, u32[]{:S(2)}) collective-permute-start(bf16[128,1024]{1,0:T(8,128)(2,1)S(1)} %add_convert_fusion.4.refs_3_), channel_id=1, source_target_pairs={{0,2},{1,3},{2,0},{3,1},{4,6},{5,7},{6,4},{7,5},{8,10},{9,11},{10,... | collective-permute-start | bytes 786440 | tf_op jit(solution)/shard_map/ppermute | solution.py:229
  54.1 6.8 %collective-permute-done.9.refs_0_ = bf16[128,1024]{1,0:T(8,128)(2,1)S(1)} collective-permute-done((bf16[128,1024]{1,0:T(8,128)(2,1)S(1)}, bf16[128,1024]{1,0:T(8,128)(2,1)S(1)}, u32[]{:S(2)}, u32[]{:S(2)}) %collective-permute-start.9) | collective-permute-done | bytes 262176 | tf_op jit(solution)/shard_map/ppermute | solution.py:229
  63.2 3.4 %collective-permute-start.14 = (f32[1,128]{1,0:T(1,128)S(1)}, f32[1,128]{1,0:T(1,128)S(1)}, u32[]{:S(2)}, u32[]{:S(2)}) collective-permute-start(f32[1,128]{1,0:T(1,128)S(1)} %get-tuple-element.83), channel_id=1, source_target_pairs={{0,7},{1,6},{2,5},{3,4},{4,11},{5,10},{6,9},{7,8},{8,15},{9,14},{1... | collective-permute-start | bytes 1544 | tf_op jit(solution)/shard_map/ppermute | solution.py:229
  66.6 2.7 %collective-permute-start.12 = (f32[1,128]{1,0:T(1,128)S(1)}, f32[1,128]{1,0:T(1,128)S(1)}, u32[]{:S(2)}, u32[]{:S(2)}) collective-permute-start(f32[1,128]{1,0:T(1,128)S(1)} %get-tuple-element.83), channel_id=1, source_target_pairs={{0,5},{1,4},{2,7},{3,6},{4,9},{5,8},{6,11},{7,10},{8,13},{9,12},{1... | collective-permute-start | bytes 1544 | tf_op jit(solution)/shard_map/ppermute | solution.py:229
  76.4 2.4 %collective-permute-done.31.refs_2_ = bf16[128,1024]{1,0:T(8,128)(2,1)S(1)} collective-permute-done((bf16[128,1024]{1,0:T(8,128)(2,1)S(1)}, bf16[128,1024]{1,0:T(8,128)(2,1)S(1)}, u32[]{:S(2)}, u32[]{:S(2)}) %collective-permute-start.31) | collective-permute-done | bytes 262176 | tf_op jit(solution)/shard_map/ppermute | solution.py:229
  78.7 6.0 %collective-permute-done.29.refs_0_ = bf16[128,1024]{1,0:T(8,128)(2,1)S(1)} collective-permute-done((bf16[128,1024]{1,0:T(8,128)(2,1)S(1)}, bf16[128,1024]{1,0:T(8,128)(2,1)S(1)}, u32[]{:S(2)}, u32[]{:S(2)}) %collective-permute-start.29) | collective-permute-done | bytes 262176 | tf_op jit(solution)/shard_map/ppermute | solution.py:229
  86.3 2.7 %collective-permute-start.35 = (f32[1,128]{1,0:T(1,128)S(1)}, f32[1,128]{1,0:T(1,128)S(1)}, u32[]{:S(2)}, u32[]{:S(2)}) collective-permute-start(f32[1,128]{1,0:T(1,128)S(1)} %get-tuple-element.109), channel_id=1, source_target_pairs={{0,7},{1,6},{2,5},{3,4},{4,11},{5,10},{6,9},{7,8},{8,15},{9,14},{1... | collective-permute-start | bytes 1544 | tf_op jit(solution)/shard_map/ppermute | solution.py:229
  89.0 3.4 %collective-permute-start.33 = (f32[1,128]{1,0:T(1,128)S(1)}, f32[1,128]{1,0:T(1,128)S(1)}, u32[]{:S(2)}, u32[]{:S(2)}) collective-permute-start(f32[1,128]{1,0:T(1,128)S(1)} %get-tuple-element.109), channel_id=1, source_target_pairs={{0,5},{1,4},{2,7},{3,6},{4,9},{5,8},{6,11},{7,10},{8,13},{9,12},{1... | collective-permute-start | bytes 1544 | tf_op jit(solution)/shard_map/ppermute | solution.py:229
  92.9 3.0 %collective-permute-start.24 = (bf16[128,1024]{1,0:T(8,128)(2,1)S(1)}, bf16[128,1024]{1,0:T(8,128)(2,1)S(1)}, u32[]{:S(2)}, u32[]{:S(2)}) collective-permute-start(bf16[128,1024]{1,0:T(8,128)(2,1)S(1)} %add_convert_fusion.2.refs_3_), channel_id=1, source_target_pairs={{0,2},{1,3},{2,0},{3,1},{4,6},{5,7},{6,4},{7,5},{8,10},{9,11},{10,... | collective-permute-start | bytes 786440 | tf_op jit(solution)/shard_map/ppermute | solution.py:229
  98.1 9.1 %collective-permute-done.23.refs_0_ = bf16[128,1024]{1,0:T(8,128)(2,1)S(1)} collective-permute-done((bf16[128,1024]{1,0:T(8,128)(2,1)S(1)}, bf16[128,1024]{1,0:T(8,128)(2,1)S(1)}, u32[]{:S(2)}, u32[]{:S(2)}) %collective-permute-start.23) | collective-permute-done | bytes 262176 | tf_op jit(solution)/shard_map/ppermute | solution.py:229
  108.2 3.8 %collective-permute-start.28 = (f32[1,128]{1,0:T(1,128)S(1)}, f32[1,128]{1,0:T(1,128)S(1)}, u32[]{:S(2)}, u32[]{:S(2)}) collective-permute-start(f32[1,128]{1,0:T(1,128)S(1)} %get-tuple-element.103), channel_id=1, source_target_pairs={{0,7},{1,6},{2,5},{3,4},{4,11},{5,10},{6,9},{7,8},{8,15},{9,14},{1... | collective-permute-start | bytes 1544 | tf_op jit(solution)/shard_map/ppermute | solution.py:229
  122.7 6.9 %collective-permute-done.38.refs_0_ = bf16[128,1024]{1,0:T(8,128)(2,1)S(1)} collective-permute-done((bf16[128,1024]{1,0:T(8,128)(2,1)S(1)}, bf16[128,1024]{1,0:T(8,128)(2,1)S(1)}, u32[]{:S(2)}, u32[]{:S(2)}) %collective-permute-start.38) | collective-permute-done | bytes 262176 | tf_op jit(solution)/shard_map/ppermute | solution.py:229
  131.9 3.3 %collective-permute-done.37 = bf16[128,1024]{1,0:T(8,128)(2,1)S(1)} collective-permute-done((bf16[128,1024]{1,0:T(8,128)(2,1)S(1)}, bf16[128,1024]{1,0:T(8,128)(2,1)S(1)}, u32[]{:S(2)}, u32[]{:S(2)}) %collective-permute-start.37) | collective-permute-done | bytes 262176 | tf_op jit(solution)/shard_map/ppermute | solution.py:229
  135.7 3.2 %collective-permute-start.42 = (bf16[128,1024]{1,0:T(8,128)(2,1)S(1)}, bf16[128,1024]{1,0:T(8,128)(2,1)S(1)}, u32[]{:S(2)}, u32[]{:S(2)}) collective-permute-start(bf16[128,1024]{1,0:T(8,128)(2,1)S(1)} %add_convert_fusion), channel_id=1, source_target_pairs={{0,2},{1,3},{2,0},{3,1},{4,6},{5,7},{6,4},{7,5},{8,10},{9,11},{10,... | collective-permute-start | bytes 786440 | tf_op jit(solution)/shard_map/ppermute | solution.py:229
  138.8 10.0 %collective-permute-done.41.refs_0_ = bf16[128,1024]{1,0:T(8,128)(2,1)S(1)} collective-permute-done((bf16[128,1024]{1,0:T(8,128)(2,1)S(1)}, bf16[128,1024]{1,0:T(8,128)(2,1)S(1)}, u32[]{:S(2)}, u32[]{:S(2)}) %collective-permute-start.41) | collective-permute-done | bytes 262176 | tf_op jit(solution)/shard_map/ppermute | solution.py:229
  (92 shorter events, 50.3 us)
Async XLA Ops:
  0.0 14.2 %collective-permute-start.3 = (bf16[128,1024]{1,0:T(8,128)(2,1)}, bf16[128,1024]{1,0:T(8,128)(2,1)S(1)}, u32[]{:S(2)}, u32[]{:S(2)}) collective-permute-start(bf16[128,1024]{1,0:T(8,128)(2,1)} %bitcast.25), channel_id=1, source_target_pairs={{0,28},{1,29},{2,30},{3,31},{4,24},{5,25},{6,26},{7,27},{8,20},{9,... | collective-permute-start | bytes 786440 | tf_op jit(solution)/shard_map/ppermute | solution.py:229
  17.7 11.4 %collective-permute-start.2 = (f32[2,128]{1,0:T(2,128)S(1)}, f32[2,128]{1,0:T(2,128)S(1)}, u32[]{:S(2)}, u32[]{:S(2)}) collective-permute-start(f32[2,128]{1,0:T(2,128)S(1)} %squares.1), channel_id=1, source_target_pairs={{0,3},{1,2},{2,1},{3,0},{4,7},{5,6},{6,5},{7,4},{8,11},{9,10},{10,... | collective-permute-start | bytes 3080 | tf_op jit(solution)/shard_map/ppermute | solution.py:229
  25.3 14.9 %collective-permute-start.15 = (bf16[128,1024]{1,0:T(8,128)(2,1)S(1)}, bf16[128,1024]{1,0:T(8,128)(2,1)S(1)}, u32[]{:S(2)}, u32[]{:S(2)}) collective-permute-start(bf16[128,1024]{1,0:T(8,128)(2,1)S(1)} %get-tuple-element.86), channel_id=1, source_target_pairs={{0,1},{1,0},{2,3},{3,2},{4,5},{5,4},{6,7},{7,6},{8,9},{9,8},{10,11... | collective-permute-start | bytes 786440 | tf_op jit(solution)/shard_map/ppermute | solution.py:229
  26.7 13.4 %collective-permute-start.16 = (bf16[128,1024]{1,0:T(8,128)(2,1)S(1)}, bf16[128,1024]{1,0:T(8,128)(2,1)S(1)}, u32[]{:S(2)}, u32[]{:S(2)}) collective-permute-start(bf16[128,1024]{1,0:T(8,128)(2,1)S(1)} %add_convert_fusion.5.refs_3_), channel_id=1, source_target_pairs={{0,2},{1,3},{2,0},{3,1},{4,6},{5,7},{6,4},{7,5},{8,10},{9,11},{10,... | collective-permute-start | bytes 786440 | tf_op jit(solution)/shard_map/ppermute | solution.py:229
  31.1 15.3 %collective-permute-start.8 = (bf16[128,1024]{1,0:T(8,128)(2,1)S(1)}, bf16[128,1024]{1,0:T(8,128)(2,1)S(1)}, u32[]{:S(2)}, u32[]{:S(2)}) collective-permute-start(bf16[128,1024]{1,0:T(8,128)(2,1)S(1)} %get-tuple-element.77), channel_id=1, source_target_pairs={{0,1},{1,0},{2,3},{3,2},{4,5},{5,4},{6,7},{7,6},{8,9},{9,8},{10,11... | collective-permute-start | bytes 786440 | tf_op jit(solution)/shard_map/ppermute | solution.py:229
  40.6 10.1 %collective-permute-start.17 = (bf16[128,1024]{1,0:T(8,128)(2,1)S(1)}, bf16[128,1024]{1,0:T(8,128)(2,1)S(1)}, u32[]{:S(2)}, u32[]{:S(2)}) collective-permute-start(bf16[128,1024]{1,0:T(8,128)(2,1)S(1)} %get-tuple-element.87), channel_id=1, source_target_pairs={{0,4},{1,5},{2,6},{3,7},{4,8},{5,9},{6,10},{7,11},{8,12},{9,13},{1... | collective-permute-start | bytes 786440 | tf_op jit(solution)/shard_map/ppermute | solution.py:229
  46.5 14.4 %collective-permute-start.9 = (bf16[128,1024]{1,0:T(8,128)(2,1)S(1)}, bf16[128,1024]{1,0:T(8,128)(2,1)S(1)}, u32[]{:S(2)}, u32[]{:S(2)}) collective-permute-start(bf16[128,1024]{1,0:T(8,128)(2,1)S(1)} %get-tuple-element.78), channel_id=1, source_target_pairs={{0,1},{1,0},{2,3},{3,2},{4,5},{5,4},{6,7},{7,6},{8,9},{9,8},{10,11... | collective-permute-start | bytes 786440 | tf_op jit(solution)/shard_map/ppermute | solution.py:229
  48.4 14.3 %collective-permute-start.10 = (bf16[128,1024]{1,0:T(8,128)(2,1)S(1)}, bf16[128,1024]{1,0:T(8,128)(2,1)S(1)}, u32[]{:S(2)}, u32[]{:S(2)}) collective-permute-start(bf16[128,1024]{1,0:T(8,128)(2,1)S(1)} %add_convert_fusion.4.refs_3_), channel_id=1, source_target_pairs={{0,2},{1,3},{2,0},{3,1},{4,6},{5,7},{6,4},{7,5},{8,10},{9,11},{10,... | collective-permute-start | bytes 786440 | tf_op jit(solution)/shard_map/ppermute | solution.py:229
  52.6 16.7 %collective-permute-start.21 = (bf16[128,1024]{1,0:T(8,128)(2,1)S(1)}, bf16[128,1024]{1,0:T(8,128)(2,1)S(1)}, u32[]{:S(2)}, u32[]{:S(2)}) collective-permute-start(bf16[128,1024]{1,0:T(8,128)(2,1)S(1)} %get-tuple-element.93), channel_id=1, source_target_pairs={{0,1},{1,0},{2,3},{3,2},{4,5},{5,4},{6,7},{7,6},{8,9},{9,8},{10,11... | collective-permute-start | bytes 786440 | tf_op jit(solution)/shard_map/ppermute | solution.py:229
  63.1 10.2 %collective-permute-start.11 = (bf16[128,1024]{1,0:T(8,128)(2,1)S(1)}, bf16[128,1024]{1,0:T(8,128)(2,1)S(1)}, u32[]{:S(2)}, u32[]{:S(2)}) collective-permute-start(bf16[128,1024]{1,0:T(8,128)(2,1)S(1)} %get-tuple-element.81), channel_id=1, source_target_pairs={{0,4},{1,5},{2,6},{3,7},{4,8},{5,9},{6,10},{7,11},{8,12},{9,13},{1... | collective-permute-start | bytes 786440 | tf_op jit(solution)/shard_map/ppermute | solution.py:229
  70.4 14.4 %collective-permute-start.29 = (bf16[128,1024]{1,0:T(8,128)(2,1)S(1)}, bf16[128,1024]{1,0:T(8,128)(2,1)S(1)}, u32[]{:S(2)}, u32[]{:S(2)}) collective-permute-start(bf16[128,1024]{1,0:T(8,128)(2,1)S(1)} %get-tuple-element.106), channel_id=1, source_target_pairs={{0,1},{1,0},{2,3},{3,2},{4,5},{5,4},{6,7},{7,6},{8,9},{9,8},{10,11... | collective-permute-start | bytes 786440 | tf_op jit(solution)/shard_map/ppermute | solution.py:229
  72.3 13.5 %collective-permute-start.30 = (bf16[128,1024]{1,0:T(8,128)(2,1)S(1)}, bf16[128,1024]{1,0:T(8,128)(2,1)S(1)}, u32[]{:S(2)}, u32[]{:S(2)}) collective-permute-start(bf16[128,1024]{1,0:T(8,128)(2,1)S(1)} %add_convert_fusion.3.refs_3_), channel_id=1, source_target_pairs={{0,2},{1,3},{2,0},{3,1},{4,6},{5,7},{6,4},{7,5},{8,10},{9,11},{10,... | collective-permute-start | bytes 786440 | tf_op jit(solution)/shard_map/ppermute | solution.py:229
  75.3 17.2 %collective-permute-start.22 = (bf16[128,1024]{1,0:T(8,128)(2,1)S(1)}, bf16[128,1024]{1,0:T(8,128)(2,1)S(1)}, u32[]{:S(2)}, u32[]{:S(2)}) collective-permute-start(bf16[128,1024]{1,0:T(8,128)(2,1)S(1)} %get-tuple-element.98), channel_id=1, source_target_pairs={{0,1},{1,0},{2,3},{3,2},{4,5},{5,4},{6,7},{7,6},{8,9},{9,8},{10,11... | collective-permute-start | bytes 786440 | tf_op jit(solution)/shard_map/ppermute | solution.py:229
  86.2 9.7 %collective-permute-start.32 = (bf16[128,1024]{1,0:T(8,128)(2,1)S(1)}, bf16[128,1024]{1,0:T(8,128)(2,1)S(1)}, u32[]{:S(2)}, u32[]{:S(2)}) collective-permute-start(bf16[128,1024]{1,0:T(8,128)(2,1)S(1)} %get-tuple-element.108), channel_id=1, source_target_pairs={{0,4},{1,5},{2,6},{3,7},{4,8},{5,9},{6,10},{7,11},{8,12},{9,13},{1... | collective-permute-start | bytes 786440 | tf_op jit(solution)/shard_map/ppermute | solution.py:229
  92.5 14.6 %collective-permute-start.23 = (bf16[128,1024]{1,0:T(8,128)(2,1)S(1)}, bf16[128,1024]{1,0:T(8,128)(2,1)S(1)}, u32[]{:S(2)}, u32[]{:S(2)}) collective-permute-start(bf16[128,1024]{1,0:T(8,128)(2,1)S(1)} %get-tuple-element.99), channel_id=1, source_target_pairs={{0,1},{1,0},{2,3},{3,2},{4,5},{5,4},{6,7},{7,6},{8,9},{9,8},{10,11... | collective-permute-start | bytes 786440 | tf_op jit(solution)/shard_map/ppermute | solution.py:229
  92.9 14.7 %collective-permute-start.24 = (bf16[128,1024]{1,0:T(8,128)(2,1)S(1)}, bf16[128,1024]{1,0:T(8,128)(2,1)S(1)}, u32[]{:S(2)}, u32[]{:S(2)}) collective-permute-start(bf16[128,1024]{1,0:T(8,128)(2,1)S(1)} %add_convert_fusion.2.refs_3_), channel_id=1, source_target_pairs={{0,2},{1,3},{2,0},{3,1},{4,6},{5,7},{6,4},{7,5},{8,10},{9,11},{10,... | collective-permute-start | bytes 786440 | tf_op jit(solution)/shard_map/ppermute | solution.py:229
  97.9 15.3 %collective-permute-start.36 = (bf16[128,1024]{1,0:T(8,128)(2,1)S(1)}, bf16[128,1024]{1,0:T(8,128)(2,1)S(1)}, u32[]{:S(2)}, u32[]{:S(2)}) collective-permute-start(bf16[128,1024]{1,0:T(8,128)(2,1)S(1)} %get-tuple-element.114), channel_id=1, source_target_pairs={{0,1},{1,0},{2,3},{3,2},{4,5},{5,4},{6,7},{7,6},{8,9},{9,8},{10,11... | collective-permute-start | bytes 786440 | tf_op jit(solution)/shard_map/ppermute | solution.py:229
  108.1 10.5 %collective-permute-start.25 = (bf16[128,1024]{1,0:T(8,128)(2,1)S(1)}, bf16[128,1024]{1,0:T(8,128)(2,1)S(1)}, u32[]{:S(2)}, u32[]{:S(2)}) collective-permute-start(bf16[128,1024]{1,0:T(8,128)(2,1)S(1)} %get-tuple-element.102), channel_id=1, source_target_pairs={{0,4},{1,5},{2,6},{3,7},{4,8},{5,9},{6,10},{7,11},{8,12},{9,13},{1... | collective-permute-start | bytes 786440 | tf_op jit(solution)/shard_map/ppermute | solution.py:229
  115.1 14.5 %collective-permute-start.38 = (bf16[128,1024]{1,0:T(8,128)(2,1)S(1)}, bf16[128,1024]{1,0:T(8,128)(2,1)S(1)}, u32[]{:S(2)}, u32[]{:S(2)}) collective-permute-start(bf16[128,1024]{1,0:T(8,128)(2,1)S(1)} %get-tuple-element.121), channel_id=1, source_target_pairs={{0,1},{1,0},{2,3},{3,2},{4,5},{5,4},{6,7},{7,6},{8,9},{9,8},{10,11... | collective-permute-start | bytes 786440 | tf_op jit(solution)/shard_map/ppermute | solution.py:229
  117.6 13.3 %collective-permute-start.39 = (bf16[128,1024]{1,0:T(8,128)(2,1)S(1)}, bf16[128,1024]{1,0:T(8,128)(2,1)S(1)}, u32[]{:S(2)}, u32[]{:S(2)}) collective-permute-start(bf16[128,1024]{1,0:T(8,128)(2,1)S(1)} %add_convert_fusion.1.refs_3_), channel_id=1, source_target_pairs={{0,2},{1,3},{2,0},{3,1},{4,6},{5,7},{6,4},{7,5},{8,10},{9,11},{10,... | collective-permute-start | bytes 786440 | tf_op jit(solution)/shard_map/ppermute | solution.py:229
  120.6 14.6 %collective-permute-start.37 = (bf16[128,1024]{1,0:T(8,128)(2,1)S(1)}, bf16[128,1024]{1,0:T(8,128)(2,1)S(1)}, u32[]{:S(2)}, u32[]{:S(2)}) collective-permute-start(bf16[128,1024]{1,0:T(8,128)(2,1)S(1)} %get-tuple-element.119), channel_id=1, source_target_pairs={{0,1},{1,0},{2,3},{3,2},{4,5},{5,4},{6,7},{7,6},{8,9},{9,8},{10,11... | collective-permute-start | bytes 786440 | tf_op jit(solution)/shard_map/ppermute | solution.py:229
  135.3 13.5 %collective-permute-start.41 = (bf16[128,1024]{1,0:T(8,128)(2,1)S(1)}, bf16[128,1024]{1,0:T(8,128)(2,1)S(1)}, u32[]{:S(2)}, u32[]{:S(2)}) collective-permute-start(bf16[128,1024]{1,0:T(8,128)(2,1)S(1)} %get-tuple-element.125), channel_id=1, source_target_pairs={{0,1},{1,0},{2,3},{3,2},{4,5},{5,4},{6,7},{7,6},{8,9},{9,8},{10,11... | collective-permute-start | bytes 786440 | tf_op jit(solution)/shard_map/ppermute | solution.py:229
  135.7 14.8 %collective-permute-start.42 = (bf16[128,1024]{1,0:T(8,128)(2,1)S(1)}, bf16[128,1024]{1,0:T(8,128)(2,1)S(1)}, u32[]{:S(2)}, u32[]{:S(2)}) collective-permute-start(bf16[128,1024]{1,0:T(8,128)(2,1)S(1)} %add_convert_fusion), channel_id=1, source_target_pairs={{0,2},{1,3},{2,0},{3,1},{4,6},{5,7},{6,4},{7,5},{8,10},{9,11},{10,... | collective-permute-start | bytes 786440 | tf_op jit(solution)/shard_map/ppermute | solution.py:229
  138.8 12.8 %collective-permute-start.43 = (bf16[128,1024]{1,0:T(8,128)(2,1)S(1)}, bf16[128,1024]{1,0:T(8,128)(2,1)S(1)}, u32[]{:S(2)}, u32[]{:S(2)}) collective-permute-start(bf16[128,1024]{1,0:T(8,128)(2,1)S(1)} %get-tuple-element.128), channel_id=1, source_target_pairs={{0,28},{1,29},{2,30},{3,31},{4,24},{5,25},{6,26},{7,27},{8,20},{9,... | collective-permute-start | bytes 786440 | tf_op jit(solution)/shard_map/ppermute | solution.py:229
  (22 other events, 161.4 us)

commit v4 on v3

--- a/solution.py
+++ b/solution.py
@@ -190,12 +190,16 @@
     )(x, gains, blocks, weight, *squares, *after)
 
 
-def merge_kernel(count, x_ref, fresh_ref, own_ref, *refs):
-    arrived, (y_ref, sent_ref, squares_ref) = refs[:count], refs[-3:]
+def section_output(x_ref, own_ref, arrived):
     total = own_ref[...]
     for ref in arrived:
         total = total + ref[...].astype(jnp.float32)
-    y = (x_ref[...].astype(jnp.float32) + total).astype(jnp.bfloat16)
+    return (x_ref[...].astype(jnp.float32) + total).astype(jnp.bfloat16)
+
+
+def merge_kernel(count, x_ref, fresh_ref, own_ref, *refs):
+    arrived, (y_ref, sent_ref, squares_ref) = refs[:count], refs[-3:]
+    y = section_output(x_ref, own_ref, arrived)
     y_ref[...] = y
     last = lax.axis_index("pipe") == lax.axis_size("pipe") - 1
     sent = jnp.where(last, fresh_ref[...].astype(jnp.float32), y.astype(jnp.float32))
@@ -219,6 +223,51 @@
     )(x, fresh, own, *arrived, *after)
 
 
+def end_kernel(count, x_ref, own_ref, *refs):
+    refs[-1][...] = section_output(x_ref, own_ref, refs[:count])
+
+
+def end(x, own, arrived, after):
+    return pl.pallas_call(
+        functools.partial(end_kernel, len(arrived)),
+        out_shape=jax.ShapeDtypeStruct(x.shape, jnp.bfloat16),
+        in_specs=[IN_VMEM] * (2 + len(arrived)) + [IN_PLACE] * len(after),
+        out_specs=IN_VMEM,
+        compiler_params=pltpu.CompilerParams(vmem_limit_bytes=6 * 2**20),
+        name="end",
+    )(x, own, *arrived, *after)
+
+
+def collect_kernel(count, spots, x_ref, own_ref, *refs):
+    arrived, earlier, (all_ref, y_ref, sems) = refs[:count], refs[count:-3], refs[-3:]
+    targets = [all_ref.at[tick, way, 0] for tick, way in spots]
+    copies = [
+        pltpu.make_async_copy(source, target, sems.at[spot])
+        for spot, (source, target) in enumerate(zip([*earlier, y_ref], targets))
+    ]
+    for copy in copies[:-1]:
+        copy.start()
+    y_ref[...] = section_output(x_ref, own_ref, arrived)
+    copies[-1].start()
+    for copy in copies:
+        copy.wait()
+
+
+def collect(x, own, arrived, earlier, spots):
+    return pl.pallas_call(
+        functools.partial(collect_kernel, len(arrived), spots),
+        out_shape=jax.ShapeDtypeStruct((TICK_COUNT, 2, 1, *x.shape), jnp.bfloat16),
+        in_specs=[IN_VMEM] * (2 + len(arrived)) + [IN_PLACE] * len(earlier),
+        out_specs=IN_PLACE,
+        scratch_shapes=[
+            pltpu.VMEM(x.shape, jnp.bfloat16),
+            pltpu.SemaphoreType.DMA((len(spots),)),
+        ],
+        compiler_params=pltpu.CompilerParams(vmem_limit_bytes=6 * 2**20),
+        name="collect",
+    )(x, own, *arrived, *earlier)
+
+
 def send(values, target):
     pipe, tensor = lax.axis_size("pipe"), lax.axis_size("tensor")
     pairs = []
@@ -245,7 +294,7 @@
 
 def other_halvings(partials):
     pair, rest = partials[:2], partials[2:]
-    arrived = [send(pair[1], lambda k, z: (k, z ^ 1))]
+    arrived = []
     left = {2 * (spot + 1): partial for spot, partial in enumerate(rest)}
     bit = 2
     while left:
@@ -261,7 +310,7 @@
                         jnp.float32
                     )
         bit *= 2
-    return arrived
+    return arrived + [send(pair[1], lambda k, z: (k, z ^ 1))]
 
 
 def local(
@@ -296,7 +345,7 @@
         rest = lax.optimization_barrier(rest)
         return own, other_halvings([own, *rest]), rest[1:2]
 
-    def run_layer(way, tick, after, held):
+    def run_layer(way, tick, after):
         *partials, neighbour = layer_partials(
             entering[way],
             squares[way],
@@ -307,31 +356,38 @@
             tensor,
             after,
         )
-        if way == up and tick > 0:
+        if (way, tick) in ((up, 1), (down, 2)):
             neighbour, y = lax.optimization_barrier((neighbour, leaving[up].pop()))
             leaving[up].append(send(y, lambda k, z: (mirrored(k), z)))
-        return first_halving([*partials, neighbour], held)
+        return [*partials, neighbour]
 
     def finish(way, tick, own, arrived):
-        newcomer = fresh[way][min(tick, TICK_COUNT - 2)]
-        y, sent, sums = merge(entering[way], newcomer, own, arrived, leaving[way][-1:])
+        after = leaving[up][-1:] if (way, tick) in ((down, 0), (up, 2)) else []
+        if tick == TICK_COUNT - 1:
+            leaving[way].append(end(entering[way], own, arrived, after))
+            return
+        y, sent, sums = merge(entering[way], fresh[way][tick], own, arrived, after)
         leaving[way].append(y)
-        if tick < TICK_COUNT - 1:
-            entering[way] = send(sent, lambda k, z: (following(k), z))
-            squares[way] = spread(sums, following)
+        entering[way] = send(sent, lambda k, z: (following(k), z))
+        squares[way] = spread(sums, following)
 
     leaving = [[], []]
-    early = []
-    for tick in range(TICK_COUNT):
-        for way in (up, down):
-            ending = tick == TICK_COUNT - 1 and way == down
-            held = [leaving[up].pop()] if ending else []
-            partials, held = run_layer(way, tick, early, held)
-            leaving[up].extend(held)
-            own, arrived, early = go_on(partials)
-            finish(way, tick, own, arrived)
+    partials, _ = first_halving(run_layer(up, 0, []), [])
+    own, arrived, early = go_on(partials)
+    for turn in range(1, 2 * TICK_COUNT):
+        way, tick = (up, down)[turn % 2], turn // 2
+        partials = run_layer(way, tick, early)
+        finish(1 - way, (turn - 1) // 2, own, arrived)
+        ending = turn == 2 * TICK_COUNT - 1
+        held = [leaving[up].pop()] if ending else []
+        partials, held = first_halving(partials, held)
+        leaving[up].extend(held)
+        own, arrived, early = go_on(partials)
     leaving[up].append(send(leaving[up].pop(), lambda k, z: (mirrored(k), z)))
-    return jnp.stack([jnp.stack(way) for way in leaving], axis=1)[:, :, None]
+    earlier = [*leaving[down], *leaving[up]]
+    spots = [(tick, down) for tick in range(TICK_COUNT - 1)]
+    spots += [(tick, up) for tick in range(TICK_COUNT)] + [(TICK_COUNT - 1, down)]
+    return collect(entering[down], own, arrived, earlier, spots)
 
 
 def solution(mesh):

time: 153 us -> 147 us (0.961)
  waiting for transfers between devices: 66.1 us -> 63.2 us
    ppermute x44, waiting for transfers between devices: 66.1 us -> 63.2 us  [send(): return lax.ppermute(values, ('pipe', 'tensor'), pairs)]
    pallas_call x6 -> x4, Pallas kernels: 3.75 us -> 1.73 us  [merge(): pl.pallas_call(functools.partial(merge_kernel, len(arrived)), out_shape=[...]
  transfers between devices with their start and end apart: 44 -> 44, of which waited for: 19 -> 17; matrix products, arithmetic and copies ran while one was open for 0% -> 0% of each run, Pallas kernels for 12% -> 11%
where the time goes in v4:
time: 147 us
  waiting for transfers between devices  63.2 us (43%)
  starting transfers between devices  63 us (43%)
  Pallas kernels  19.8 us (13%)
    ppermute x44, waiting for transfers between devices, send(): return lax.ppermute(values, ('pipe', 'tensor'), pairs)  63.2 us
    ppermute x44, starting transfers between devices, send(): return lax.ppermute(values, ('pipe', 'tensor'), pairs)  63 us
    pallas_call x6, Pallas kernels, layer_partials(): pl.pallas_call(functools.partial(layer_kernel, count, line), out_shape=[j...  11.7 us
    pallas_call x1, Pallas kernels, prepare(): pl.pallas_call(functools.partial(prepare_kernel, ticks), out_shape=[jax.S...  3.82 us
  transfers between devices with their start and end apart: 44, of which 17 were waited for; matrix products, arithmetic and copies ran while one was open for 0% of the time, Pallas kernels for 11%

profile of v4, /device:TPU:0, one launch (start us, length us, event | category | flops | bytes accessed | tf_op | source)
XLA Modules:
  0.0 146.8 jit_solution(14815877386690308142)
XLA Ops:
  0.0 3.3 %collective-permute-start.3 = (bf16[128,1024]{1,0:T(8,128)(2,1)}, bf16[128,1024]{1,0:T(8,128)(2,1)S(1)}, u32[]{:S(2)}, u32[]{:S(2)}) collective-permute-start(bf16[128,1024]{1,0:T(8,128)(2,1)} %bitcast.8), channel_id=1, source_target_pairs={{0,28},{1,29},{2,30},{3,31},{4,24},{5,25},{6,26},{7,27},{8,20},{9,... | collective-permute-start | bytes 786440 | tf_op jit(solution)/shard_map/ppermute | solution.py:278
  4.6 3.9 %collective-permute-start.6 = (f32[2,128]{1,0:T(2,128)S(1)}, f32[2,128]{1,0:T(2,128)S(1)}, u32[]{:S(2)}, u32[]{:S(2)}) collective-permute-start(f32[2,128]{1,0:T(2,128)S(1)} %squares.1), channel_id=1, source_target_pairs={{0,31},{1,30},{2,29},{3,28},{4,27},{5,26},{6,25},{7,24},{8,23},{9,... | collective-permute-start | bytes 3080 | tf_op jit(solution)/shard_map/ppermute | solution.py:278
  10.4 3.8 %prepare.1 = (bf16[8,128,1024]{2,1,0:T(8,128)(2,1)S(1)}, bf16[1024,4096]{1,0:T(8,128)(2,1)S(1)}, bf16[128,1024]{1,0:T(8,128)(2,1)S(1)}, bf16[128,1024]{1,0:T(8,1...) custom-call(s32[2,8]{1,0:T(2,128)} %order_hbm.1, f32[64,128]{1,0:T(8,128)} %bitcast.10, ...), custom_call_target="tpu_custom_call" | custom-call | tf_op jit(solution)/shard_map/prepare/pallas_call | solution.py:79
  14.3 2.0 %layer.6 = (f32[128,1024]{1,0:T(8,128)S(1)}, bf16[128,1024]{1,0:T(8,128)(2,1)S(1)}, f32[128,1024]{1,0:T(8,128)S(1)}, bf16[128,1024]{1,0:T(8,128)(2,1)S(1)}) custom-call(bf16[128,1024]{1,0:T(8,128)(2,1)S(1)} %collective-permute-done.3.x_ref, f32[1,1024]{1,0:T(1,128)S(1)} %copy-done.1, bf16[8,128,1024]{2,1,0:T(8,128)(2,1)S(1)} %get-tuple-element.66.blocks_ref, ...), custom_call_target="tpu_custom_call" | custom-call | flops 1073741824 | bytes 8388608 | tf_op jit(solution)/shard_map/layer/pallas_call | solution.py:177
  17.7 3.3 %collective-permute-start.2 = (f32[2,128]{1,0:T(2,128)S(1)}, f32[2,128]{1,0:T(2,128)S(1)}, u32[]{:S(2)}, u32[]{:S(2)}) collective-permute-start(f32[2,128]{1,0:T(2,128)S(1)} %squares.1), channel_id=1, source_target_pairs={{0,3},{1,2},{2,1},{3,0},{4,7},{5,6},{6,5},{7,4},{8,11},{9,10},{10,... | collective-permute-start | bytes 3080 | tf_op jit(solution)/shard_map/ppermute | solution.py:278
  22.1 3.1 %collective-permute-done.7 = bf16[128,1024]{1,0:T(8,128)(2,1)S(1)} collective-permute-done((bf16[128,1024]{1,0:T(8,128)(2,1)S(1)}, bf16[128,1024]{1,0:T(8,128)(2,1)S(1)}, u32[]{:S(2)}, u32[]{:S(2)}) %collective-permute-start.7) | collective-permute-done | bytes 262176 | tf_op jit(solution)/shard_map/ppermute | solution.py:278
  26.7 2.4 %collective-permute-start.11 = (bf16[128,1024]{1,0:T(8,128)(2,1)S(1)}, bf16[128,1024]{1,0:T(8,128)(2,1)S(1)}, u32[]{:S(2)}, u32[]{:S(2)}) collective-permute-start(bf16[128,1024]{1,0:T(8,128)(2,1)S(1)} %add_convert_fusion.5.refs_3_), channel_id=1, source_target_pairs={{0,2},{1,3},{2,0},{3,1},{4,6},{5,7},{6,4},{7,5},{8,10},{9,11},{10,... | collective-permute-start | bytes 786440 | tf_op jit(solution)/shard_map/ppermute | solution.py:278
  29.2 2.0 %layer.7 = (f32[128,1024]{1,0:T(8,128)S(1)}, bf16[128,1024]{1,0:T(8,128)(2,1)S(1)}, f32[128,1024]{1,0:T(8,128)S(1)}, bf16[128,1024]{1,0:T(8,128)(2,1)S(1)}) custom-call(bf16[128,1024]{1,0:T(8,128)(2,1)S(1)} %bitcast.5, f32[1,1024]{1,0:T(1,128)S(1)} %copy-done.1, bf16[8,128,1024]{2,1,0:T(8,128)(2,1)S(1)} %get-tuple-element.66.blocks_ref, ...), custom_call_target="tpu_custom_call" | custom-call | flops 1073741824 | bytes 8388608 | tf_op jit(solution)/shard_map/layer/pallas_call | solution.py:177
  32.6 7.5 %collective-permute-done.12.refs_1_ = bf16[128,1024]{1,0:T(8,128)(2,1)S(1)} collective-permute-done((bf16[128,1024]{1,0:T(8,128)(2,1)S(1)}, bf16[128,1024]{1,0:T(8,128)(2,1)S(1)}, u32[]{:S(2)}, u32[]{:S(2)}) %collective-permute-start.12) | collective-permute-done | bytes 262176 | tf_op jit(solution)/shard_map/ppermute | solution.py:278
  40.7 4.3 %collective-permute-start.16 = (f32[1,128]{1,0:T(1,128)S(1)}, f32[1,128]{1,0:T(1,128)S(1)}, u32[]{:S(2)}, u32[]{:S(2)}) collective-permute-start(f32[1,128]{1,0:T(1,128)S(1)} %get-tuple-element.82), channel_id=1, source_target_pairs={{0,7},{1,6},{2,5},{3,4},{4,11},{5,10},{6,9},{7,8},{8,15},{9,14},{1... | collective-permute-start | bytes 1544 | tf_op jit(solution)/shard_map/ppermute | solution.py:278
  48.4 2.2 %collective-permute-start.9 = (bf16[128,1024]{1,0:T(8,128)(2,1)S(1)}, bf16[128,1024]{1,0:T(8,128)(2,1)S(1)}, u32[]{:S(2)}, u32[]{:S(2)}) collective-permute-start(bf16[128,1024]{1,0:T(8,128)(2,1)S(1)} %add_convert_fusion.4.refs_3_), channel_id=1, source_target_pairs={{0,2},{1,3},{2,0},{3,1},{4,6},{5,7},{6,4},{7,5},{8,10},{9,11},{10,... | collective-permute-start | bytes 786440 | tf_op jit(solution)/shard_map/ppermute | solution.py:278
  54.6 6.3 %collective-permute-done.10.refs_1_ = bf16[128,1024]{1,0:T(8,128)(2,1)S(1)} collective-permute-done((bf16[128,1024]{1,0:T(8,128)(2,1)S(1)}, bf16[128,1024]{1,0:T(8,128)(2,1)S(1)}, u32[]{:S(2)}, u32[]{:S(2)}) %collective-permute-start.10) | collective-permute-done | bytes 262176 | tf_op jit(solution)/shard_map/ppermute | solution.py:278
  63.2 3.4 %collective-permute-start.21 = (f32[1,128]{1,0:T(1,128)S(1)}, f32[1,128]{1,0:T(1,128)S(1)}, u32[]{:S(2)}, u32[]{:S(2)}) collective-permute-start(f32[1,128]{1,0:T(1,128)S(1)} %get-tuple-element.88), channel_id=1, source_target_pairs={{0,7},{1,6},{2,5},{3,4},{4,11},{5,10},{6,9},{7,8},{8,15},{9,14},{1... | collective-permute-start | bytes 1544 | tf_op jit(solution)/shard_map/ppermute | solution.py:278
  66.6 2.7 %collective-permute-start.19 = (f32[1,128]{1,0:T(1,128)S(1)}, f32[1,128]{1,0:T(1,128)S(1)}, u32[]{:S(2)}, u32[]{:S(2)}) collective-permute-start(f32[1,128]{1,0:T(1,128)S(1)} %get-tuple-element.88), channel_id=1, source_target_pairs={{0,5},{1,4},{2,7},{3,6},{4,9},{5,8},{6,11},{7,10},{8,13},{9,12},{1... | collective-permute-start | bytes 1544 | tf_op jit(solution)/shard_map/ppermute | solution.py:278
  69.8 2.9 %collective-permute-start.30 = (bf16[128,1024]{1,0:T(8,128)(2,1)S(1)}, bf16[128,1024]{1,0:T(8,128)(2,1)S(1)}, u32[]{:S(2)}, u32[]{:S(2)}) collective-permute-start(bf16[128,1024]{1,0:T(8,128)(2,1)S(1)} %add_convert_fusion.3.refs_3_), channel_id=1, source_target_pairs={{0,2},{1,3},{2,0},{3,1},{4,6},{5,7},{6,4},{7,5},{8,10},{9,11},{10,... | collective-permute-start | bytes 786440 | tf_op jit(solution)/shard_map/ppermute | solution.py:278
  75.0 9.1 %collective-permute-done.31.refs_1_ = bf16[128,1024]{1,0:T(8,128)(2,1)S(1)} collective-permute-done((bf16[128,1024]{1,0:T(8,128)(2,1)S(1)}, bf16[128,1024]{1,0:T(8,128)(2,1)S(1)}, u32[]{:S(2)}, u32[]{:S(2)}) %collective-permute-start.31) | collective-permute-done | bytes 262176 | tf_op jit(solution)/shard_map/ppermute | solution.py:278
  85.0 3.8 %collective-permute-start.35 = (f32[1,128]{1,0:T(1,128)S(1)}, f32[1,128]{1,0:T(1,128)S(1)}, u32[]{:S(2)}, u32[]{:S(2)}) collective-permute-start(f32[1,128]{1,0:T(1,128)S(1)} %get-tuple-element.105), channel_id=1, source_target_pairs={{0,7},{1,6},{2,5},{3,4},{4,11},{5,10},{6,9},{7,8},{8,15},{9,14},{1... | collective-permute-start | bytes 1544 | tf_op jit(solution)/shard_map/ppermute | solution.py:278
  91.6 2.7 %collective-permute-start.24 = (bf16[128,1024]{1,0:T(8,128)(2,1)S(1)}, bf16[128,1024]{1,0:T(8,128)(2,1)S(1)}, u32[]{:S(2)}, u32[]{:S(2)}) collective-permute-start(bf16[128,1024]{1,0:T(8,128)(2,1)S(1)} %add_convert_fusion.2.refs_3_), channel_id=1, source_target_pairs={{0,2},{1,3},{2,0},{3,1},{4,6},{5,7},{6,4},{7,5},{8,10},{9,11},{10,... | collective-permute-start | bytes 786440 | tf_op jit(solution)/shard_map/ppermute | solution.py:278
  96.9 8.0 %collective-permute-done.25.refs_1_ = bf16[128,1024]{1,0:T(8,128)(2,1)S(1)} collective-permute-done((bf16[128,1024]{1,0:T(8,128)(2,1)S(1)}, bf16[128,1024]{1,0:T(8,128)(2,1)S(1)}, u32[]{:S(2)}, u32[]{:S(2)}) %collective-permute-start.25) | collective-permute-done | bytes 262176 | tf_op jit(solution)/shard_map/ppermute | solution.py:278
  106.5 3.8 %collective-permute-start.29 = (f32[1,128]{1,0:T(1,128)S(1)}, f32[1,128]{1,0:T(1,128)S(1)}, u32[]{:S(2)}, u32[]{:S(2)}) collective-permute-start(f32[1,128]{1,0:T(1,128)S(1)} %get-tuple-element.100), channel_id=1, source_target_pairs={{0,7},{1,6},{2,5},{3,4},{4,11},{5,10},{6,9},{7,8},{8,15},{9,14},{1... | collective-permute-start | bytes 1544 | tf_op jit(solution)/shard_map/ppermute | solution.py:278
  113.1 2.4 %collective-permute-start.38 = (bf16[128,1024]{1,0:T(8,128)(2,1)S(1)}, bf16[128,1024]{1,0:T(8,128)(2,1)S(1)}, u32[]{:S(2)}, u32[]{:S(2)}) collective-permute-start(bf16[128,1024]{1,0:T(8,128)(2,1)S(1)} %add_convert_fusion.1.refs_3_), channel_id=1, source_target_pairs={{0,2},{1,3},{2,0},{3,1},{4,6},{5,7},{6,4},{7,5},{8,10},{9,11},{10,... | collective-permute-start | bytes 786440 | tf_op jit(solution)/shard_map/ppermute | solution.py:278
  119.0 7.8 %collective-permute-done.39.refs_1_ = bf16[128,1024]{1,0:T(8,128)(2,1)S(1)} collective-permute-done((bf16[128,1024]{1,0:T(8,128)(2,1)S(1)}, bf16[128,1024]{1,0:T(8,128)(2,1)S(1)}, u32[]{:S(2)}, u32[]{:S(2)}) %collective-permute-start.39) | collective-permute-done | bytes 262176 | tf_op jit(solution)/shard_map/ppermute | solution.py:278
  127.3 4.2 %collective-permute-done.37 = bf16[128,1024]{1,0:T(8,128)(2,1)S(1)} collective-permute-done((bf16[128,1024]{1,0:T(8,128)(2,1)S(1)}, bf16[128,1024]{1,0:T(8,128)(2,1)S(1)}, u32[]{:S(2)}, u32[]{:S(2)}) %collective-permute-start.37) | collective-permute-done | bytes 262176 | tf_op jit(solution)/shard_map/ppermute | solution.py:278
  135.0 10.5 %collective-permute-done.41.refs_0_ = bf16[128,1024]{1,0:T(8,128)(2,1)S(1)} collective-permute-done((bf16[128,1024]{1,0:T(8,128)(2,1)S(1)}, bf16[128,1024]{1,0:T(8,128)(2,1)S(1)}, u32[]{:S(2)}, u32[]{:S(2)}) %collective-permute-start.41) | collective-permute-done | bytes 262176 | tf_op jit(solution)/shard_map/ppermute | solution.py:278
  (88 shorter events, 41.2 us)
Async XLA Ops:
  0.0 14.3 %collective-permute-start.3 = (bf16[128,1024]{1,0:T(8,128)(2,1)}, bf16[128,1024]{1,0:T(8,128)(2,1)S(1)}, u32[]{:S(2)}, u32[]{:S(2)}) collective-permute-start(bf16[128,1024]{1,0:T(8,128)(2,1)} %bitcast.8), channel_id=1, source_target_pairs={{0,28},{1,29},{2,30},{3,31},{4,24},{5,25},{6,26},{7,27},{8,20},{9,... | collective-permute-start | bytes 786440 | tf_op jit(solution)/shard_map/ppermute | solution.py:278
  4.6 9.7 %collective-permute-start.6 = (f32[2,128]{1,0:T(2,128)S(1)}, f32[2,128]{1,0:T(2,128)S(1)}, u32[]{:S(2)}, u32[]{:S(2)}) collective-permute-start(f32[2,128]{1,0:T(2,128)S(1)} %squares.1), channel_id=1, source_target_pairs={{0,31},{1,30},{2,29},{3,28},{4,27},{5,26},{6,25},{7,24},{8,23},{9,... | collective-permute-start | bytes 3080 | tf_op jit(solution)/shard_map/ppermute | solution.py:278
  17.7 11.4 %collective-permute-start.2 = (f32[2,128]{1,0:T(2,128)S(1)}, f32[2,128]{1,0:T(2,128)S(1)}, u32[]{:S(2)}, u32[]{:S(2)}) collective-permute-start(f32[2,128]{1,0:T(2,128)S(1)} %squares.1), channel_id=1, source_target_pairs={{0,3},{1,2},{2,1},{3,0},{4,7},{5,6},{6,5},{7,4},{8,11},{9,10},{10,... | collective-permute-start | bytes 3080 | tf_op jit(solution)/shard_map/ppermute | solution.py:278
  25.3 14.9 %collective-permute-start.12 = (bf16[128,1024]{1,0:T(8,128)(2,1)S(1)}, bf16[128,1024]{1,0:T(8,128)(2,1)S(1)}, u32[]{:S(2)}, u32[]{:S(2)}) collective-permute-start(bf16[128,1024]{1,0:T(8,128)(2,1)S(1)} %get-tuple-element.80), channel_id=1, source_target_pairs={{0,1},{1,0},{2,3},{3,2},{4,5},{5,4},{6,7},{7,6},{8,9},{9,8},{10,11... | collective-permute-start | bytes 786440 | tf_op jit(solution)/shard_map/ppermute | solution.py:278
  26.7 13.4 %collective-permute-start.11 = (bf16[128,1024]{1,0:T(8,128)(2,1)S(1)}, bf16[128,1024]{1,0:T(8,128)(2,1)S(1)}, u32[]{:S(2)}, u32[]{:S(2)}) collective-permute-start(bf16[128,1024]{1,0:T(8,128)(2,1)S(1)} %add_convert_fusion.5.refs_3_), channel_id=1, source_target_pairs={{0,2},{1,3},{2,0},{3,1},{4,6},{5,7},{6,4},{7,5},{8,10},{9,11},{10,... | collective-permute-start | bytes 786440 | tf_op jit(solution)/shard_map/ppermute | solution.py:278
  31.1 15.3 %collective-permute-start.8 = (bf16[128,1024]{1,0:T(8,128)(2,1)S(1)}, bf16[128,1024]{1,0:T(8,128)(2,1)S(1)}, u32[]{:S(2)}, u32[]{:S(2)}) collective-permute-start(bf16[128,1024]{1,0:T(8,128)(2,1)S(1)} %get-tuple-element.75), channel_id=1, source_target_pairs={{0,1},{1,0},{2,3},{3,2},{4,5},{5,4},{6,7},{7,6},{8,9},{9,8},{10,11... | collective-permute-start | bytes 786440 | tf_op jit(solution)/shard_map/ppermute | solution.py:278
  40.6 10.1 %collective-permute-start.13 = (bf16[128,1024]{1,0:T(8,128)(2,1)S(1)}, bf16[128,1024]{1,0:T(8,128)(2,1)S(1)}, u32[]{:S(2)}, u32[]{:S(2)}) collective-permute-start(bf16[128,1024]{1,0:T(8,128)(2,1)S(1)} %get-tuple-element.81), channel_id=1, source_target_pairs={{0,4},{1,5},{2,6},{3,7},{4,8},{5,9},{6,10},{7,11},{8,12},{9,13},{1... | collective-permute-start | bytes 786440 | tf_op jit(solution)/shard_map/ppermute | solution.py:278
  46.5 14.4 %collective-permute-start.10 = (bf16[128,1024]{1,0:T(8,128)(2,1)S(1)}, bf16[128,1024]{1,0:T(8,128)(2,1)S(1)}, u32[]{:S(2)}, u32[]{:S(2)}) collective-permute-start(bf16[128,1024]{1,0:T(8,128)(2,1)S(1)} %get-tuple-element.77), channel_id=1, source_target_pairs={{0,1},{1,0},{2,3},{3,2},{4,5},{5,4},{6,7},{7,6},{8,9},{9,8},{10,11... | collective-permute-start | bytes 786440 | tf_op jit(solution)/shard_map/ppermute | solution.py:278
  48.4 14.3 %collective-permute-start.9 = (bf16[128,1024]{1,0:T(8,128)(2,1)S(1)}, bf16[128,1024]{1,0:T(8,128)(2,1)S(1)}, u32[]{:S(2)}, u32[]{:S(2)}) collective-permute-start(bf16[128,1024]{1,0:T(8,128)(2,1)S(1)} %add_convert_fusion.4.refs_3_), channel_id=1, source_target_pairs={{0,2},{1,3},{2,0},{3,1},{4,6},{5,7},{6,4},{7,5},{8,10},{9,11},{10,... | collective-permute-start | bytes 786440 | tf_op jit(solution)/shard_map/ppermute | solution.py:278
  52.6 10.1 %collective-permute-start.17 = (bf16[128,1024]{1,0:T(8,128)(2,1)S(1)}, bf16[128,1024]{1,0:T(8,128)(2,1)S(1)}, u32[]{:S(2)}, u32[]{:S(2)}) collective-permute-start(bf16[128,1024]{1,0:T(8,128)(2,1)S(1)} %get-tuple-element.85), channel_id=1, source_target_pairs={{0,28},{1,29},{2,30},{3,31},{4,24},{5,25},{6,26},{7,27},{8,20},{9,... | collective-permute-start | bytes 786440 | tf_op jit(solution)/shard_map/ppermute | solution.py:278
  53.1 16.2 %collective-permute-start.22 = (bf16[128,1024]{1,0:T(8,128)(2,1)S(1)}, bf16[128,1024]{1,0:T(8,128)(2,1)S(1)}, u32[]{:S(2)}, u32[]{:S(2)}) collective-permute-start(bf16[128,1024]{1,0:T(8,128)(2,1)S(1)} %get-tuple-element.91), channel_id=1, source_target_pairs={{0,1},{1,0},{2,3},{3,2},{4,5},{5,4},{6,7},{7,6},{8,9},{9,8},{10,11... | collective-permute-start | bytes 786440 | tf_op jit(solution)/shard_map/ppermute | solution.py:278
  63.2 9.6 %collective-permute-start.18 = (bf16[128,1024]{1,0:T(8,128)(2,1)S(1)}, bf16[128,1024]{1,0:T(8,128)(2,1)S(1)}, u32[]{:S(2)}, u32[]{:S(2)}) collective-permute-start(bf16[128,1024]{1,0:T(8,128)(2,1)S(1)} %get-tuple-element.86), channel_id=1, source_target_pairs={{0,4},{1,5},{2,6},{3,7},{4,8},{5,9},{6,10},{7,11},{8,12},{9,13},{1... | collective-permute-start | bytes 786440 | tf_op jit(solution)/shard_map/ppermute | solution.py:278
  69.4 14.7 %collective-permute-start.31 = (bf16[128,1024]{1,0:T(8,128)(2,1)S(1)}, bf16[128,1024]{1,0:T(8,128)(2,1)S(1)}, u32[]{:S(2)}, u32[]{:S(2)}) collective-permute-start(bf16[128,1024]{1,0:T(8,128)(2,1)S(1)} %get-tuple-element.103), channel_id=1, source_target_pairs={{0,1},{1,0},{2,3},{3,2},{4,5},{5,4},{6,7},{7,6},{8,9},{9,8},{10,11... | collective-permute-start | bytes 786440 | tf_op jit(solution)/shard_map/ppermute | solution.py:278
  69.8 14.6 %collective-permute-start.30 = (bf16[128,1024]{1,0:T(8,128)(2,1)S(1)}, bf16[128,1024]{1,0:T(8,128)(2,1)S(1)}, u32[]{:S(2)}, u32[]{:S(2)}) collective-permute-start(bf16[128,1024]{1,0:T(8,128)(2,1)S(1)} %add_convert_fusion.3.refs_3_), channel_id=1, source_target_pairs={{0,2},{1,3},{2,0},{3,1},{4,6},{5,7},{6,4},{7,5},{8,10},{9,11},{10,... | collective-permute-start | bytes 786440 | tf_op jit(solution)/shard_map/ppermute | solution.py:278
  74.7 15.5 %collective-permute-start.23 = (bf16[128,1024]{1,0:T(8,128)(2,1)S(1)}, bf16[128,1024]{1,0:T(8,128)(2,1)S(1)}, u32[]{:S(2)}, u32[]{:S(2)}) collective-permute-start(bf16[128,1024]{1,0:T(8,128)(2,1)S(1)} %get-tuple-element.96), channel_id=1, source_target_pairs={{0,1},{1,0},{2,3},{3,2},{4,5},{5,4},{6,7},{7,6},{8,9},{9,8},{10,11... | collective-permute-start | bytes 786440 | tf_op jit(solution)/shard_map/ppermute | solution.py:278
  90.2 14.6 %collective-permute-start.25 = (bf16[128,1024]{1,0:T(8,128)(2,1)S(1)}, bf16[128,1024]{1,0:T(8,128)(2,1)S(1)}, u32[]{:S(2)}, u32[]{:S(2)}) collective-permute-start(bf16[128,1024]{1,0:T(8,128)(2,1)S(1)} %get-tuple-element.98), channel_id=1, source_target_pairs={{0,1},{1,0},{2,3},{3,2},{4,5},{5,4},{6,7},{7,6},{8,9},{9,8},{10,11... | collective-permute-start | bytes 786440 | tf_op jit(solution)/shard_map/ppermute | solution.py:278
  91.6 14.4 %collective-permute-start.24 = (bf16[128,1024]{1,0:T(8,128)(2,1)S(1)}, bf16[128,1024]{1,0:T(8,128)(2,1)S(1)}, u32[]{:S(2)}, u32[]{:S(2)}) collective-permute-start(bf16[128,1024]{1,0:T(8,128)(2,1)S(1)} %add_convert_fusion.2.refs_3_), channel_id=1, source_target_pairs={{0,2},{1,3},{2,0},{3,1},{4,6},{5,7},{6,4},{7,5},{8,10},{9,11},{10,... | collective-permute-start | bytes 786440 | tf_op jit(solution)/shard_map/ppermute | solution.py:278
  96.3 15.7 %collective-permute-start.36 = (bf16[128,1024]{1,0:T(8,128)(2,1)S(1)}, bf16[128,1024]{1,0:T(8,128)(2,1)S(1)}, u32[]{:S(2)}, u32[]{:S(2)}) collective-permute-start(bf16[128,1024]{1,0:T(8,128)(2,1)S(1)} %get-tuple-element.108), channel_id=1, source_target_pairs={{0,1},{1,0},{2,3},{3,2},{4,5},{5,4},{6,7},{7,6},{8,9},{9,8},{10,11... | collective-permute-start | bytes 786440 | tf_op jit(solution)/shard_map/ppermute | solution.py:278
  112.1 14.7 %collective-permute-start.39 = (bf16[128,1024]{1,0:T(8,128)(2,1)S(1)}, bf16[128,1024]{1,0:T(8,128)(2,1)S(1)}, u32[]{:S(2)}, u32[]{:S(2)}) collective-permute-start(bf16[128,1024]{1,0:T(8,128)(2,1)S(1)} %get-tuple-element.117), channel_id=1, source_target_pairs={{0,1},{1,0},{2,3},{3,2},{4,5},{5,4},{6,7},{7,6},{8,9},{9,8},{10,11... | collective-permute-start | bytes 786440 | tf_op jit(solution)/shard_map/ppermute | solution.py:278
  113.1 14.1 %collective-permute-start.38 = (bf16[128,1024]{1,0:T(8,128)(2,1)S(1)}, bf16[128,1024]{1,0:T(8,128)(2,1)S(1)}, u32[]{:S(2)}, u32[]{:S(2)}) collective-permute-start(bf16[128,1024]{1,0:T(8,128)(2,1)S(1)} %add_convert_fusion.1.refs_3_), channel_id=1, source_target_pairs={{0,2},{1,3},{2,0},{3,1},{4,6},{5,7},{6,4},{7,5},{8,10},{9,11},{10,... | collective-permute-start | bytes 786440 | tf_op jit(solution)/shard_map/ppermute | solution.py:278
  118.4 13.1 %collective-permute-start.37 = (bf16[128,1024]{1,0:T(8,128)(2,1)S(1)}, bf16[128,1024]{1,0:T(8,128)(2,1)S(1)}, u32[]{:S(2)}, u32[]{:S(2)}) collective-permute-start(bf16[128,1024]{1,0:T(8,128)(2,1)S(1)} %get-tuple-element.115), channel_id=1, source_target_pairs={{0,1},{1,0},{2,3},{3,2},{4,5},{5,4},{6,7},{7,6},{8,9},{9,8},{10,11... | collective-permute-start | bytes 786440 | tf_op jit(solution)/shard_map/ppermute | solution.py:278
  131.6 13.8 %collective-permute-start.41 = (bf16[128,1024]{1,0:T(8,128)(2,1)S(1)}, bf16[128,1024]{1,0:T(8,128)(2,1)S(1)}, u32[]{:S(2)}, u32[]{:S(2)}) collective-permute-start(bf16[128,1024]{1,0:T(8,128)(2,1)S(1)} %add_convert_fusion), channel_id=1, source_target_pairs={{0,2},{1,3},{2,0},{3,1},{4,6},{5,7},{6,4},{7,5},{8,10},{9,11},{10,... | collective-permute-start | bytes 786440 | tf_op jit(solution)/shard_map/ppermute | solution.py:278
  133.5 12.0 %collective-permute-start.42 = (bf16[128,1024]{1,0:T(8,128)(2,1)S(1)}, bf16[128,1024]{1,0:T(8,128)(2,1)S(1)}, u32[]{:S(2)}, u32[]{:S(2)}) collective-permute-start(bf16[128,1024]{1,0:T(8,128)(2,1)S(1)} %get-tuple-element.121), channel_id=1, source_target_pairs={{0,1},{1,0},{2,3},{3,2},{4,5},{5,4},{6,7},{7,6},{8,9},{9,8},{10,11... | collective-permute-start | bytes 786440 | tf_op jit(solution)/shard_map/ppermute | solution.py:278
  134.9 10.5 %collective-permute-start.43 = (bf16[128,1024]{1,0:T(8,128)(2,1)S(1)}, bf16[128,1024]{1,0:T(8,128)(2,1)S(1)}, u32[]{:S(2)}, u32[]{:S(2)}) collective-permute-start(bf16[128,1024]{1,0:T(8,128)(2,1)S(1)} %end.1), channel_id=1, source_target_pairs={{0,28},{1,29},{2,30},{3,31},{4,24},{5,25},{6,26},{7,27},{8,20},{9,... | collective-permute-start | bytes 786440 | tf_op jit(solution)/shard_map/ppermute | solution.py:278
  (22 other events, 171.2 us)

commit v5 on v4

--- a/solution.py
+++ b/solution.py
@@ -18,6 +18,11 @@
 PER_BLOCK = LANES // GROUP_SIZE
 IN_VMEM = pl.BlockSpec(memory_space=pltpu.VMEM)
 IN_PLACE = pl.BlockSpec(memory_space=pl.ANY)
+
+
+def halves(values):
+    high = values.astype(jnp.bfloat16)
+    return high, (values - high.astype(jnp.float32)).astype(jnp.bfloat16)
 
 
 def prepare_kernel(
@@ -44,18 +49,19 @@
     groups, seq = filters_ref.shape
     taps = jnp.where(lax.axis_index("pipe") % 2 == 0, SHORT_TAPS, LONG_TAPS)
     lane = lax.broadcasted_iota(jnp.int32, (groups, seq), 1)
-    kept = jnp.where(lane < taps, filters_ref[...], 0.0).astype(jnp.bfloat16)
+    kept = jnp.where(lane < taps, filters_ref[...], 0.0)
     row = lax.broadcasted_iota(jnp.int32, (seq, seq), 0)
     col = lax.broadcasted_iota(jnp.int32, (seq, seq), 1)
     flip = ((row + col) % seq == 0).astype(jnp.bfloat16)
-    backward = jnp.dot(kept, flip, preferred_element_type=jnp.float32)
+    backward = sum(
+        jnp.dot(part, flip, preferred_element_type=jnp.float32) for part in halves(kept)
+    )
     for group in range(groups):
         wide = jnp.broadcast_to(backward[group : group + 1, :], (seq, seq))
         turned = pltpu.roll(wide, 0, 1, stride=1, stride_axis=0)
         start = group % PER_BLOCK * seq
-        blocks_ref[group // PER_BLOCK, :, start : start + seq] = jnp.where(
-            row >= col, turned, 0.0
-        ).astype(jnp.bfloat16)
+        for half, part in enumerate(halves(jnp.where(row >= col, turned, 0.0))):
+            blocks_ref[group // PER_BLOCK, half, :, start : start + seq] = part
     for copy in copies[1:4]:
         copy.wait()
     word = lax.broadcasted_iota(jnp.int32, (table_ref.shape[0], seq), 0)
@@ -79,7 +85,7 @@
     blocks, held, *fresh = pl.pallas_call(
         functools.partial(prepare_kernel, ticks),
         out_shape=[
-            jax.ShapeDtypeStruct((groups // PER_BLOCK, seq, PER_BLOCK * seq), jnp.bfloat16),
+            jax.ShapeDtypeStruct((groups // PER_BLOCK, 2, seq, PER_BLOCK * seq), jnp.bfloat16),
             jax.ShapeDtypeStruct(weight.shape, weight.dtype),
         ]
         + [jax.ShapeDtypeStruct((seq, table.shape[1]), table.dtype)] * (2 * ticks),
@@ -92,7 +98,7 @@
             pltpu.VMEM(table.shape, table.dtype),
             pltpu.SemaphoreType.DMA((5,)),
         ],
-        compiler_params=pltpu.CompilerParams(vmem_limit_bytes=16 * 2**20),
+        compiler_params=pltpu.CompilerParams(vmem_limit_bytes=20 * 2**20),
         name="prepare",
     )(in_hbm(order), in_hbm(filters), in_hbm(tokens), in_hbm(table), in_hbm(weight))
     return blocks, held, [fresh[:ticks], fresh[ticks:]]
@@ -152,15 +158,21 @@
     for block in range(channels // LANES):
         lanes = slice(block * LANES, (block + 1) * LANES)
         normed = values[:, lanes] * scale * gains_ref[:, lanes]
-        narrow = normed.astype(jnp.bfloat16)
-        spread = jnp.concatenate(
-            [
-                jnp.where(lane_group == part, narrow, jnp.zeros_like(narrow))
-                for part in range(PER_BLOCK)
-            ],
-            axis=0,
+        high, low = [
+            jnp.concatenate(
+                [
+                    jnp.where(lane_group == part, half, jnp.zeros_like(half))
+                    for part in range(PER_BLOCK)
+                ],
+                axis=0,
+            )
+            for half in halves(normed)
+        ]
+        mixed = (
+            jnp.dot(blocks_ref[block, 0], high, preferred_element_type=jnp.float32)
+            + jnp.dot(blocks_ref[block, 1], high, preferred_element_type=jnp.float32)
+            + jnp.dot(blocks_ref[block, 0], low, preferred_element_type=jnp.float32)
         )
-        mixed = jnp.dot(blocks_ref[block], spread, preferred_element_type=jnp.float32)
         gated_buf[:, lanes] = (normed * mixed).astype(jnp.bfloat16)
     for apart in reversed(range(count)):
         start = pl.multiple_of((place ^ apart) * channels, channels)
@@ -180,7 +192,7 @@
         in_specs=[IN_VMEM] * (3 + count) + [IN_PLACE] * len(after),
         out_specs=[IN_VMEM] * count,
         scratch_shapes=[pltpu.VMEM((seq, channels), jnp.bfloat16)],
-        compiler_params=pltpu.CompilerParams(vmem_limit_bytes=12 * 2**20),
+        compiler_params=pltpu.CompilerParams(vmem_limit_bytes=16 * 2**20),
         cost_estimate=pl.CostEstimate(
             flops=1 * 2 * seq * channels * channels * count,
             transcendentals=0,
@@ -334,8 +346,9 @@
     down, up = 0, 1
     entering = [down_state[0], up_state[0]]
     sums = squares_of(*entering)
+    entering[up], sums = lax.optimization_barrier((entering[up], sums))
+    entering[up] = send(entering[up], lambda k, z: (mirrored(k), z))
     squares = [spread(sums, lambda k: k), spread(sums, mirrored)]
-    entering[up] = send(entering[up], lambda k, z: (mirrored(k), z))
     blocks, weight, fresh = prepare(
         conv_filters[0], layer_proj[0], dna_tokens, entry_order, embedding
     )

time: 147 us -> 148 us (level)
  Pallas kernels: 19.8 us -> 26.3 us
  waiting for transfers between devices: 63.2 us -> 57.8 us
    pallas_call x6, Pallas kernels: 11.7 us -> 18.3 us  [layer_partials(): pl.pallas_call(functools.partial(layer_kernel, count, line), out_shape=[j...]
    ppermute x44, waiting for transfers between devices: 63.2 us -> 57.8 us  [send(): return lax.ppermute(values, ('pipe', 'tensor'), pairs)]
  transfers between devices with their start and end apart: 44 -> 44, of which waited for: 17 -> 18; matrix products, arithmetic and copies ran while one was open for 0% -> 0% of each run, Pallas kernels for 11% -> 14%
where the time goes in v5:
time: 148 us
  starting transfers between devices  63 us (43%)
  waiting for transfers between devices  57.8 us (39%)
  Pallas kernels  26.3 us (18%)
    ppermute x44, starting transfers between devices, send(): return lax.ppermute(values, ('pipe', 'tensor'), pairs)  63 us
    ppermute x44, waiting for transfers between devices, send(): return lax.ppermute(values, ('pipe', 'tensor'), pairs)  57.8 us
    pallas_call x6, Pallas kernels, layer_partials(): pl.pallas_call(functools.partial(layer_kernel, count, line), out_shape=[j...  18.3 us
    pallas_call x1, Pallas kernels, prepare(): pl.pallas_call(functools.partial(prepare_kernel, ticks), out_shape=[jax.S...  3.79 us
  transfers between devices with their start and end apart: 44, of which 18 were waited for; matrix products, arithmetic and copies ran while one was open for 0% of the time, Pallas kernels for 14%

profile of v5, /device:TPU:0, one launch (start us, length us, event | category | flops | bytes accessed | tf_op | source)
XLA Modules:
  0.0 147.9 jit_solution(16098207496741618394)
XLA Ops:
  1.2 3.4 %collective-permute-start.3 = (bf16[128,1024]{1,0:T(8,128)(2,1)}, bf16[128,1024]{1,0:T(8,128)(2,1)S(1)}, u32[]{:S(2)}, u32[]{:S(2)}) collective-permute-start(bf16[128,1024]{1,0:T(8,128)(2,1)} %bitcast.9), channel_id=1, source_target_pairs={{0,28},{1,29},{2,30},{3,31},{4,24},{5,25},{6,26},{7,27},{8,20},{9,... | collective-permute-start | bytes 786440 | tf_op jit(solution)/shard_map/ppermute | solution.py:290
  4.6 3.8 %collective-permute-start.6 = (f32[2,128]{1,0:T(2,128)S(1)}, f32[2,128]{1,0:T(2,128)S(1)}, u32[]{:S(2)}, u32[]{:S(2)}) collective-permute-start(f32[2,128]{1,0:T(2,128)S(1)} %squares.1), channel_id=1, source_target_pairs={{0,31},{1,30},{2,29},{3,28},{4,27},{5,26},{6,25},{7,24},{8,23},{9,... | collective-permute-start | bytes 3080 | tf_op jit(solution)/shard_map/ppermute | solution.py:290
  10.3 3.8 %prepare.1 = (bf16[8,2,128,1024]{3,2,1,0:T(8,128)(2,1)S(1)}, bf16[1024,4096]{1,0:T(8,128)(2,1)S(1)}, bf16[128,1024]{1,0:T(8,128)(2,1)S(1)}, bf16[128,1024]{1,0:T...) custom-call(s32[2,8]{1,0:T(2,128)} %order_hbm.1, f32[64,128]{1,0:T(8,128)} %bitcast.10, ...), custom_call_target="tpu_custom_call" | custom-call | tf_op jit(solution)/shard_map/prepare/pallas_call | solution.py:85
  14.2 3.0 %layer.6 = (f32[128,1024]{1,0:T(8,128)S(1)}, bf16[128,1024]{1,0:T(8,128)(2,1)S(1)}, f32[128,1024]{1,0:T(8,128)S(1)}, bf16[128,1024]{1,0:T(8,128)(2,1)S(1)}) custom-call(bf16[128,1024]{1,0:T(8,128)(2,1)S(1)} %collective-permute-done.3.x_ref, f32[1,1024]{1,0:T(1,128)S(1)} %copy-done.1, bf16[8,2,128,1024]{3,2,1,0:T(8,128)(2,1)S(1)} %get-tuple-element.68.blocks_ref, ...), custom_call_target="tpu_custom_call" | custom-call | flops 1073741824 | bytes 8388608 | tf_op jit(solution)/shard_map/layer/pallas_call | solution.py:189
  18.8 3.3 %collective-permute-start.2 = (f32[2,128]{1,0:T(2,128)S(1)}, f32[2,128]{1,0:T(2,128)S(1)}, u32[]{:S(2)}, u32[]{:S(2)}) collective-permute-start(f32[2,128]{1,0:T(2,128)S(1)} %squares.1), channel_id=1, source_target_pairs={{0,3},{1,2},{2,1},{3,0},{4,7},{5,6},{6,5},{7,4},{8,11},{9,10},{10,... | collective-permute-start | bytes 3080 | tf_op jit(solution)/shard_map/ppermute | solution.py:290
  23.2 3.0 %collective-permute-done.7 = bf16[128,1024]{1,0:T(8,128)(2,1)S(1)} collective-permute-done((bf16[128,1024]{1,0:T(8,128)(2,1)S(1)}, bf16[128,1024]{1,0:T(8,128)(2,1)S(1)}, u32[]{:S(2)}, u32[]{:S(2)}) %collective-permute-start.7) | collective-permute-done | bytes 262176 | tf_op jit(solution)/shard_map/ppermute | solution.py:290
  30.3 3.0 %layer.7 = (f32[128,1024]{1,0:T(8,128)S(1)}, bf16[128,1024]{1,0:T(8,128)(2,1)S(1)}, f32[128,1024]{1,0:T(8,128)S(1)}, bf16[128,1024]{1,0:T(8,128)(2,1)S(1)}) custom-call(bf16[128,1024]{1,0:T(8,128)(2,1)S(1)} %bitcast.5, f32[1,1024]{1,0:T(1,128)S(1)} %copy-done.1, bf16[8,2,128,1024]{3,2,1,0:T(8,128)(2,1)S(1)} %get-tuple-element.68.blocks_ref, ...), custom_call_target="tpu_custom_call" | custom-call | flops 1073741824 | bytes 8388608 | tf_op jit(solution)/shard_map/layer/pallas_call | solution.py:189
  34.8 6.3 %collective-permute-done.12.refs_1_ = bf16[128,1024]{1,0:T(8,128)(2,1)S(1)} collective-permute-done((bf16[128,1024]{1,0:T(8,128)(2,1)S(1)}, bf16[128,1024]{1,0:T(8,128)(2,1)S(1)}, u32[]{:S(2)}, u32[]{:S(2)}) %collective-permute-start.12) | collective-permute-done | bytes 262176 | tf_op jit(solution)/shard_map/ppermute | solution.py:290
  41.7 4.4 %collective-permute-start.16 = (f32[1,128]{1,0:T(1,128)S(1)}, f32[1,128]{1,0:T(1,128)S(1)}, u32[]{:S(2)}, u32[]{:S(2)}) collective-permute-start(f32[1,128]{1,0:T(1,128)S(1)} %get-tuple-element.86), channel_id=1, source_target_pairs={{0,7},{1,6},{2,5},{3,4},{4,11},{5,10},{6,9},{7,8},{8,15},{9,14},{1... | collective-permute-start | bytes 1544 | tf_op jit(solution)/shard_map/ppermute | solution.py:290
  51.8 3.0 %layer.8 = (f32[128,1024]{1,0:T(8,128)S(1)}, bf16[128,1024]{1,0:T(8,128)(2,1)S(1)}, f32[128,1024]{1,0:T(8,128)S(1)}, bf16[128,1024]{1,0:T(8,128)(2,1)S(1)}) custom-call(bf16[128,1024]{1,0:T(8,128)(2,1)S(1)} %collective-permute-done.13.x_ref, f32[1,1024]{1,0:T(1,128)S(1)} %copy-done.1, bf16[8,2,128,1024]{3,2,1,0:T(8,128)(2,1)S(1)} %get-tuple-element.68.blocks_ref, ...), custom_call_target="tpu_custom_call" | custom-call | flops 1073741824 | bytes 8388608 | tf_op jit(solution)/shard_map/layer/pallas_call | solution.py:189
  56.8 5.2 %collective-permute-done.10.refs_1_ = bf16[128,1024]{1,0:T(8,128)(2,1)S(1)} collective-permute-done((bf16[128,1024]{1,0:T(8,128)(2,1)S(1)}, bf16[128,1024]{1,0:T(8,128)(2,1)S(1)}, u32[]{:S(2)}, u32[]{:S(2)}) %collective-permute-start.10) | collective-permute-done | bytes 262176 | tf_op jit(solution)/shard_map/ppermute | solution.py:290
  64.4 3.3 %collective-permute-start.21 = (f32[1,128]{1,0:T(1,128)S(1)}, f32[1,128]{1,0:T(1,128)S(1)}, u32[]{:S(2)}, u32[]{:S(2)}) collective-permute-start(f32[1,128]{1,0:T(1,128)S(1)} %get-tuple-element.92), channel_id=1, source_target_pairs={{0,7},{1,6},{2,5},{3,4},{4,11},{5,10},{6,9},{7,8},{8,15},{9,14},{1... | collective-permute-start | bytes 1544 | tf_op jit(solution)/shard_map/ppermute | solution.py:290
  67.7 3.1 %collective-permute-start.19 = (f32[1,128]{1,0:T(1,128)S(1)}, f32[1,128]{1,0:T(1,128)S(1)}, u32[]{:S(2)}, u32[]{:S(2)}) collective-permute-start(f32[1,128]{1,0:T(1,128)S(1)} %get-tuple-element.92), channel_id=1, source_target_pairs={{0,5},{1,4},{2,7},{3,6},{4,9},{5,8},{6,11},{7,10},{8,13},{9,12},{1... | collective-permute-start | bytes 1544 | tf_op jit(solution)/shard_map/ppermute | solution.py:290
  71.0 2.8 %collective-permute-start.30 = (bf16[128,1024]{1,0:T(8,128)(2,1)S(1)}, bf16[128,1024]{1,0:T(8,128)(2,1)S(1)}, u32[]{:S(2)}, u32[]{:S(2)}) collective-permute-start(bf16[128,1024]{1,0:T(8,128)(2,1)S(1)} %add_convert_fusion.3.refs_3_), channel_id=1, source_target_pairs={{0,2},{1,3},{2,0},{3,1},{4,6},{5,7},{6,4},{7,5},{8,10},{9,11},{10,... | collective-permute-start | bytes 786440 | tf_op jit(solution)/shard_map/ppermute | solution.py:290
  73.8 3.1 %layer.9 = (f32[128,1024]{1,0:T(8,128)S(1)}, bf16[128,1024]{1,0:T(8,128)(2,1)S(1)}, f32[128,1024]{1,0:T(8,128)S(1)}, bf16[128,1024]{1,0:T(8,128)(2,1)S(1)}) custom-call(bf16[128,1024]{1,0:T(8,128)(2,1)S(1)} %collective-permute-done.18.x_ref, f32[1,1024]{1,0:T(1,128)S(1)} %copy-done.1, bf16[8,2,128,1024]{3,2,1,0:T(8,128)(2,1)S(1)} %get-tuple-element.68.blocks_ref, ...), custom_call_target="tpu_custom_call" | custom-call | flops 1073741824 | bytes 8388608 | tf_op jit(solution)/shard_map/layer/pallas_call | solution.py:189
  77.2 8.6 %collective-permute-done.31.refs_1_ = bf16[128,1024]{1,0:T(8,128)(2,1)S(1)} collective-permute-done((bf16[128,1024]{1,0:T(8,128)(2,1)S(1)}, bf16[128,1024]{1,0:T(8,128)(2,1)S(1)}, u32[]{:S(2)}, u32[]{:S(2)}) %collective-permute-start.31) | collective-permute-done | bytes 262176 | tf_op jit(solution)/shard_map/ppermute | solution.py:290
  86.3 3.5 %collective-permute-start.35 = (f32[1,128]{1,0:T(1,128)S(1)}, f32[1,128]{1,0:T(1,128)S(1)}, u32[]{:S(2)}, u32[]{:S(2)}) collective-permute-start(f32[1,128]{1,0:T(1,128)S(1)} %get-tuple-element.109), channel_id=1, source_target_pairs={{0,7},{1,6},{2,5},{3,4},{4,11},{5,10},{6,9},{7,8},{8,15},{9,14},{1... | collective-permute-start | bytes 1544 | tf_op jit(solution)/shard_map/ppermute | solution.py:290
  95.5 3.0 %layer.10 = (f32[128,1024]{1,0:T(8,128)S(1)}, bf16[128,1024]{1,0:T(8,128)(2,1)S(1)}, f32[128,1024]{1,0:T(8,128)S(1)}, bf16[128,1024]{1,0:T(8,128)(2,1)S(1)}) custom-call(bf16[128,1024]{1,0:T(8,128)(2,1)S(1)} %collective-permute-done.32.x_ref, f32[1,1024]{1,0:T(1,128)S(1)} %copy-done.1, bf16[8,2,128,1024]{3,2,1,0:T(8,128)(2,1)S(1)} %get-tuple-element.68.blocks_ref, ...), custom_call_target="tpu_custom_call" | custom-call | flops 1073741824 | bytes 8388608 | tf_op jit(solution)/shard_map/layer/pallas_call | solution.py:189
  99.1 6.9 %collective-permute-done.25.refs_1_ = bf16[128,1024]{1,0:T(8,128)(2,1)S(1)} collective-permute-done((bf16[128,1024]{1,0:T(8,128)(2,1)S(1)}, bf16[128,1024]{1,0:T(8,128)(2,1)S(1)}, u32[]{:S(2)}, u32[]{:S(2)}) %collective-permute-start.25) | collective-permute-done | bytes 262176 | tf_op jit(solution)/shard_map/ppermute | solution.py:290
  107.6 3.8 %collective-permute-start.29 = (f32[1,128]{1,0:T(1,128)S(1)}, f32[1,128]{1,0:T(1,128)S(1)}, u32[]{:S(2)}, u32[]{:S(2)}) collective-permute-start(f32[1,128]{1,0:T(1,128)S(1)} %get-tuple-element.104), channel_id=1, source_target_pairs={{0,7},{1,6},{2,5},{3,4},{4,11},{5,10},{6,9},{7,8},{8,15},{9,14},{1... | collective-permute-start | bytes 1544 | tf_op jit(solution)/shard_map/ppermute | solution.py:290
  117.0 3.0 %layer.11 = (f32[128,1024]{1,0:T(8,128)S(1)}, bf16[128,1024]{1,0:T(8,128)(2,1)S(1)}, f32[128,1024]{1,0:T(8,128)S(1)}, bf16[128,1024]{1,0:T(8,128)(2,1)S(1)}) custom-call(bf16[128,1024]{1,0:T(8,128)(2,1)S(1)} %collective-permute-done.26.x_ref, f32[1,1024]{1,0:T(1,128)S(1)} %copy-done.1, bf16[8,2,128,1024]{3,2,1,0:T(8,128)(2,1)S(1)} %get-tuple-element.68.blocks_ref, ...), custom_call_target="tpu_custom_call" | custom-call | flops 1073741824 | bytes 8388608 | tf_op jit(solution)/shard_map/layer/pallas_call | solution.py:189
  121.2 6.7 %collective-permute-done.39.refs_1_ = bf16[128,1024]{1,0:T(8,128)(2,1)S(1)} collective-permute-done((bf16[128,1024]{1,0:T(8,128)(2,1)S(1)}, bf16[128,1024]{1,0:T(8,128)(2,1)S(1)}, u32[]{:S(2)}, u32[]{:S(2)}) %collective-permute-start.39) | collective-permute-done | bytes 262176 | tf_op jit(solution)/shard_map/ppermute | solution.py:290
  128.9 3.7 %collective-permute-done.37 = bf16[128,1024]{1,0:T(8,128)(2,1)S(1)} collective-permute-done((bf16[128,1024]{1,0:T(8,128)(2,1)S(1)}, bf16[128,1024]{1,0:T(8,128)(2,1)S(1)}, u32[]{:S(2)}, u32[]{:S(2)}) %collective-permute-start.37) | collective-permute-done | bytes 262176 | tf_op jit(solution)/shard_map/ppermute | solution.py:290
  136.1 10.5 %collective-permute-done.41.refs_0_ = bf16[128,1024]{1,0:T(8,128)(2,1)S(1)} collective-permute-done((bf16[128,1024]{1,0:T(8,128)(2,1)S(1)}, bf16[128,1024]{1,0:T(8,128)(2,1)S(1)}, u32[]{:S(2)}, u32[]{:S(2)}) %collective-permute-start.41) | collective-permute-done | bytes 262176 | tf_op jit(solution)/shard_map/ppermute | solution.py:290
  (88 shorter events, 43.0 us)
Async XLA Ops:
  1.2 12.9 %collective-permute-start.3 = (bf16[128,1024]{1,0:T(8,128)(2,1)}, bf16[128,1024]{1,0:T(8,128)(2,1)S(1)}, u32[]{:S(2)}, u32[]{:S(2)}) collective-permute-start(bf16[128,1024]{1,0:T(8,128)(2,1)} %bitcast.9), channel_id=1, source_target_pairs={{0,28},{1,29},{2,30},{3,31},{4,24},{5,25},{6,26},{7,27},{8,20},{9,... | collective-permute-start | bytes 786440 | tf_op jit(solution)/shard_map/ppermute | solution.py:290
  4.6 9.5 %collective-permute-start.6 = (f32[2,128]{1,0:T(2,128)S(1)}, f32[2,128]{1,0:T(2,128)S(1)}, u32[]{:S(2)}, u32[]{:S(2)}) collective-permute-start(f32[2,128]{1,0:T(2,128)S(1)} %squares.1), channel_id=1, source_target_pairs={{0,31},{1,30},{2,29},{3,28},{4,27},{5,26},{6,25},{7,24},{8,23},{9,... | collective-permute-start | bytes 3080 | tf_op jit(solution)/shard_map/ppermute | solution.py:290
  18.8 11.5 %collective-permute-start.2 = (f32[2,128]{1,0:T(2,128)S(1)}, f32[2,128]{1,0:T(2,128)S(1)}, u32[]{:S(2)}, u32[]{:S(2)}) collective-permute-start(f32[2,128]{1,0:T(2,128)S(1)} %squares.1), channel_id=1, source_target_pairs={{0,3},{1,2},{2,1},{3,0},{4,7},{5,6},{6,5},{7,4},{8,11},{9,10},{10,... | collective-permute-start | bytes 3080 | tf_op jit(solution)/shard_map/ppermute | solution.py:290
  26.3 14.9 %collective-permute-start.12 = (bf16[128,1024]{1,0:T(8,128)(2,1)S(1)}, bf16[128,1024]{1,0:T(8,128)(2,1)S(1)}, u32[]{:S(2)}, u32[]{:S(2)}) collective-permute-start(bf16[128,1024]{1,0:T(8,128)(2,1)S(1)} %get-tuple-element.84), channel_id=1, source_target_pairs={{0,1},{1,0},{2,3},{3,2},{4,5},{5,4},{6,7},{7,6},{8,9},{9,8},{10,11... | collective-permute-start | bytes 786440 | tf_op jit(solution)/shard_map/ppermute | solution.py:290
  27.8 13.3 %collective-permute-start.11 = (bf16[128,1024]{1,0:T(8,128)(2,1)S(1)}, bf16[128,1024]{1,0:T(8,128)(2,1)S(1)}, u32[]{:S(2)}, u32[]{:S(2)}) collective-permute-start(bf16[128,1024]{1,0:T(8,128)(2,1)S(1)} %add_convert_fusion.5.refs_3_), channel_id=1, source_target_pairs={{0,2},{1,3},{2,0},{3,1},{4,6},{5,7},{6,4},{7,5},{8,10},{9,11},{10,... | collective-permute-start | bytes 786440 | tf_op jit(solution)/shard_map/ppermute | solution.py:290
  33.4 14.2 %collective-permute-start.8 = (bf16[128,1024]{1,0:T(8,128)(2,1)S(1)}, bf16[128,1024]{1,0:T(8,128)(2,1)S(1)}, u32[]{:S(2)}, u32[]{:S(2)}) collective-permute-start(bf16[128,1024]{1,0:T(8,128)(2,1)S(1)} %get-tuple-element.79), channel_id=1, source_target_pairs={{0,1},{1,0},{2,3},{3,2},{4,5},{5,4},{6,7},{7,6},{8,9},{9,8},{10,11... | collective-permute-start | bytes 786440 | tf_op jit(solution)/shard_map/ppermute | solution.py:290
  41.6 10.2 %collective-permute-start.13 = (bf16[128,1024]{1,0:T(8,128)(2,1)S(1)}, bf16[128,1024]{1,0:T(8,128)(2,1)S(1)}, u32[]{:S(2)}, u32[]{:S(2)}) collective-permute-start(bf16[128,1024]{1,0:T(8,128)(2,1)S(1)} %get-tuple-element.85), channel_id=1, source_target_pairs={{0,4},{1,5},{2,6},{3,7},{4,8},{5,9},{6,10},{7,11},{8,12},{9,13},{1... | collective-permute-start | bytes 786440 | tf_op jit(solution)/shard_map/ppermute | solution.py:290
  47.6 14.4 %collective-permute-start.10 = (bf16[128,1024]{1,0:T(8,128)(2,1)S(1)}, bf16[128,1024]{1,0:T(8,128)(2,1)S(1)}, u32[]{:S(2)}, u32[]{:S(2)}) collective-permute-start(bf16[128,1024]{1,0:T(8,128)(2,1)S(1)} %get-tuple-element.81), channel_id=1, source_target_pairs={{0,1},{1,0},{2,3},{3,2},{4,5},{5,4},{6,7},{7,6},{8,9},{9,8},{10,11... | collective-permute-start | bytes 786440 | tf_op jit(solution)/shard_map/ppermute | solution.py:290
  49.5 14.3 %collective-permute-start.9 = (bf16[128,1024]{1,0:T(8,128)(2,1)S(1)}, bf16[128,1024]{1,0:T(8,128)(2,1)S(1)}, u32[]{:S(2)}, u32[]{:S(2)}) collective-permute-start(bf16[128,1024]{1,0:T(8,128)(2,1)S(1)} %add_convert_fusion.4.refs_3_), channel_id=1, source_target_pairs={{0,2},{1,3},{2,0},{3,1},{4,6},{5,7},{6,4},{7,5},{8,10},{9,11},{10,... | collective-permute-start | bytes 786440 | tf_op jit(solution)/shard_map/ppermute | solution.py:290
  55.3 15.5 %collective-permute-start.22 = (bf16[128,1024]{1,0:T(8,128)(2,1)S(1)}, bf16[128,1024]{1,0:T(8,128)(2,1)S(1)}, u32[]{:S(2)}, u32[]{:S(2)}) collective-permute-start(bf16[128,1024]{1,0:T(8,128)(2,1)S(1)} %get-tuple-element.95), channel_id=1, source_target_pairs={{0,1},{1,0},{2,3},{3,2},{4,5},{5,4},{6,7},{7,6},{8,9},{9,8},{10,11... | collective-permute-start | bytes 786440 | tf_op jit(solution)/shard_map/ppermute | solution.py:290
  64.3 9.5 %collective-permute-start.18 = (bf16[128,1024]{1,0:T(8,128)(2,1)S(1)}, bf16[128,1024]{1,0:T(8,128)(2,1)S(1)}, u32[]{:S(2)}, u32[]{:S(2)}) collective-permute-start(bf16[128,1024]{1,0:T(8,128)(2,1)S(1)} %get-tuple-element.90), channel_id=1, source_target_pairs={{0,4},{1,5},{2,6},{3,7},{4,8},{5,9},{6,10},{7,11},{8,12},{9,13},{1... | collective-permute-start | bytes 786440 | tf_op jit(solution)/shard_map/ppermute | solution.py:290
  70.9 14.9 %collective-permute-start.31 = (bf16[128,1024]{1,0:T(8,128)(2,1)S(1)}, bf16[128,1024]{1,0:T(8,128)(2,1)S(1)}, u32[]{:S(2)}, u32[]{:S(2)}) collective-permute-start(bf16[128,1024]{1,0:T(8,128)(2,1)S(1)} %get-tuple-element.107), channel_id=1, source_target_pairs={{0,1},{1,0},{2,3},{3,2},{4,5},{5,4},{6,7},{7,6},{8,9},{9,8},{10,11... | collective-permute-start | bytes 786440 | tf_op jit(solution)/shard_map/ppermute | solution.py:290
  71.0 14.7 %collective-permute-start.30 = (bf16[128,1024]{1,0:T(8,128)(2,1)S(1)}, bf16[128,1024]{1,0:T(8,128)(2,1)S(1)}, u32[]{:S(2)}, u32[]{:S(2)}) collective-permute-start(bf16[128,1024]{1,0:T(8,128)(2,1)S(1)} %add_convert_fusion.3.refs_3_), channel_id=1, source_target_pairs={{0,2},{1,3},{2,0},{3,1},{4,6},{5,7},{6,4},{7,5},{8,10},{9,11},{10,... | collective-permute-start | bytes 786440 | tf_op jit(solution)/shard_map/ppermute | solution.py:290
  76.9 14.4 %collective-permute-start.23 = (bf16[128,1024]{1,0:T(8,128)(2,1)S(1)}, bf16[128,1024]{1,0:T(8,128)(2,1)S(1)}, u32[]{:S(2)}, u32[]{:S(2)}) collective-permute-start(bf16[128,1024]{1,0:T(8,128)(2,1)S(1)} %get-tuple-element.100), channel_id=1, source_target_pairs={{0,1},{1,0},{2,3},{3,2},{4,5},{5,4},{6,7},{7,6},{8,9},{9,8},{10,11... | collective-permute-start | bytes 786440 | tf_op jit(solution)/shard_map/ppermute | solution.py:290
  91.4 14.6 %collective-permute-start.25 = (bf16[128,1024]{1,0:T(8,128)(2,1)S(1)}, bf16[128,1024]{1,0:T(8,128)(2,1)S(1)}, u32[]{:S(2)}, u32[]{:S(2)}) collective-permute-start(bf16[128,1024]{1,0:T(8,128)(2,1)S(1)} %get-tuple-element.102), channel_id=1, source_target_pairs={{0,1},{1,0},{2,3},{3,2},{4,5},{5,4},{6,7},{7,6},{8,9},{9,8},{10,11... | collective-permute-start | bytes 786440 | tf_op jit(solution)/shard_map/ppermute | solution.py:290
  92.9 14.2 %collective-permute-start.24 = (bf16[128,1024]{1,0:T(8,128)(2,1)S(1)}, bf16[128,1024]{1,0:T(8,128)(2,1)S(1)}, u32[]{:S(2)}, u32[]{:S(2)}) collective-permute-start(bf16[128,1024]{1,0:T(8,128)(2,1)S(1)} %add_convert_fusion.2.refs_3_), channel_id=1, source_target_pairs={{0,2},{1,3},{2,0},{3,1},{4,6},{5,7},{6,4},{7,5},{8,10},{9,11},{10,... | collective-permute-start | bytes 786440 | tf_op jit(solution)/shard_map/ppermute | solution.py:290
  98.5 14.6 %collective-permute-start.36 = (bf16[128,1024]{1,0:T(8,128)(2,1)S(1)}, bf16[128,1024]{1,0:T(8,128)(2,1)S(1)}, u32[]{:S(2)}, u32[]{:S(2)}) collective-permute-start(bf16[128,1024]{1,0:T(8,128)(2,1)S(1)} %get-tuple-element.112), channel_id=1, source_target_pairs={{0,1},{1,0},{2,3},{3,2},{4,5},{5,4},{6,7},{7,6},{8,9},{9,8},{10,11... | collective-permute-start | bytes 786440 | tf_op jit(solution)/shard_map/ppermute | solution.py:290
  107.5 9.5 %collective-permute-start.26 = (bf16[128,1024]{1,0:T(8,128)(2,1)S(1)}, bf16[128,1024]{1,0:T(8,128)(2,1)S(1)}, u32[]{:S(2)}, u32[]{:S(2)}) collective-permute-start(bf16[128,1024]{1,0:T(8,128)(2,1)S(1)} %get-tuple-element.103), channel_id=1, source_target_pairs={{0,4},{1,5},{2,6},{3,7},{4,8},{5,9},{6,10},{7,11},{8,12},{9,13},{1... | collective-permute-start | bytes 786440 | tf_op jit(solution)/shard_map/ppermute | solution.py:290
  113.2 14.7 %collective-permute-start.39 = (bf16[128,1024]{1,0:T(8,128)(2,1)S(1)}, bf16[128,1024]{1,0:T(8,128)(2,1)S(1)}, u32[]{:S(2)}, u32[]{:S(2)}) collective-permute-start(bf16[128,1024]{1,0:T(8,128)(2,1)S(1)} %get-tuple-element.121), channel_id=1, source_target_pairs={{0,1},{1,0},{2,3},{3,2},{4,5},{5,4},{6,7},{7,6},{8,9},{9,8},{10,11... | collective-permute-start | bytes 786440 | tf_op jit(solution)/shard_map/ppermute | solution.py:290
  114.2 14.0 %collective-permute-start.38 = (bf16[128,1024]{1,0:T(8,128)(2,1)S(1)}, bf16[128,1024]{1,0:T(8,128)(2,1)S(1)}, u32[]{:S(2)}, u32[]{:S(2)}) collective-permute-start(bf16[128,1024]{1,0:T(8,128)(2,1)S(1)} %add_convert_fusion.1.refs_3_), channel_id=1, source_target_pairs={{0,2},{1,3},{2,0},{3,1},{4,6},{5,7},{6,4},{7,5},{8,10},{9,11},{10,... | collective-permute-start | bytes 786440 | tf_op jit(solution)/shard_map/ppermute | solution.py:290
  120.6 12.0 %collective-permute-start.37 = (bf16[128,1024]{1,0:T(8,128)(2,1)S(1)}, bf16[128,1024]{1,0:T(8,128)(2,1)S(1)}, u32[]{:S(2)}, u32[]{:S(2)}) collective-permute-start(bf16[128,1024]{1,0:T(8,128)(2,1)S(1)} %get-tuple-element.119), channel_id=1, source_target_pairs={{0,1},{1,0},{2,3},{3,2},{4,5},{5,4},{6,7},{7,6},{8,9},{9,8},{10,11... | collective-permute-start | bytes 786440 | tf_op jit(solution)/shard_map/ppermute | solution.py:290
  132.7 13.8 %collective-permute-start.41 = (bf16[128,1024]{1,0:T(8,128)(2,1)S(1)}, bf16[128,1024]{1,0:T(8,128)(2,1)S(1)}, u32[]{:S(2)}, u32[]{:S(2)}) collective-permute-start(bf16[128,1024]{1,0:T(8,128)(2,1)S(1)} %add_convert_fusion), channel_id=1, source_target_pairs={{0,2},{1,3},{2,0},{3,1},{4,6},{5,7},{6,4},{7,5},{8,10},{9,11},{10,... | collective-permute-start | bytes 786440 | tf_op jit(solution)/shard_map/ppermute | solution.py:290
  134.5 12.0 %collective-permute-start.42 = (bf16[128,1024]{1,0:T(8,128)(2,1)S(1)}, bf16[128,1024]{1,0:T(8,128)(2,1)S(1)}, u32[]{:S(2)}, u32[]{:S(2)}) collective-permute-start(bf16[128,1024]{1,0:T(8,128)(2,1)S(1)} %get-tuple-element.125), channel_id=1, source_target_pairs={{0,1},{1,0},{2,3},{3,2},{4,5},{5,4},{6,7},{7,6},{8,9},{9,8},{10,11... | collective-permute-start | bytes 786440 | tf_op jit(solution)/shard_map/ppermute | solution.py:290
  136.0 10.5 %collective-permute-start.43 = (bf16[128,1024]{1,0:T(8,128)(2,1)S(1)}, bf16[128,1024]{1,0:T(8,128)(2,1)S(1)}, u32[]{:S(2)}, u32[]{:S(2)}) collective-permute-start(bf16[128,1024]{1,0:T(8,128)(2,1)S(1)} %end.1), channel_id=1, source_target_pairs={{0,28},{1,29},{2,30},{3,31},{4,24},{5,25},{6,26},{7,27},{8,20},{9,... | collective-permute-start | bytes 786440 | tf_op jit(solution)/shard_map/ppermute | solution.py:290
  (22 other events, 167.1 us)

commit v6 on v5

--- a/solution.py
+++ b/solution.py
@@ -168,11 +168,11 @@
             )
             for half in halves(normed)
         ]
-        mixed = (
-            jnp.dot(blocks_ref[block, 0], high, preferred_element_type=jnp.float32)
-            + jnp.dot(blocks_ref[block, 1], high, preferred_element_type=jnp.float32)
-            + jnp.dot(blocks_ref[block, 0], low, preferred_element_type=jnp.float32)
+        filters = blocks_ref[block].reshape(2 * seq, PER_BLOCK * seq)
+        parts = jnp.dot(
+            filters, jnp.concatenate([high, low], axis=1), preferred_element_type=jnp.float32
         )
+        mixed = parts[:seq, :LANES] + (parts[seq:, :LANES] + parts[:seq, LANES:])
         gated_buf[:, lanes] = (normed * mixed).astype(jnp.bfloat16)
     for apart in reversed(range(count)):
         start = pl.multiple_of((place ^ apart) * channels, channels)

time: 148 us -> 147 us (level)
  Pallas kernels: 26.3 us -> 23.1 us
  waiting for transfers between devices: 57.8 us -> 60.2 us
    pallas_call x6, Pallas kernels: 18.3 us -> 15.1 us  [layer_partials(): pl.pallas_call(functools.partial(layer_kernel, count, line), out_shape=[j...]
    ppermute x44, waiting for transfers between devices: 57.8 us -> 60.2 us  [send(): return lax.ppermute(values, ('pipe', 'tensor'), pairs)]
  transfers between devices with their start and end apart: 44 -> 44, of which waited for: 18 -> 18; matrix products, arithmetic and copies ran while one was open for 0% -> 0% of each run, Pallas kernels for 14% -> 12%
where the time goes in v6:
time: 147 us
  starting transfers between devices  63.2 us (43%)
  waiting for transfers between devices  60.2 us (41%)
  Pallas kernels  23.1 us (16%)
    ppermute x44, starting transfers between devices, send(): return lax.ppermute(values, ('pipe', 'tensor'), pairs)  63.2 us
    ppermute x44, waiting for transfers between devices, send(): return lax.ppermute(values, ('pipe', 'tensor'), pairs)  60.2 us
    pallas_call x6, Pallas kernels, layer_partials(): pl.pallas_call(functools.partial(layer_kernel, count, line), out_shape=[j...  15.1 us
    pallas_call x1, Pallas kernels, prepare(): pl.pallas_call(functools.partial(prepare_kernel, ticks), out_shape=[jax.S...  3.79 us
  transfers between devices with their start and end apart: 44, of which 18 were waited for; matrix products, arithmetic and copies ran while one was open for 0% of the time, Pallas kernels for 12%

profile of v6, /device:TPU:0, one launch (start us, length us, event | category | flops | bytes accessed | tf_op | source)
XLA Modules:
  0.0 147.3 jit_solution(8156491442109960379)
XLA Ops:
  1.2 3.4 %collective-permute-start.3 = (bf16[128,1024]{1,0:T(8,128)(2,1)}, bf16[128,1024]{1,0:T(8,128)(2,1)S(1)}, u32[]{:S(2)}, u32[]{:S(2)}) collective-permute-start(bf16[128,1024]{1,0:T(8,128)(2,1)} %bitcast.9), channel_id=1, source_target_pairs={{0,28},{1,29},{2,30},{3,31},{4,24},{5,25},{6,26},{7,27},{8,20},{9,... | collective-permute-start | bytes 786440 | tf_op jit(solution)/shard_map/ppermute | solution.py:290
  4.6 3.8 %collective-permute-start.6 = (f32[2,128]{1,0:T(2,128)S(1)}, f32[2,128]{1,0:T(2,128)S(1)}, u32[]{:S(2)}, u32[]{:S(2)}) collective-permute-start(f32[2,128]{1,0:T(2,128)S(1)} %squares.1), channel_id=1, source_target_pairs={{0,31},{1,30},{2,29},{3,28},{4,27},{5,26},{6,25},{7,24},{8,23},{9,... | collective-permute-start | bytes 3080 | tf_op jit(solution)/shard_map/ppermute | solution.py:290
  10.3 3.8 %prepare.1 = (bf16[8,2,128,1024]{3,2,1,0:T(8,128)(2,1)S(1)}, bf16[1024,4096]{1,0:T(8,128)(2,1)S(1)}, bf16[128,1024]{1,0:T(8,128)(2,1)S(1)}, bf16[128,1024]{1,0:T...) custom-call(s32[2,8]{1,0:T(2,128)} %order_hbm.1, f32[64,128]{1,0:T(8,128)} %bitcast.10, ...), custom_call_target="tpu_custom_call" | custom-call | tf_op jit(solution)/shard_map/prepare/pallas_call | solution.py:85
  14.2 2.5 %layer.6 = (f32[128,1024]{1,0:T(8,128)S(1)}, bf16[128,1024]{1,0:T(8,128)(2,1)S(1)}, f32[128,1024]{1,0:T(8,128)S(1)}, bf16[128,1024]{1,0:T(8,128)(2,1)S(1)}) custom-call(bf16[128,1024]{1,0:T(8,128)(2,1)S(1)} %collective-permute-done.3.x_ref, f32[1,1024]{1,0:T(1,128)S(1)} %copy-done.1, bf16[8,2,128,1024]{3,2,1,0:T(8,128)(2,1)S(1)} %get-tuple-element.68.blocks_ref, ...), custom_call_target="tpu_custom_call" | custom-call | flops 1073741824 | bytes 8388608 | tf_op jit(solution)/shard_map/layer/pallas_call | solution.py:189
  18.2 3.3 %collective-permute-start.2 = (f32[2,128]{1,0:T(2,128)S(1)}, f32[2,128]{1,0:T(2,128)S(1)}, u32[]{:S(2)}, u32[]{:S(2)}) collective-permute-start(f32[2,128]{1,0:T(2,128)S(1)} %squares.1), channel_id=1, source_target_pairs={{0,3},{1,2},{2,1},{3,0},{4,7},{5,6},{6,5},{7,4},{8,11},{9,10},{10,... | collective-permute-start | bytes 3080 | tf_op jit(solution)/shard_map/ppermute | solution.py:290
  22.6 3.1 %collective-permute-done.7 = bf16[128,1024]{1,0:T(8,128)(2,1)S(1)} collective-permute-done((bf16[128,1024]{1,0:T(8,128)(2,1)S(1)}, bf16[128,1024]{1,0:T(8,128)(2,1)S(1)}, u32[]{:S(2)}, u32[]{:S(2)}) %collective-permute-start.7) | collective-permute-done | bytes 262176 | tf_op jit(solution)/shard_map/ppermute | solution.py:290
  29.8 2.5 %layer.7 = (f32[128,1024]{1,0:T(8,128)S(1)}, bf16[128,1024]{1,0:T(8,128)(2,1)S(1)}, f32[128,1024]{1,0:T(8,128)S(1)}, bf16[128,1024]{1,0:T(8,128)(2,1)S(1)}) custom-call(bf16[128,1024]{1,0:T(8,128)(2,1)S(1)} %bitcast.5, f32[1,1024]{1,0:T(1,128)S(1)} %copy-done.1, bf16[8,2,128,1024]{3,2,1,0:T(8,128)(2,1)S(1)} %get-tuple-element.68.blocks_ref, ...), custom_call_target="tpu_custom_call" | custom-call | flops 1073741824 | bytes 8388608 | tf_op jit(solution)/shard_map/layer/pallas_call | solution.py:189
  33.8 6.9 %collective-permute-done.12.refs_1_ = bf16[128,1024]{1,0:T(8,128)(2,1)S(1)} collective-permute-done((bf16[128,1024]{1,0:T(8,128)(2,1)S(1)}, bf16[128,1024]{1,0:T(8,128)(2,1)S(1)}, u32[]{:S(2)}, u32[]{:S(2)}) %collective-permute-start.12) | collective-permute-done | bytes 262176 | tf_op jit(solution)/shard_map/ppermute | solution.py:290
  41.1 4.4 %collective-permute-start.16 = (f32[1,128]{1,0:T(1,128)S(1)}, f32[1,128]{1,0:T(1,128)S(1)}, u32[]{:S(2)}, u32[]{:S(2)}) collective-permute-start(f32[1,128]{1,0:T(1,128)S(1)} %get-tuple-element.86), channel_id=1, source_target_pairs={{0,7},{1,6},{2,5},{3,4},{4,11},{5,10},{6,9},{7,8},{8,15},{9,14},{1... | collective-permute-start | bytes 1544 | tf_op jit(solution)/shard_map/ppermute | solution.py:290
  51.2 2.5 %layer.8 = (f32[128,1024]{1,0:T(8,128)S(1)}, bf16[128,1024]{1,0:T(8,128)(2,1)S(1)}, f32[128,1024]{1,0:T(8,128)S(1)}, bf16[128,1024]{1,0:T(8,128)(2,1)S(1)}) custom-call(bf16[128,1024]{1,0:T(8,128)(2,1)S(1)} %collective-permute-done.13.x_ref, f32[1,1024]{1,0:T(1,128)S(1)} %copy-done.1, bf16[8,2,128,1024]{3,2,1,0:T(8,128)(2,1)S(1)} %get-tuple-element.68.blocks_ref, ...), custom_call_target="tpu_custom_call" | custom-call | flops 1073741824 | bytes 8388608 | tf_op jit(solution)/shard_map/layer/pallas_call | solution.py:189
  55.8 5.7 %collective-permute-done.10.refs_1_ = bf16[128,1024]{1,0:T(8,128)(2,1)S(1)} collective-permute-done((bf16[128,1024]{1,0:T(8,128)(2,1)S(1)}, bf16[128,1024]{1,0:T(8,128)(2,1)S(1)}, u32[]{:S(2)}, u32[]{:S(2)}) %collective-permute-start.10) | collective-permute-done | bytes 262176 | tf_op jit(solution)/shard_map/ppermute | solution.py:290
  63.8 3.4 %collective-permute-start.21 = (f32[1,128]{1,0:T(1,128)S(1)}, f32[1,128]{1,0:T(1,128)S(1)}, u32[]{:S(2)}, u32[]{:S(2)}) collective-permute-start(f32[1,128]{1,0:T(1,128)S(1)} %get-tuple-element.92), channel_id=1, source_target_pairs={{0,7},{1,6},{2,5},{3,4},{4,11},{5,10},{6,9},{7,8},{8,15},{9,14},{1... | collective-permute-start | bytes 1544 | tf_op jit(solution)/shard_map/ppermute | solution.py:290
  67.2 2.7 %collective-permute-start.19 = (f32[1,128]{1,0:T(1,128)S(1)}, f32[1,128]{1,0:T(1,128)S(1)}, u32[]{:S(2)}, u32[]{:S(2)}) collective-permute-start(f32[1,128]{1,0:T(1,128)S(1)} %get-tuple-element.92), channel_id=1, source_target_pairs={{0,5},{1,4},{2,7},{3,6},{4,9},{5,8},{6,11},{7,10},{8,13},{9,12},{1... | collective-permute-start | bytes 1544 | tf_op jit(solution)/shard_map/ppermute | solution.py:290
  70.4 2.9 %collective-permute-start.30 = (bf16[128,1024]{1,0:T(8,128)(2,1)S(1)}, bf16[128,1024]{1,0:T(8,128)(2,1)S(1)}, u32[]{:S(2)}, u32[]{:S(2)}) collective-permute-start(bf16[128,1024]{1,0:T(8,128)(2,1)S(1)} %add_convert_fusion.3.refs_3_), channel_id=1, source_target_pairs={{0,2},{1,3},{2,0},{3,1},{4,6},{5,7},{6,4},{7,5},{8,10},{9,11},{10,... | collective-permute-start | bytes 786440 | tf_op jit(solution)/shard_map/ppermute | solution.py:290
  73.3 2.5 %layer.9 = (f32[128,1024]{1,0:T(8,128)S(1)}, bf16[128,1024]{1,0:T(8,128)(2,1)S(1)}, f32[128,1024]{1,0:T(8,128)S(1)}, bf16[128,1024]{1,0:T(8,128)(2,1)S(1)}) custom-call(bf16[128,1024]{1,0:T(8,128)(2,1)S(1)} %collective-permute-done.18.x_ref, f32[1,1024]{1,0:T(1,128)S(1)} %copy-done.1, bf16[8,2,128,1024]{3,2,1,0:T(8,128)(2,1)S(1)} %get-tuple-element.68.blocks_ref, ...), custom_call_target="tpu_custom_call" | custom-call | flops 1073741824 | bytes 8388608 | tf_op jit(solution)/shard_map/layer/pallas_call | solution.py:189
  76.1 8.5 %collective-permute-done.31.refs_1_ = bf16[128,1024]{1,0:T(8,128)(2,1)S(1)} collective-permute-done((bf16[128,1024]{1,0:T(8,128)(2,1)S(1)}, bf16[128,1024]{1,0:T(8,128)(2,1)S(1)}, u32[]{:S(2)}, u32[]{:S(2)}) %collective-permute-start.31) | collective-permute-done | bytes 262176 | tf_op jit(solution)/shard_map/ppermute | solution.py:290
  85.5 3.8 %collective-permute-start.35 = (f32[1,128]{1,0:T(1,128)S(1)}, f32[1,128]{1,0:T(1,128)S(1)}, u32[]{:S(2)}, u32[]{:S(2)}) collective-permute-start(f32[1,128]{1,0:T(1,128)S(1)} %get-tuple-element.109), channel_id=1, source_target_pairs={{0,7},{1,6},{2,5},{3,4},{4,11},{5,10},{6,9},{7,8},{8,15},{9,14},{1... | collective-permute-start | bytes 1544 | tf_op jit(solution)/shard_map/ppermute | solution.py:290
  92.1 2.7 %collective-permute-start.24 = (bf16[128,1024]{1,0:T(8,128)(2,1)S(1)}, bf16[128,1024]{1,0:T(8,128)(2,1)S(1)}, u32[]{:S(2)}, u32[]{:S(2)}) collective-permute-start(bf16[128,1024]{1,0:T(8,128)(2,1)S(1)} %add_convert_fusion.2.refs_3_), channel_id=1, source_target_pairs={{0,2},{1,3},{2,0},{3,1},{4,6},{5,7},{6,4},{7,5},{8,10},{9,11},{10,... | collective-permute-start | bytes 786440 | tf_op jit(solution)/shard_map/ppermute | solution.py:290
  94.9 2.5 %layer.10 = (f32[128,1024]{1,0:T(8,128)S(1)}, bf16[128,1024]{1,0:T(8,128)(2,1)S(1)}, f32[128,1024]{1,0:T(8,128)S(1)}, bf16[128,1024]{1,0:T(8,128)(2,1)S(1)}) custom-call(bf16[128,1024]{1,0:T(8,128)(2,1)S(1)} %collective-permute-done.32.x_ref, f32[1,1024]{1,0:T(1,128)S(1)} %copy-done.1, bf16[8,2,128,1024]{3,2,1,0:T(8,128)(2,1)S(1)} %get-tuple-element.68.blocks_ref, ...), custom_call_target="tpu_custom_call" | custom-call | flops 1073741824 | bytes 8388608 | tf_op jit(solution)/shard_map/layer/pallas_call | solution.py:189
  98.0 7.4 %collective-permute-done.25.refs_1_ = bf16[128,1024]{1,0:T(8,128)(2,1)S(1)} collective-permute-done((bf16[128,1024]{1,0:T(8,128)(2,1)S(1)}, bf16[128,1024]{1,0:T(8,128)(2,1)S(1)}, u32[]{:S(2)}, u32[]{:S(2)}) %collective-permute-start.25) | collective-permute-done | bytes 262176 | tf_op jit(solution)/shard_map/ppermute | solution.py:290
  107.1 3.8 %collective-permute-start.29 = (f32[1,128]{1,0:T(1,128)S(1)}, f32[1,128]{1,0:T(1,128)S(1)}, u32[]{:S(2)}, u32[]{:S(2)}) collective-permute-start(f32[1,128]{1,0:T(1,128)S(1)} %get-tuple-element.104), channel_id=1, source_target_pairs={{0,7},{1,6},{2,5},{3,4},{4,11},{5,10},{6,9},{7,8},{8,15},{9,14},{1... | collective-permute-start | bytes 1544 | tf_op jit(solution)/shard_map/ppermute | solution.py:290
  120.1 7.2 %collective-permute-done.39.refs_1_ = bf16[128,1024]{1,0:T(8,128)(2,1)S(1)} collective-permute-done((bf16[128,1024]{1,0:T(8,128)(2,1)S(1)}, bf16[128,1024]{1,0:T(8,128)(2,1)S(1)}, u32[]{:S(2)}, u32[]{:S(2)}) %collective-permute-start.39) | collective-permute-done | bytes 262176 | tf_op jit(solution)/shard_map/ppermute | solution.py:290
  127.9 4.2 %collective-permute-done.37 = bf16[128,1024]{1,0:T(8,128)(2,1)S(1)} collective-permute-done((bf16[128,1024]{1,0:T(8,128)(2,1)S(1)}, bf16[128,1024]{1,0:T(8,128)(2,1)S(1)}, u32[]{:S(2)}, u32[]{:S(2)}) %collective-permute-start.37) | collective-permute-done | bytes 262176 | tf_op jit(solution)/shard_map/ppermute | solution.py:290
  135.5 10.4 %collective-permute-done.41.refs_0_ = bf16[128,1024]{1,0:T(8,128)(2,1)S(1)} collective-permute-done((bf16[128,1024]{1,0:T(8,128)(2,1)S(1)}, bf16[128,1024]{1,0:T(8,128)(2,1)S(1)}, u32[]{:S(2)}, u32[]{:S(2)}) %collective-permute-start.41) | collective-permute-done | bytes 262176 | tf_op jit(solution)/shard_map/ppermute | solution.py:290
  (88 shorter events, 43.0 us)
Async XLA Ops:
  1.2 12.9 %collective-permute-start.3 = (bf16[128,1024]{1,0:T(8,128)(2,1)}, bf16[128,1024]{1,0:T(8,128)(2,1)S(1)}, u32[]{:S(2)}, u32[]{:S(2)}) collective-permute-start(bf16[128,1024]{1,0:T(8,128)(2,1)} %bitcast.9), channel_id=1, source_target_pairs={{0,28},{1,29},{2,30},{3,31},{4,24},{5,25},{6,26},{7,27},{8,20},{9,... | collective-permute-start | bytes 786440 | tf_op jit(solution)/shard_map/ppermute | solution.py:290
  4.6 9.5 %collective-permute-start.6 = (f32[2,128]{1,0:T(2,128)S(1)}, f32[2,128]{1,0:T(2,128)S(1)}, u32[]{:S(2)}, u32[]{:S(2)}) collective-permute-start(f32[2,128]{1,0:T(2,128)S(1)} %squares.1), channel_id=1, source_target_pairs={{0,31},{1,30},{2,29},{3,28},{4,27},{5,26},{6,25},{7,24},{8,23},{9,... | collective-permute-start | bytes 3080 | tf_op jit(solution)/shard_map/ppermute | solution.py:290
  18.2 11.5 %collective-permute-start.2 = (f32[2,128]{1,0:T(2,128)S(1)}, f32[2,128]{1,0:T(2,128)S(1)}, u32[]{:S(2)}, u32[]{:S(2)}) collective-permute-start(f32[2,128]{1,0:T(2,128)S(1)} %squares.1), channel_id=1, source_target_pairs={{0,3},{1,2},{2,1},{3,0},{4,7},{5,6},{6,5},{7,4},{8,11},{9,10},{10,... | collective-permute-start | bytes 3080 | tf_op jit(solution)/shard_map/ppermute | solution.py:290
  25.8 14.9 %collective-permute-start.12 = (bf16[128,1024]{1,0:T(8,128)(2,1)S(1)}, bf16[128,1024]{1,0:T(8,128)(2,1)S(1)}, u32[]{:S(2)}, u32[]{:S(2)}) collective-permute-start(bf16[128,1024]{1,0:T(8,128)(2,1)S(1)} %get-tuple-element.84), channel_id=1, source_target_pairs={{0,1},{1,0},{2,3},{3,2},{4,5},{5,4},{6,7},{7,6},{8,9},{9,8},{10,11... | collective-permute-start | bytes 786440 | tf_op jit(solution)/shard_map/ppermute | solution.py:290
  27.3 13.3 %collective-permute-start.11 = (bf16[128,1024]{1,0:T(8,128)(2,1)S(1)}, bf16[128,1024]{1,0:T(8,128)(2,1)S(1)}, u32[]{:S(2)}, u32[]{:S(2)}) collective-permute-start(bf16[128,1024]{1,0:T(8,128)(2,1)S(1)} %add_convert_fusion.5.refs_3_), channel_id=1, source_target_pairs={{0,2},{1,3},{2,0},{3,1},{4,6},{5,7},{6,4},{7,5},{8,10},{9,11},{10,... | collective-permute-start | bytes 786440 | tf_op jit(solution)/shard_map/ppermute | solution.py:290
  32.3 14.7 %collective-permute-start.8 = (bf16[128,1024]{1,0:T(8,128)(2,1)S(1)}, bf16[128,1024]{1,0:T(8,128)(2,1)S(1)}, u32[]{:S(2)}, u32[]{:S(2)}) collective-permute-start(bf16[128,1024]{1,0:T(8,128)(2,1)S(1)} %get-tuple-element.79), channel_id=1, source_target_pairs={{0,1},{1,0},{2,3},{3,2},{4,5},{5,4},{6,7},{7,6},{8,9},{9,8},{10,11... | collective-permute-start | bytes 786440 | tf_op jit(solution)/shard_map/ppermute | solution.py:290
  41.1 10.2 %collective-permute-start.13 = (bf16[128,1024]{1,0:T(8,128)(2,1)S(1)}, bf16[128,1024]{1,0:T(8,128)(2,1)S(1)}, u32[]{:S(2)}, u32[]{:S(2)}) collective-permute-start(bf16[128,1024]{1,0:T(8,128)(2,1)S(1)} %get-tuple-element.85), channel_id=1, source_target_pairs={{0,4},{1,5},{2,6},{3,7},{4,8},{5,9},{6,10},{7,11},{8,12},{9,13},{1... | collective-permute-start | bytes 786440 | tf_op jit(solution)/shard_map/ppermute | solution.py:290
  47.1 14.4 %collective-permute-start.10 = (bf16[128,1024]{1,0:T(8,128)(2,1)S(1)}, bf16[128,1024]{1,0:T(8,128)(2,1)S(1)}, u32[]{:S(2)}, u32[]{:S(2)}) collective-permute-start(bf16[128,1024]{1,0:T(8,128)(2,1)S(1)} %get-tuple-element.81), channel_id=1, source_target_pairs={{0,1},{1,0},{2,3},{3,2},{4,5},{5,4},{6,7},{7,6},{8,9},{9,8},{10,11... | collective-permute-start | bytes 786440 | tf_op jit(solution)/shard_map/ppermute | solution.py:290
  48.9 14.3 %collective-permute-start.9 = (bf16[128,1024]{1,0:T(8,128)(2,1)S(1)}, bf16[128,1024]{1,0:T(8,128)(2,1)S(1)}, u32[]{:S(2)}, u32[]{:S(2)}) collective-permute-start(bf16[128,1024]{1,0:T(8,128)(2,1)S(1)} %add_convert_fusion.4.refs_3_), channel_id=1, source_target_pairs={{0,2},{1,3},{2,0},{3,1},{4,6},{5,7},{6,4},{7,5},{8,10},{9,11},{10,... | collective-permute-start | bytes 786440 | tf_op jit(solution)/shard_map/ppermute | solution.py:290
  54.3 15.6 %collective-permute-start.22 = (bf16[128,1024]{1,0:T(8,128)(2,1)S(1)}, bf16[128,1024]{1,0:T(8,128)(2,1)S(1)}, u32[]{:S(2)}, u32[]{:S(2)}) collective-permute-start(bf16[128,1024]{1,0:T(8,128)(2,1)S(1)} %get-tuple-element.95), channel_id=1, source_target_pairs={{0,1},{1,0},{2,3},{3,2},{4,5},{5,4},{6,7},{7,6},{8,9},{9,8},{10,11... | collective-permute-start | bytes 786440 | tf_op jit(solution)/shard_map/ppermute | solution.py:290
  63.7 9.6 %collective-permute-start.18 = (bf16[128,1024]{1,0:T(8,128)(2,1)S(1)}, bf16[128,1024]{1,0:T(8,128)(2,1)S(1)}, u32[]{:S(2)}, u32[]{:S(2)}) collective-permute-start(bf16[128,1024]{1,0:T(8,128)(2,1)S(1)} %get-tuple-element.90), channel_id=1, source_target_pairs={{0,4},{1,5},{2,6},{3,7},{4,8},{5,9},{6,10},{7,11},{8,12},{9,13},{1... | collective-permute-start | bytes 786440 | tf_op jit(solution)/shard_map/ppermute | solution.py:290
  69.9 14.7 %collective-permute-start.31 = (bf16[128,1024]{1,0:T(8,128)(2,1)S(1)}, bf16[128,1024]{1,0:T(8,128)(2,1)S(1)}, u32[]{:S(2)}, u32[]{:S(2)}) collective-permute-start(bf16[128,1024]{1,0:T(8,128)(2,1)S(1)} %get-tuple-element.107), channel_id=1, source_target_pairs={{0,1},{1,0},{2,3},{3,2},{4,5},{5,4},{6,7},{7,6},{8,9},{9,8},{10,11... | collective-permute-start | bytes 786440 | tf_op jit(solution)/shard_map/ppermute | solution.py:290
  70.4 14.6 %collective-permute-start.30 = (bf16[128,1024]{1,0:T(8,128)(2,1)S(1)}, bf16[128,1024]{1,0:T(8,128)(2,1)S(1)}, u32[]{:S(2)}, u32[]{:S(2)}) collective-permute-start(bf16[128,1024]{1,0:T(8,128)(2,1)S(1)} %add_convert_fusion.3.refs_3_), channel_id=1, source_target_pairs={{0,2},{1,3},{2,0},{3,1},{4,6},{5,7},{6,4},{7,5},{8,10},{9,11},{10,... | collective-permute-start | bytes 786440 | tf_op jit(solution)/shard_map/ppermute | solution.py:290
  75.8 14.9 %collective-permute-start.23 = (bf16[128,1024]{1,0:T(8,128)(2,1)S(1)}, bf16[128,1024]{1,0:T(8,128)(2,1)S(1)}, u32[]{:S(2)}, u32[]{:S(2)}) collective-permute-start(bf16[128,1024]{1,0:T(8,128)(2,1)S(1)} %get-tuple-element.100), channel_id=1, source_target_pairs={{0,1},{1,0},{2,3},{3,2},{4,5},{5,4},{6,7},{7,6},{8,9},{9,8},{10,11... | collective-permute-start | bytes 786440 | tf_op jit(solution)/shard_map/ppermute | solution.py:290
  90.7 14.6 %collective-permute-start.25 = (bf16[128,1024]{1,0:T(8,128)(2,1)S(1)}, bf16[128,1024]{1,0:T(8,128)(2,1)S(1)}, u32[]{:S(2)}, u32[]{:S(2)}) collective-permute-start(bf16[128,1024]{1,0:T(8,128)(2,1)S(1)} %get-tuple-element.102), channel_id=1, source_target_pairs={{0,1},{1,0},{2,3},{3,2},{4,5},{5,4},{6,7},{7,6},{8,9},{9,8},{10,11... | collective-permute-start | bytes 786440 | tf_op jit(solution)/shard_map/ppermute | solution.py:290
  92.1 14.4 %collective-permute-start.24 = (bf16[128,1024]{1,0:T(8,128)(2,1)S(1)}, bf16[128,1024]{1,0:T(8,128)(2,1)S(1)}, u32[]{:S(2)}, u32[]{:S(2)}) collective-permute-start(bf16[128,1024]{1,0:T(8,128)(2,1)S(1)} %add_convert_fusion.2.refs_3_), channel_id=1, source_target_pairs={{0,2},{1,3},{2,0},{3,1},{4,6},{5,7},{6,4},{7,5},{8,10},{9,11},{10,... | collective-permute-start | bytes 786440 | tf_op jit(solution)/shard_map/ppermute | solution.py:290
  97.5 15.1 %collective-permute-start.36 = (bf16[128,1024]{1,0:T(8,128)(2,1)S(1)}, bf16[128,1024]{1,0:T(8,128)(2,1)S(1)}, u32[]{:S(2)}, u32[]{:S(2)}) collective-permute-start(bf16[128,1024]{1,0:T(8,128)(2,1)S(1)} %get-tuple-element.112), channel_id=1, source_target_pairs={{0,1},{1,0},{2,3},{3,2},{4,5},{5,4},{6,7},{7,6},{8,9},{9,8},{10,11... | collective-permute-start | bytes 786440 | tf_op jit(solution)/shard_map/ppermute | solution.py:290
  107.0 9.5 %collective-permute-start.26 = (bf16[128,1024]{1,0:T(8,128)(2,1)S(1)}, bf16[128,1024]{1,0:T(8,128)(2,1)S(1)}, u32[]{:S(2)}, u32[]{:S(2)}) collective-permute-start(bf16[128,1024]{1,0:T(8,128)(2,1)S(1)} %get-tuple-element.103), channel_id=1, source_target_pairs={{0,4},{1,5},{2,6},{3,7},{4,8},{5,9},{6,10},{7,11},{8,12},{9,13},{1... | collective-permute-start | bytes 786440 | tf_op jit(solution)/shard_map/ppermute | solution.py:290
  112.7 14.7 %collective-permute-start.39 = (bf16[128,1024]{1,0:T(8,128)(2,1)S(1)}, bf16[128,1024]{1,0:T(8,128)(2,1)S(1)}, u32[]{:S(2)}, u32[]{:S(2)}) collective-permute-start(bf16[128,1024]{1,0:T(8,128)(2,1)S(1)} %get-tuple-element.121), channel_id=1, source_target_pairs={{0,1},{1,0},{2,3},{3,2},{4,5},{5,4},{6,7},{7,6},{8,9},{9,8},{10,11... | collective-permute-start | bytes 786440 | tf_op jit(solution)/shard_map/ppermute | solution.py:290
  113.7 14.1 %collective-permute-start.38 = (bf16[128,1024]{1,0:T(8,128)(2,1)S(1)}, bf16[128,1024]{1,0:T(8,128)(2,1)S(1)}, u32[]{:S(2)}, u32[]{:S(2)}) collective-permute-start(bf16[128,1024]{1,0:T(8,128)(2,1)S(1)} %add_convert_fusion.1.refs_3_), channel_id=1, source_target_pairs={{0,2},{1,3},{2,0},{3,1},{4,6},{5,7},{6,4},{7,5},{8,10},{9,11},{10,... | collective-permute-start | bytes 786440 | tf_op jit(solution)/shard_map/ppermute | solution.py:290
  119.5 12.6 %collective-permute-start.37 = (bf16[128,1024]{1,0:T(8,128)(2,1)S(1)}, bf16[128,1024]{1,0:T(8,128)(2,1)S(1)}, u32[]{:S(2)}, u32[]{:S(2)}) collective-permute-start(bf16[128,1024]{1,0:T(8,128)(2,1)S(1)} %get-tuple-element.119), channel_id=1, source_target_pairs={{0,1},{1,0},{2,3},{3,2},{4,5},{5,4},{6,7},{7,6},{8,9},{9,8},{10,11... | collective-permute-start | bytes 786440 | tf_op jit(solution)/shard_map/ppermute | solution.py:290
  132.2 13.8 %collective-permute-start.41 = (bf16[128,1024]{1,0:T(8,128)(2,1)S(1)}, bf16[128,1024]{1,0:T(8,128)(2,1)S(1)}, u32[]{:S(2)}, u32[]{:S(2)}) collective-permute-start(bf16[128,1024]{1,0:T(8,128)(2,1)S(1)} %add_convert_fusion), channel_id=1, source_target_pairs={{0,2},{1,3},{2,0},{3,1},{4,6},{5,7},{6,4},{7,5},{8,10},{9,11},{10,... | collective-permute-start | bytes 786440 | tf_op jit(solution)/shard_map/ppermute | solution.py:290
  134.0 12.0 %collective-permute-start.42 = (bf16[128,1024]{1,0:T(8,128)(2,1)S(1)}, bf16[128,1024]{1,0:T(8,128)(2,1)S(1)}, u32[]{:S(2)}, u32[]{:S(2)}) collective-permute-start(bf16[128,1024]{1,0:T(8,128)(2,1)S(1)} %get-tuple-element.125), channel_id=1, source_target_pairs={{0,1},{1,0},{2,3},{3,2},{4,5},{5,4},{6,7},{7,6},{8,9},{9,8},{10,11... | collective-permute-start | bytes 786440 | tf_op jit(solution)/shard_map/ppermute | solution.py:290
  135.5 10.5 %collective-permute-start.43 = (bf16[128,1024]{1,0:T(8,128)(2,1)S(1)}, bf16[128,1024]{1,0:T(8,128)(2,1)S(1)}, u32[]{:S(2)}, u32[]{:S(2)}) collective-permute-start(bf16[128,1024]{1,0:T(8,128)(2,1)S(1)} %end.1), channel_id=1, source_target_pairs={{0,28},{1,29},{2,30},{3,31},{4,24},{5,25},{6,26},{7,27},{8,20},{9,... | collective-permute-start | bytes 786440 | tf_op jit(solution)/shard_map/ppermute | solution.py:290
  (22 other events, 167.2 us)
